TPU v7x, 256 devices: a whole 4x4x8 slice. The times are simulated.
256 devices in a mesh: lon: 8 (over x, y_lo), lat: 8 (over z), lev: 4 (over y_hi, core).
Axes of the slice: x: 4, y: 4 (y_hi: 2, y_lo: 2; y = y_hi * 2 + y_lo), z: 8, core: 2. Of those that a mesh axis runs over, the one named last changes fastest.
Arguments:
- tokens_in: bfloat16 [4, 128, 128, 512], P('lev', 'lat', 'lon'), may hold values from -6 to 6
- cotangent: bfloat16 [4, 128, 128, 512], P('lev', 'lat', 'lon'), may hold values from -6 to 6
- qkv_weight: bfloat16 [512, 1536], replicated, may hold values from -5 to 5
- out_weight: bfloat16 [512, 512], replicated, may hold values from -0.25 to 0.25
- norm_gain: float32 [512], replicated, may hold values from 0.5 to 1.5
- ocean_mask: int32 [4, 128, 128], P('lev', 'lat', 'lon'), may hold values from 0 to 1, as said below
Outputs:
- layer_out: bfloat16 [4, 128, 128, 512], P('lev', 'lat', 'lon')
- input_grad: bfloat16 [4, 128, 128, 512], P('lev', 'lat', 'lon')
- qkv_grad: float32 [512, 1536], P('lev')
- out_grad: float32 [512, 512], P('lev')
- gain_grad: float32 [512], P('lev')
Inputs may be any that keep to these rules, and one draw needn't show every extreme that they name: `ocean_mask`: at each level group, at most 3 of the windows of one device hold an ocean patch, and some device holds exactly 3 such windows.
All inputs are finite; a program needn't handle non-finite values.
Results may differ from a plain program's by a relative error of at most 0.017.
The roundings to bfloat16 on the way count: a program that leaves them out, or rounds other values in their place, can miss the bound.
Values may be sent and summed in bfloat16 or wider, within the bound.
A program may use at most 128 MiB of HBM per device.

v0:
```python
import jax
import jax.numpy as jnp
from jax import lax
from jax.sharding import PartitionSpec as P

HEADS = 8
WIN = 8


def with_halo(block, sides, width, periodic):
    for axis, dim in sides:
        count = lax.axis_size(axis)
        forward = [(i, i + 1) for i in range(count - 1)]
        if periodic:
            forward.append((count - 1, 0))
        backward = [(target, source) for source, target in forward]
        low = lax.ppermute(
            lax.slice_in_dim(block, block.shape[dim] - width, None, axis=dim), axis, forward
        )
        high = lax.ppermute(lax.slice_in_dim(block, 0, width, axis=dim), axis, backward)
        block = jnp.concatenate([low, block, high], axis=dim)
    return block


def norm_rows(values_in):
    center = values_in - jnp.mean(values_in, axis=-1, keepdims=True)
    spread = jnp.mean(center * center, axis=-1, keepdims=True)
    scaling = lax.rsqrt(spread + 1e-05)
    return (center * scaling, scaling)


def to_windows(grid_in, lat_windows, lon_windows, window_side):
    channels = grid_in.shape[-1]
    blocks = grid_in.reshape(lat_windows, window_side, lon_windows, window_side, channels)
    return jnp.transpose(blocks, (0, 2, 1, 3, 4)).reshape(
        lat_windows * lon_windows, window_side * window_side, channels
    )


def from_windows(blocks, lat_windows, lon_windows, window_side):
    channels = blocks.shape[-1]
    grid_out = blocks.reshape(lat_windows, lon_windows, window_side, window_side, channels)
    return jnp.transpose(grid_out, (0, 2, 1, 3, 4)).reshape(
        lat_windows * window_side, lon_windows * window_side, channels
    )


def neighbours(padded, lat_windows, lon_windows, window_side):
    pieces = []
    for lat_step in range(3):
        for lon_step in range(3):
            section = padded[
                lat_step * window_side : (lat_step + lat_windows) * window_side,
                lon_step * window_side : (lon_step + lon_windows) * window_side,
            ]
            pieces.append(to_windows(section, lat_windows, lon_windows, window_side))
    return jnp.concatenate(pieces, axis=1)


def spread_back(gathered, lat_windows, lon_windows, window_side):
    channels = gathered.shape[-1]
    window_area = window_side * window_side
    totals = jnp.zeros(
        ((lat_windows + 2) * window_side, (lon_windows + 2) * window_side, channels), jnp.float32
    )
    for lat_step in range(3):
        for lon_step in range(3):
            slot_index = lat_step * 3 + lon_step
            section = from_windows(
                gathered[:, slot_index * window_area : (slot_index + 1) * window_area],
                lat_windows,
                lon_windows,
                window_side,
            )
            totals = totals.at[
                lat_step * window_side : (lat_step + lat_windows) * window_side,
                lon_step * window_side : (lon_step + lon_windows) * window_side,
            ].add(section)
    return totals


def split_heads(array_in, head_count):
    return array_in.reshape(
        array_in.shape[0], array_in.shape[1], head_count, array_in.shape[2] // head_count
    )


def attend_forward(queries, key_rows, value_rows, key_mask, alive_flag, head_count):
    features = queries.shape[-1]
    inv_root = (features // head_count) ** (-0.5)
    scores = (
        jnp.einsum(
            "wqhd,wkhd->whqk",
            split_heads(queries, head_count),
            split_heads(key_rows, head_count),
            preferred_element_type=jnp.float32,
        )
        * inv_root
    )
    scores = scores + (key_mask[:, None, None, :] - 1.0) * 1000000000.0
    row_top = jnp.max(scores, axis=-1, keepdims=True)
    weights = jnp.exp(scores - row_top)
    probabilities = weights / jnp.sum(weights, axis=-1, keepdims=True)
    probabilities_low = probabilities.astype(jnp.bfloat16)
    mixed_out = jnp.einsum(
        "whqk,wkhd->wqhd",
        probabilities_low,
        split_heads(value_rows, head_count),
        preferred_element_type=jnp.float32,
    )
    mixed_out = mixed_out.reshape(queries.shape) * alive_flag[:, None, None]
    return (mixed_out.astype(jnp.bfloat16), probabilities)


def attend_backward(
    queries, key_rows, value_rows, probabilities, mixed_out, grad_mixed, head_count
):
    features = queries.shape[-1]
    inv_root = (features // head_count) ** (-0.5)
    grad_heads = split_heads(grad_mixed, head_count)
    query_heads = split_heads(queries, head_count)
    grad_probs = jnp.einsum(
        "wqhd,wkhd->whqk",
        grad_heads,
        split_heads(value_rows, head_count),
        preferred_element_type=jnp.float32,
    )
    delta_rows = jnp.einsum(
        "wqhd,wqhd->whq",
        grad_heads,
        split_heads(mixed_out, head_count),
        preferred_element_type=jnp.float32,
    )
    grad_scores = (probabilities * (grad_probs - delta_rows[..., None]) * inv_root).astype(
        jnp.bfloat16
    )
    grad_query = jnp.einsum(
        "whqk,wkhd->wqhd",
        grad_scores,
        split_heads(key_rows, head_count),
        preferred_element_type=jnp.float32,
    ).reshape(queries.shape)
    key_shape = (key_rows.shape[0], key_rows.shape[1], features)
    grad_key = jnp.einsum(
        "whqk,wqhd->wkhd", grad_scores, query_heads, preferred_element_type=jnp.float32
    ).reshape(key_shape)
    grad_value = jnp.einsum(
        "whqk,wqhd->wkhd",
        probabilities.astype(jnp.bfloat16),
        grad_heads,
        preferred_element_type=jnp.float32,
    ).reshape(key_shape)
    return (grad_query, jnp.concatenate([grad_key, grad_value], axis=-1))


def fold_lat(grad_pad, window_side):
    inner_rows = grad_pad.shape[0] - 2 * window_side
    filler = jnp.zeros((inner_rows - 2 * window_side,) + grad_pad.shape[1:], jnp.float32)
    folded = jnp.concatenate(
        [grad_pad[:window_side], filler, grad_pad[inner_rows + window_side :]], axis=0
    )
    arrived = with_halo(folded, (("lat", 0),), window_side, False)
    middle = grad_pad[window_side : inner_rows + window_side]
    middle = middle.at[:window_side].add(arrived[:window_side])
    return middle.at[inner_rows - window_side :].add(arrived[inner_rows + window_side :])


def fold_lon(grad_pad, window_side):
    inner_cols = grad_pad.shape[1] - 2 * window_side
    filler = jnp.zeros(
        (grad_pad.shape[0], inner_cols - 2 * window_side, grad_pad.shape[2]), jnp.float32
    )
    folded = jnp.concatenate(
        [grad_pad[:, :window_side], filler, grad_pad[:, inner_cols + window_side :]], axis=1
    )
    arrived = with_halo(folded, (("lon", 1),), window_side, True)
    middle = grad_pad[:, window_side : inner_cols + window_side]
    middle = middle.at[:, :window_side].add(arrived[:, :window_side])
    return middle.at[:, inner_cols - window_side :].add(arrived[:, inner_cols + window_side :])


def plane_sum(gradients):
    return lax.psum((gradients[0], gradients[1], gradients[2]), ("lon", "lat"))


def level_share(gradients):
    return (
        lax.psum_scatter(gradients[0], "lev", scatter_dimension=0, tiled=True),
        lax.psum_scatter(gradients[1], "lev", scatter_dimension=0, tiled=True),
        lax.psum_scatter(gradients[2], "lev", scatter_dimension=0, tiled=True),
    )


def on_device(tokens_in, cotangent, qkv_weight, out_weight, norm_gain, ocean_mask):
    lat_rows = tokens_in.shape[1]
    lon_cols = tokens_in.shape[2]
    features = tokens_in.shape[3]
    window_side = WIN
    lat_windows = lat_rows // window_side
    lon_windows = lon_cols // window_side
    flat_in = tokens_in.reshape(-1, features).astype(jnp.float32)
    normed, scaling = norm_rows(flat_in)
    hidden = (normed * norm_gain).astype(jnp.bfloat16)
    ocean = ocean_mask[0].astype(jnp.float32)
    ocean_low = ocean.astype(jnp.bfloat16)
    projected = jnp.dot(hidden, qkv_weight, preferred_element_type=jnp.float32).astype(jnp.bfloat16)
    queries = projected[:, :features]
    payload = projected[:, features:].reshape(lat_rows, lon_cols, 2 * features)
    padded, padded_mask = (
        with_halo(payload, (("lat", 0), ("lon", 1)), window_side, True),
        with_halo(ocean_low, (("lat", 0), ("lon", 1)), window_side, True),
    )
    lat_place = lax.axis_index("lat")
    lat_count = lax.axis_size("lat")
    row_ids = jnp.arange(lat_rows + 2 * window_side)
    keep_rows = jnp.where(
        row_ids < window_side,
        lat_place > 0,
        jnp.where(row_ids >= lat_rows + window_side, lat_place < lat_count - 1, True),
    )
    keep_low = keep_rows.astype(jnp.bfloat16)
    padded = padded * keep_low[:, None, None]
    padded_mask = padded_mask * keep_low[:, None]
    near = neighbours(padded, lat_windows, lon_windows, window_side)
    near_mask = neighbours(padded_mask[..., None], lat_windows, lon_windows, window_side)[
        ..., 0
    ].astype(jnp.float32)
    query_windows = to_windows(
        queries.reshape(lat_rows, lon_cols, features), lat_windows, lon_windows, window_side
    )
    ocean_windows = to_windows(ocean[..., None], lat_windows, lon_windows, window_side)[..., 0]
    alive_flag = jnp.max(ocean_windows, axis=1)
    grad_branch = (cotangent[0] * ocean_low[..., None]).reshape(-1, features)
    grad_mixed = jnp.einsum(
        "te,de->td", grad_branch, out_weight, preferred_element_type=jnp.float32
    ).astype(jnp.bfloat16)
    grad_windows = to_windows(
        grad_mixed.reshape(lat_rows, lon_cols, features), lat_windows, lon_windows, window_side
    )
    key_rows = near[..., :features]
    value_rows = near[..., features:]
    mixed_windows, probabilities = attend_forward(
        query_windows, key_rows, value_rows, near_mask, alive_flag, HEADS
    )
    grad_query, grad_near = attend_backward(
        query_windows, key_rows, value_rows, probabilities, mixed_windows, grad_windows, HEADS
    )
    mixed_flat = from_windows(mixed_windows, lat_windows, lon_windows, window_side).reshape(
        -1, features
    )
    branch = jnp.dot(mixed_flat, out_weight, preferred_element_type=jnp.float32)
    layer_out = (
        (flat_in + ocean.reshape(-1, 1) * branch).astype(jnp.bfloat16).reshape(tokens_in.shape)
    )
    out_grad_local = jnp.einsum(
        "td,te->de", mixed_flat, grad_branch, preferred_element_type=jnp.float32
    )
    grad_pad = spread_back(grad_near, lat_windows, lon_windows, window_side)
    grad_kv = fold_lon(fold_lat(grad_pad, window_side), window_side)
    grad_query_flat = from_windows(grad_query, lat_windows, lon_windows, window_side).reshape(
        -1, features
    )
    grad_qkv = jnp.concatenate(
        [
            grad_query_flat.astype(jnp.bfloat16),
            grad_kv.reshape(-1, 2 * features).astype(jnp.bfloat16),
        ],
        axis=1,
    )
    grad_hidden = jnp.einsum("tc,dc->td", grad_qkv, qkv_weight, preferred_element_type=jnp.float32)
    qkv_grad_local = jnp.einsum("td,tc->dc", hidden, grad_qkv, preferred_element_type=jnp.float32)
    gain_grad_local = jnp.sum(grad_hidden * normed, axis=0)
    scaled = grad_hidden * norm_gain
    correction = (
        scaled
        - jnp.mean(scaled, axis=-1, keepdims=True)
        - normed * jnp.mean(scaled * normed, axis=-1, keepdims=True)
    )
    input_grad = (
        (cotangent.reshape(-1, features).astype(jnp.float32) + scaling * correction)
        .astype(jnp.bfloat16)
        .reshape(tokens_in.shape)
    )
    local_grads = (qkv_grad_local, out_grad_local, gain_grad_local)
    qkv_grad, out_grad, gain_grad = level_share(plane_sum(local_grads))
    return (layer_out, input_grad, qkv_grad, out_grad, gain_grad)


def solution(mesh):
    placed = (
        P("lev", "lat", "lon", None),
        P("lev", "lat", "lon", None),
        P(),
        P(),
        P(),
        P("lev", "lat", "lon"),
    )
    return jax.shard_map(
        on_device,
        mesh=mesh,
        in_specs=placed,
        out_specs=(
            P("lev", "lat", "lon", None),
            P("lev", "lat", "lon", None),
            P("lev", None),
            P("lev", None),
            P("lev"),
        ),
        check_vma=False,
    )
```

profile of v0, /device:TPU:8, one launch (start us, length us, event | category | flops | bytes accessed | tf_op | source)
XLA Modules:
  0.0 895.1 jit_solution(12721827022408746523)
XLA Ops:
  10.0 3.9 collective-permute-start.5
  26.2 2.5 copy.151
  41.9 20.2 %collective-permute-done.2 = bf16[32,8,1024]{2,1,0:T(8,128)(2,1)} collective-permute-done((bf16[32,8,1024]{2,1,0:T(8,128)(2,1)}, bf16[32,8,1024]{2,1,0:T(8,128)(2,1)}, u32[]{:S(2)}, u32[]{:S(2)}) %collective-permute-start.2) | collective-permute-done | bytes 524320 | tf_op jit(solution)/shard_map/ppermute | solution.py:17
  65.2 2.6 fusion.37
  67.7 4.3 copy.116
  72.1 4.4 copy.114
  76.5 5.9 fusion.48
  82.4 3.0 fusion.4
  85.5 3.2 fusion.50
  92.2 3.2 fusion.49
  95.4 5.7 copy.135
  101.1 5.7 copy.136
  106.8 4.1 pad_maximum_fusion
  117.6 2.5 scatter-add.44
  120.1 3.2 add_select_fusion.1
  123.3 7.2 scatter-add.45
  130.5 4.6 add_select_fusion
  135.2 6.7 scatter-add.46
  141.9 2.9 fusion.23
  144.8 2.8 fusion.22
  154.6 2.4 fusion.18
  157.0 3.3 fusion.38
  160.3 3.2 collective-permute-start.8
  171.7 11.8 %collective-permute-done.8 = f32[8,32,1024]{2,1,0:T(8,128)} collective-permute-done((f32[8,32,1024]{2,1,0:T(8,128)}, f32[8,32,1024]{2,1,0:T(8,128)}, u32[]{:S(2)}, u32[]{:S(2)}) %collective-permute-start.8) | collective-permute-done | bytes 1048608 | tf_op jit(solution)/shard_map/ppermute | solution.py:17
  183.5 2.7 fusion.17
  188.6 2.8 fusion.16
  193.7 4.2 collective-permute-start.10
  200.9 20.8 %collective-permute-done.10 = f32[16,8,1024]{2,1,0:T(8,128)} collective-permute-done((f32[16,8,1024]{2,1,0:T(8,128)}, f32[16,8,1024]{2,1,0:T(8,128)}, u32[]{:S(2)}, u32[]{:S(2)}) %collective-permute-start.10) | collective-permute-done | bytes 524320 | tf_op jit(solution)/shard_map/ppermute | solution.py:17
  229.7 51.7 %reduce-scatter.3.cloned.1.call-done = f32[128,1536]{1,0:T(8,128)} async-done(((f32[512,1536]{1,0:T(8,128)}), f32[128,1536]{1,0:T(8,128)}) %reduce-scatter.3.cloned.1.call-update) | async-done | bytes 786448 | tf_op jit(solution)/shard_map/reduce_scatter | solution.py:188
  284.3 7.8 all-reduce.1
  292.2 143.6 %psum.26 = f32[128]{0:T(128)} all-reduce(f32[128]{0:T(128)S(1)} %dynamic-slice.107), channel_id=1, replica_groups=mesh['lon'=8,'lat'=8,'lev'=4] {'lon','lat'}, use_global_device_ids=true, to_apply=%region_14.15 | all-reduce | flops 128 | bytes 1024 | tf_op jit(solution)/shard_map/psum | solution.py:183
  436.8 448.1 %all-reduce.5.cloned.1.call-done = (f32[128,1536]{1,0:T(8,128)}, f32[128,512]{1,0:T(8,128)}) async-done(((f32[128,1536]{1,0:T(8,128)}, f32[128,512]{1,0:T(8,128)}), (f32[128,1536]{1,0:T(8,128)}, f32[128,512]{1,0:T(8,128)})) %all-reduce.5.cloned.1.call-update) | async-done | bytes 1048592 | tf_op jit(solution)/shard_map/psum | solution.py:183
  (199 shorter events, 78.8 us)
Async XLA Ops:
  7.2 11.1 %copy-start = (bf16[512,1536]{1,0:T(8,128)(2,1)S(1)}, bf16[512,1536]{1,0:T(8,128)(2,1)}, u32[]{:S(2)}) copy-start(bf16[512,1536]{1,0:T(8,128)(2,1)} %param.34) | copy-start | bytes 4718596
  7.2 14.7 %copy-start.13 = (bf16[1,16,16,512]{3,2,1,0:T(8,128)(2,1)S(1)}, bf16[1,16,16,512]{3,2,1,0:T(8,128)(2,1)}, u32[]{:S(2)}) copy-start(bf16[1,16,16,512]{3,2,1,0:T(8,128)(2,1)} %param.33) | copy-start | bytes 786436
  7.2 14.8 %copy-start.15 = (bf16[512,512]{1,0:T(8,128)(2,1)S(1)}, bf16[512,512]{1,0:T(8,128)(2,1)}, u32[]{:S(2)}) copy-start(bf16[512,512]{1,0:T(8,128)(2,1)} %param.35) | copy-start | bytes 1572868
  7.2 222.5 %reduce-scatter.5.cloned.1.call-start = ((), (), s32[]{:S(2)}) async-start(), calls=%async_computation.3 | async-start | bytes 1310720 | tf_op jit(solution)/shard_map/reduce_scatter | solution.py:189
  8.1 24.9 %collective-permute-start.4 = (bf16[8,16]{1,0:T(8,128)(2,1)S(1)}, bf16[8,16]{1,0:T(8,128)(2,1)S(1)}, u32[]{:S(2)}, u32[]{:S(2)}) collective-permute-start(bf16[8,16]{1,0:T(8,128)(2,1)S(1)} %get-tuple-element.211), channel_id=1, source_target_pairs={{0,4},{4,8},{8,12},{12,16},{16,20},{20,24},{24,28},{28,0},{1,5},{5... | collective-permute-start | bytes 776 | tf_op jit(solution)/shard_map/ppermute | solution.py:17
  10.0 23.0 %collective-permute-start.5 = (bf16[8,16]{1,0:T(8,128)(2,1)S(1)}, bf16[8,16]{1,0:T(8,128)(2,1)S(1)}, u32[]{:S(2)}, u32[]{:S(2)}) collective-permute-start(bf16[8,16]{1,0:T(8,128)(2,1)S(1)} %get-tuple-element.212), channel_id=1, source_target_pairs={{4,0},{8,4},{12,8},{16,12},{20,16},{24,20},{28,24},{0,28},{5,1},{9... | collective-permute-start | bytes 776 | tf_op jit(solution)/shard_map/ppermute | solution.py:20
  19.7 15.5 %collective-permute-start.1 = (bf16[8,16,1024]{2,1,0:T(8,128)(2,1)}, bf16[8,16,1024]{2,1,0:T(8,128)(2,1)}, u32[]{:S(2)}, u32[]{:S(2)}) collective-permute-start(bf16[8,16,1024]{2,1,0:T(8,128)(2,1)} %bitcast.5), channel_id=1, source_target_pairs={{4,0},{8,4},{12,8},{16,12},{20,16},{24,20},{28,24},{0,28},{5,1},{9... | collective-permute-start | bytes 786440 | tf_op jit(solution)/shard_map/ppermute | solution.py:20
  21.7 13.5 %collective-permute-start = (bf16[8,16,1024]{2,1,0:T(8,128)(2,1)}, bf16[8,16,1024]{2,1,0:T(8,128)(2,1)}, u32[]{:S(2)}, u32[]{:S(2)}) collective-permute-start(bf16[8,16,1024]{2,1,0:T(8,128)(2,1)} %bitcast.3), channel_id=1, source_target_pairs={{0,4},{4,8},{8,12},{12,16},{16,20},{20,24},{24,28},{28,0},{1,5},{5... | collective-permute-start | bytes 786440 | tf_op jit(solution)/shard_map/ppermute | solution.py:17
  22.0 6.8 copy-start.19
  33.1 6.8 collective-permute-start.6
  34.5 5.5 collective-permute-start.7
  37.4 24.6 %collective-permute-start.2 = (bf16[32,8,1024]{2,1,0:T(8,128)(2,1)}, bf16[32,8,1024]{2,1,0:T(8,128)(2,1)}, u32[]{:S(2)}, u32[]{:S(2)}) collective-permute-start(bf16[32,8,1024]{2,1,0:T(8,128)(2,1)} %get-tuple-element.192), channel_id=1, source_target_pairs={{0,32},{32,64},{64,96},{96,128},{128,160},{160,192},{192,224},{224... | collective-permute-start | bytes 1572872 | tf_op jit(solution)/shard_map/ppermute | solution.py:17
  39.7 22.4 %collective-permute-start.3 = (bf16[32,8,1024]{2,1,0:T(8,128)(2,1)}, bf16[32,8,1024]{2,1,0:T(8,128)(2,1)}, u32[]{:S(2)}, u32[]{:S(2)}) collective-permute-start(bf16[32,8,1024]{2,1,0:T(8,128)(2,1)} %get-tuple-element.193), channel_id=1, source_target_pairs={{32,0},{64,32},{96,64},{128,96},{160,128},{192,160},{224,192},{0,2... | collective-permute-start | bytes 1572872 | tf_op jit(solution)/shard_map/ppermute | solution.py:20
  82.4 8.3 slice-start
  85.5 5.2 slice-start.1
  141.9 5.7 copy-start.9
  141.9 8.0 copy-start.7
  144.8 7.5 copy-start.8
  154.6 10.4 %copy-start.14 = (bf16[1,16,16,512]{3,2,1,0:T(8,128)(2,1)S(1)}, bf16[1,16,16,512]{3,2,1,0:T(8,128)(2,1)}, u32[]{:S(2)}) copy-start(bf16[1,16,16,512]{3,2,1,0:T(8,128)(2,1)} %param.33) | copy-start | bytes 786436
  157.0 8.8 copy-start.1
  160.3 23.2 %collective-permute-start.8 = (f32[8,32,1024]{2,1,0:T(8,128)}, f32[8,32,1024]{2,1,0:T(8,128)}, u32[]{:S(2)}, u32[]{:S(2)}) collective-permute-start(f32[8,32,1024]{2,1,0:T(8,128)} %get-tuple-element.180), channel_id=1, source_target_pairs={{0,4},{4,8},{8,12},{12,16},{16,20},{20,24},{24,28},{1,5},{5,9},{9,... | collective-permute-start | bytes 3145736 | tf_op jit(solution)/shard_map/ppermute | solution.py:17
  163.5 25.1 %collective-permute-start.9 = (f32[8,32,1024]{2,1,0:T(8,128)}, f32[8,32,1024]{2,1,0:T(8,128)}, u32[]{:S(2)}, u32[]{:S(2)}) collective-permute-start(f32[8,32,1024]{2,1,0:T(8,128)} %get-tuple-element.179), channel_id=1, source_target_pairs={{4,0},{8,4},{12,8},{16,12},{20,16},{24,20},{28,24},{5,1},{9,5},{13... | collective-permute-start | bytes 3145736 | tf_op jit(solution)/shard_map/ppermute | solution.py:20
  171.6 109.8 %reduce-scatter.3.cloned.1.call-start = ((), (), s32[]{:S(2)}) async-start(), calls=%async_computation.2 | async-start | bytes 3932160 | tf_op jit(solution)/shard_map/reduce_scatter | solution.py:188
  171.6 26.2 %copy-start.2 = (bf16[4,576,512]{1,2,0:T(8,128)(2,1)S(1)}, bf16[4,576,512]{1,2,0:T(8,128)(2,1)}, u32[]{:S(2)}) copy-start(bf16[4,576,512]{1,2,0:T(8,128)(2,1)} %copy.116) | copy-start | bytes 7077892
  171.7 26.2 %copy-start.4 = (bf16[4,8,64,576]{3,2,1,0:T(8,128)(2,1)S(1)}, bf16[4,8,64,576]{3,2,1,0:T(8,128)(2,1)}, u32[]{:S(2)}) copy-start(bf16[4,8,64,576]{3,2,1,0:T(8,128)(2,1)} %copy-done.3) | copy-start | bytes 7077892
  193.7 28.0 %collective-permute-start.10 = (f32[16,8,1024]{2,1,0:T(8,128)}, f32[16,8,1024]{2,1,0:T(8,128)}, u32[]{:S(2)}, u32[]{:S(2)}) collective-permute-start(f32[16,8,1024]{2,1,0:T(8,128)} %get-tuple-element.182), channel_id=1, source_target_pairs={{0,32},{32,64},{64,96},{96,128},{128,160},{160,192},{192,224},{224... | collective-permute-start | bytes 1572872 | tf_op jit(solution)/shard_map/ppermute | solution.py:17
  197.9 26.2 %collective-permute-start.11 = (f32[16,8,1024]{2,1,0:T(8,128)}, f32[16,8,1024]{2,1,0:T(8,128)}, u32[]{:S(2)}, u32[]{:S(2)}) collective-permute-start(f32[16,8,1024]{2,1,0:T(8,128)} %get-tuple-element.181), channel_id=1, source_target_pairs={{32,0},{64,32},{96,64},{128,96},{160,128},{192,160},{224,192},{0,2... | collective-permute-start | bytes 1572872 | tf_op jit(solution)/shard_map/ppermute | solution.py:20
  199.2 26.9 %copy-start.12 = (bf16[256,512]{1,0:T(8,128)(2,1)S(1)}, bf16[256,512]{1,0:T(8,128)(2,1)}, u32[]{:S(2)}) copy-start(bf16[256,512]{1,0:T(8,128)(2,1)} %copy-done.11) | copy-start | bytes 786436
  226.1 55.4 %copy-start.6 = (bf16[1,16,16,512]{3,2,1,0:T(8,128)(2,1)S(1)}, bf16[1,16,16,512]{3,2,1,0:T(8,128)(2,1)}, u32[]{:S(2)}) copy-start(bf16[1,16,16,512]{3,2,1,0:T(8,128)(2,1)} %param.32) | copy-start | bytes 786436
  226.1 55.4 %copy-start.16 = (bf16[512,512]{1,0:T(8,128)(2,1)S(1)}, bf16[512,512]{1,0:T(8,128)(2,1)}, u32[]{:S(2)}) copy-start(bf16[512,512]{1,0:T(8,128)(2,1)} %param.35) | copy-start | bytes 1572868
  226.1 56.4 %copy-start.18 = (f32[512]{0:T(512)S(1)}, f32[512]{0:T(512)}, u32[]{:S(2)}) copy-start(f32[512]{0:T(512)} %param.36) | copy-start | bytes 6148
  228.4 656.5 %all-reduce.5.cloned.1.call-start = ((), (), s32[]{:S(2)}) async-start(), calls=%async_computation.4 | async-start | bytes 2097152 | tf_op jit(solution)/shard_map/psum | solution.py:183
  (6 other events, 14.5 us)
Sparse Core Ops, SparseCore 0:
  171.7 51.0 reduce-scatter.4
  228.5 52.8 reduce-scatter.2
  284.1 600.7 all-reduce.4
where the time goes:
time: 907 us; the launch traced here: 895 us
  waiting for transfers between devices  556 us (61%)
  blocking collectives  151 us (17%)
  local copies, waits for them, and re-layouts  76.9 us (8%)
  other arithmetic  49.1 us (5%)
  matrix products  24.9 us (3%)
  starting transfers between devices  21.5 us (2%)
  between operations  15.1 us (2%)
    psum x1, waiting for transfers between devices, plane_sum(): return lax.psum((gradients[0], gradients[1], gradients[2]), ('lon', 'lat'))  448 us
    psum x1, blocking collectives, plane_sum(): return lax.psum((gradients[0], gradients[1], gradients[2]), ('lon', 'lat'))  144 us
    ppermute x6, waiting for transfers between devices, with_halo(): lax.ppermute(lax.slice_in_dim(block, block.shape[dim] - width, None, axis...  52.8 us
    reduce_scatter x1, waiting for transfers between devices, level_share(): lax.psum_scatter(gradients[0], 'lev', scatter_dimension=0, tiled=True)  51.7 us
  transfers between devices with their start and end apart: 15, of which 7 were waited for; matrix products, arithmetic and copies ran while one was open for 5% of the time, Pallas kernels for 0%

commit v1 on v0

--- a/solution.py
+++ b/solution.py
@@ -1,8 +1,11 @@
 import jax
 import jax.numpy as jnp
 from jax import lax
+from jax.experimental import pallas as pl
+from jax.experimental.pallas import tpu as pltpu
 from jax.sharding import PartitionSpec as P
 
+MESH = pl.DeviceIdType.MESH
 HEADS = 8
 WIN = 8
 
@@ -179,16 +182,175 @@
     return middle.at[:, inner_cols - window_side :].add(arrived[:, inner_cols + window_side :])
 
 
-def plane_sum(gradients):
-    return lax.psum((gradients[0], gradients[1], gradients[2]), ("lon", "lat"))
-
-
-def level_share(gradients):
-    return (
-        lax.psum_scatter(gradients[0], "lev", scatter_dimension=0, tiled=True),
-        lax.psum_scatter(gradients[1], "lev", scatter_dimension=0, tiled=True),
-        lax.psum_scatter(gradients[2], "lev", scatter_dimension=0, tiled=True),
-    )
+def reduce_kernel(wg_ref, out_ref, r1, a1, r2, a2, r3, a3, g4, g5,
+                  s1, v1, s2, v2, s3, v3, s4, v4, s5, v5):
+    lon = lax.axis_index("lon")
+    lat = lax.axis_index("lat")
+    lev = lax.axis_index("lev")
+    hi = lev // 2
+    core = lev % 2
+    here = hi * 8 + lon
+    barrier = pltpu.get_barrier_semaphore()
+
+    def plane_peer(step):
+        there = (here + step) % 16
+        return there // 8, there % 8
+
+    def greet_plane(step, carry):
+        peer_hi, peer_lon = plane_peer(step)
+        pl.semaphore_signal(
+            barrier, inc=1, device_id=(peer_lon, lat, peer_hi * 2 + core), device_id_type=MESH
+        )
+        return carry
+
+    def greet_lat(step, carry):
+        pl.semaphore_signal(
+            barrier, inc=1, device_id=(lon, (lat + step) % 8, lev), device_id_type=MESH
+        )
+        return carry
+
+    pl.semaphore_signal(
+        barrier, inc=1, device_id=(lon, lat, hi * 2 + 1 - core), device_id_type=MESH
+    )
+    lax.fori_loop(1, 16, greet_plane, 0)
+    lax.fori_loop(1, 8, greet_lat, 0)
+    pl.semaphore_wait(barrier, 23)
+
+    def pair_copy(part):
+        return pltpu.make_async_remote_copy(
+            src_ref=wg_ref.at[part * 2 + 1 - core],
+            dst_ref=r1.at[part],
+            send_sem=s1.at[part],
+            recv_sem=v1.at[part],
+            device_id=(lon, lat, hi * 2 + 1 - core),
+            device_id_type=MESH,
+        )
+
+    for part in range(2):
+        pair_copy(part).start()
+    for part in range(2):
+        pair_copy(part).wait()
+
+        def add_pair(piece, carry):
+            rows = pl.ds(pl.multiple_of(piece * 16, 16), 16)
+            total = wg_ref[part * 2 + core, rows, :].astype(jnp.float32) + r1[
+                part, rows, :
+            ].astype(jnp.float32)
+            a1[part * 8 + piece] = total.astype(jnp.bfloat16)
+            return carry
+
+        lax.fori_loop(0, 8, add_pair, 0)
+
+    def plane_copy(step):
+        peer_hi, peer_lon = plane_peer(step)
+        return pltpu.make_async_remote_copy(
+            src_ref=a1.at[peer_hi * 8 + peer_lon],
+            dst_ref=r2.at[step - 1],
+            send_sem=s2.at[step - 1],
+            recv_sem=v2.at[step - 1],
+            device_id=(peer_lon, lat, peer_hi * 2 + core),
+            device_id_type=MESH,
+        )
+
+    def begin(copy):
+        def one(step, carry):
+            copy(step).start()
+            return carry
+
+        return one
+
+    def finish(copy):
+        def one(step, carry):
+            copy(step).wait()
+            return carry
+
+        return one
+
+    lax.fori_loop(1, 16, begin(plane_copy), 0)
+    lax.fori_loop(1, 16, finish(plane_copy), 0)
+    for part in range(8):
+        cols = slice(part * 256, (part + 1) * 256)
+        total = a1[here, :, cols].astype(jnp.float32)
+        for step in range(15):
+            total = total + r2[step, :, cols].astype(jnp.float32)
+        a2[part] = total.astype(jnp.bfloat16)
+
+    def lat_copy(step):
+        peer = (lat + step) % 8
+        return pltpu.make_async_remote_copy(
+            src_ref=a2.at[peer],
+            dst_ref=r3.at[step - 1],
+            send_sem=s3.at[step - 1],
+            recv_sem=v3.at[step - 1],
+            device_id=(lon, peer, lev),
+            device_id_type=MESH,
+        )
+
+    lax.fori_loop(1, 8, begin(lat_copy), 0)
+    lax.fori_loop(1, 8, finish(lat_copy), 0)
+    total = a2[lat].astype(jnp.float32)
+    for step in range(7):
+        total = total + r3[step].astype(jnp.float32)
+    a3[...] = total.astype(jnp.bfloat16)
+    g4[lat] = a3[...]
+
+    def lat_gather(step):
+        return pltpu.make_async_remote_copy(
+            src_ref=a3,
+            dst_ref=g4.at[lat],
+            send_sem=s4.at[step - 1],
+            recv_sem=v4.at[step - 1],
+            device_id=(lon, (lat + step) % 8, lev),
+            device_id_type=MESH,
+        )
+
+    lax.fori_loop(1, 8, begin(lat_gather), 0)
+    lax.fori_loop(1, 8, finish(lat_gather), 0)
+    g5[lon] = g4[...]
+
+    def lon_gather(step):
+        return pltpu.make_async_remote_copy(
+            src_ref=g4,
+            dst_ref=g5.at[lon],
+            send_sem=s5.at[step - 1],
+            recv_sem=v5.at[step - 1],
+            device_id=((lon + step) % 8, lat, lev),
+            device_id_type=MESH,
+        )
+
+    lax.fori_loop(1, 8, begin(lon_gather), 0)
+    lax.fori_loop(1, 8, finish(lon_gather), 0)
+    for row in range(8):
+        for col in range(8):
+            out_ref[row * 16 : (row + 1) * 16, col * 256 : (col + 1) * 256] = g5[row, col].astype(
+                jnp.float32
+            )
+
+
+def reduce_weights(wg):
+    dma = pltpu.SemaphoreType.DMA
+    low = jnp.bfloat16
+    return pl.pallas_call(
+        reduce_kernel,
+        out_shape=jax.ShapeDtypeStruct((128, 2048), jnp.float32),
+        in_specs=[pl.BlockSpec(memory_space=pltpu.VMEM)],
+        out_specs=pl.BlockSpec(memory_space=pltpu.VMEM),
+        scratch_shapes=[
+            pltpu.VMEM((2, 128, 2048), low),
+            pltpu.VMEM((16, 16, 2048), low),
+            pltpu.VMEM((15, 16, 2048), low),
+            pltpu.VMEM((8, 16, 256), low),
+            pltpu.VMEM((7, 16, 256), low),
+            pltpu.VMEM((16, 256), low),
+            pltpu.VMEM((8, 16, 256), low),
+            pltpu.VMEM((8, 8, 16, 256), low),
+            dma((2,)), dma((2,)), dma((15,)), dma((15,)), dma((7,)), dma((7,)),
+            dma((7,)), dma((7,)), dma((7,)), dma((7,)),
+        ],
+        compiler_params=pltpu.CompilerParams(
+            collective_id=1, has_side_effects=True, vmem_limit_bytes=40 << 20
+        ),
+    )(wg)
 
 
 def on_device(tokens_in, cotangent, qkv_weight, out_weight, norm_gain, ocean_mask):
@@ -269,7 +431,6 @@
     )
     grad_hidden = jnp.einsum("tc,dc->td", grad_qkv, qkv_weight, preferred_element_type=jnp.float32)
     qkv_grad_local = jnp.einsum("td,tc->dc", hidden, grad_qkv, preferred_element_type=jnp.float32)
-    gain_grad_local = jnp.sum(grad_hidden * normed, axis=0)
     scaled = grad_hidden * norm_gain
     correction = (
         scaled
@@ -281,8 +442,14 @@
         .astype(jnp.bfloat16)
         .reshape(tokens_in.shape)
     )
-    local_grads = (qkv_grad_local, out_grad_local, gain_grad_local)
-    qkv_grad, out_grad, gain_grad = level_share(plane_sum(local_grads))
+    wg = jnp.concatenate([qkv_grad_local, out_grad_local], axis=1).astype(jnp.bfloat16)
+    shared = reduce_weights(wg.reshape(4, features // 4, 4 * features))
+    qkv_grad = shared[:, : 3 * features]
+    out_grad = shared[:, 3 * features :]
+    first = lax.axis_index("lev") * (features // 4)
+    weight_rows = lax.dynamic_slice_in_dim(qkv_weight, first, features // 4, 0)
+    gain_rows = lax.dynamic_slice_in_dim(norm_gain, first, features // 4, 0)
+    gain_grad = jnp.sum(weight_rows.astype(jnp.float32) * qkv_grad, axis=1) / gain_rows
     return (layer_out, input_grad, qkv_grad, out_grad, gain_grad)
 
 

time: 907 us -> 260 us (0.29); the launches traced: 895 us -> 259 us
  waiting for transfers between devices: 556 us -> 38.1 us
  blocking collectives: 151 us -> 0 us
  Pallas kernels: 0 us -> 46.4 us
  between operations: 15.1 us -> 1.31 us
    psum x1 -> x0, waiting for transfers between devices: 448 us -> none  [plane_sum(): return lax.psum((gradients[0], gradients[1], gradients[2]), ('lon', 'lat'))]
    psum x1 -> x0, blocking collectives: 144 us -> none  [plane_sum(): return lax.psum((gradients[0], gradients[1], gradients[2]), ('lon', 'lat'))]
    reduce_scatter x2 -> x0, waiting for transfers between devices: 51.7 us -> none  [the longest x1 51.7 us: level_share(): lax.psum_scatter(gradients[0], 'lev', scatter_dimension=0, tiled=True)]
    pallas_call x0 -> x1, Pallas kernels: none -> 46.4 us  [reduce_weights(): pl.pallas_call(reduce_kernel, out_shape=jax.ShapeDtypeStruct((128, 2048),...]
    ppermute x6, waiting for transfers between devices: 52.8 us -> 33.4 us  [with_halo(): lax.ppermute(lax.slice_in_dim(block, block.shape[dim] - width, None, axis...]
  transfers between devices with their start and end apart: 15 -> 12, of which waited for: 7 -> 5; matrix products, arithmetic and copies ran while one was open for 5% -> 17% of each run, Pallas kernels for 0% -> 0%
where the time goes in v1:
time: 260 us; the launch traced here: 259 us
  local copies, waits for them, and re-layouts  78.8 us (30%)
  other arithmetic  47.3 us (18%)
  Pallas kernels  46.4 us (18%)
  waiting for transfers between devices  38.1 us (15%)
  matrix products  25.6 us (10%)
  starting transfers between devices  21.1 us (8%)
    pallas_call x1, Pallas kernels, reduce_weights(): pl.pallas_call(reduce_kernel, out_shape=jax.ShapeDtypeStruct((128, 2048),...  46.4 us
    ppermute x6, waiting for transfers between devices, with_halo(): lax.ppermute(lax.slice_in_dim(block, block.shape[dim] - width, None, axis...  33.4 us
    scatter-add x3, local copies, waits for them, and re-layouts, spread_back(): totals = totals.at[lat_step * window_side:(lat_step + lat_windows) * wind...  16.4 us
    scatter-add x6, other arithmetic, spread_back(): totals = totals.at[lat_step * window_side:(lat_step + lat_windows) * wind...  15.1 us
    ppermute x6, starting transfers between devices, with_halo(): lax.ppermute(lax.slice_in_dim(block, block.shape[dim] - width, None, axis...  12.7 us
    another operation x4, other arithmetic  8.7 us
    ppermute x6, starting transfers between devices, with_halo(): lax.ppermute(lax.slice_in_dim(block, 0, width, axis=dim), axis, backward)  8.41 us
    transpose x10, local copies, waits for them, and re-layouts, from_windows(): jnp.transpose(grid_out, (0, 2, 1, 3, 4))  7.75 us
  transfers between devices with their start and end apart: 12, of which 5 were waited for; matrix products, arithmetic and copies ran while one was open for 17% of the time, Pallas kernels for 0%

profile of v1, /device:TPU:8, one launch (start us, length us, event | category | flops | bytes accessed | tf_op | source)
XLA Modules:
  0.0 258.6 jit_solution(5205684373057870464)
XLA Ops:
  3.4 3.9 %collective-permute-start.5 = (bf16[8,16]{1,0:T(8,128)(2,1)S(1)}, bf16[8,16]{1,0:T(8,128)(2,1)S(1)}, u32[]{:S(2)}, u32[]{:S(2)}) collective-permute-start(bf16[8,16]{1,0:T(8,128)(2,1)S(1)} %get-tuple-element.211), channel_id=1, source_target_pairs={{4,0},{8,4},{12,8},{16,12},{20,16},{24,20},{28,24},{0,28},{5,1},{9... | collective-permute-start | bytes 776 | tf_op jit(solution)/shard_map/ppermute | solution.py:23
  31.7 20.1 %collective-permute-done.2 = bf16[32,8,1024]{2,1,0:T(8,128)(2,1)S(1)} collective-permute-done((bf16[32,8,1024]{2,1,0:T(8,128)(2,1)}, bf16[32,8,1024]{2,1,0:T(8,128)(2,1)S(1)}, u32[]{:S(2)}, u32[]{:S(2)}) %collective-permute-start.2) | collective-permute-done | bytes 524320 | tf_op jit(solution)/shard_map/ppermute | solution.py:20
  54.8 2.6 %fusion.37 = (bf16[4,576,512]{2,1,0:T(8,128)(2,1)}, bf16[4,576,512]{2,1,0:T(8,128)(2,1)}) fusion(bf16[4,576,1024]{2,1,0:T(8,128)(2,1)S(1)} %constant_dynamic-update-slice_fusion), kind=kLoop, calls=%fused_computation.124 | loop fusion | bytes 9437184 | tf_op jit(solution)/shard_map/slice | solution.py:402
  57.4 3.1 %copy.79 = bf16[4,576,512]{1,2,0:T(8,128)(2,1)S(1)} copy(bf16[4,576,512]{2,1,0:T(8,128)(2,1)} %get-tuple-element.176) | data formatting | bytes 4718592 | tf_op jit(solution)/shard_map/slice | solution.py:402
  60.5 4.4 %copy.77 = bf16[4,576,512]{1,2,0:T(8,128)(2,1)} copy(bf16[4,576,512]{2,1,0:T(8,128)(2,1)} %get-tuple-element.177) | data formatting | bytes 4718592 | tf_op jit(solution)/shard_map/slice | solution.py:403
  64.9 5.2 %fusion.48 = (f32[4,8,64]{2,1,0:T(8,128)S(1)}, f32[4,8,64,576]{3,2,1,0:T(8,128)}) fusion(f32[4,576]{1,0:T(4,128)S(1)} %multiply_bitcast_fusion, bf16[4,64,8,64]{1,3,2,0:T(8,128)(2,1)} %copy.96, bf16[4,576,8,64]{1,3,2,0:T(8,128)(2,1)S(1)} %bitcast.246), kind=kOutput, calls=%fused_computation.135 | convolution fusion | flops 155714112 | bytes 7357440 | tf_op jit(solution)/shard_map/sub | solution.py:105
  70.1 3.0 %fusion.4 = bf16[4,8,64,576]{3,2,1,0:T(8,128)(2,1)S(1)} fusion(f32[4,8,64,576]{3,2,1,0:T(8,128)} %get-tuple-element.217, f32[4,8,64]{2,1,0:T(8,128)S(1)} %get-tuple-element.216), kind=kLoop, calls=%fused_computation.26 | loop fusion | flops 2359296 | bytes 7086080 | tf_op jit(solution)/shard_map/convert_element_type | solution.py:107
  73.2 3.2 %fusion.50 = f32[4,8,64,576]{3,2,1,0:T(8,128)} fusion(bf16[4,64,8,64]{1,3,2,0:T(8,128)(2,1)S(1)} %copy-done.13, bf16[4,8,64,576]{3,2,1,0:T(8,128)(2,1)S(1)} %fusion.4), kind=kOutput, calls=%fused_computation.137 | convolution fusion | flops 150994944 | bytes 7340032 | tf_op jit(solution)/shard_map/whqk,wqhd->wkhd/dot_general | solution.py:150
  79.9 3.2 %fusion.49 = f32[4,8,64,576]{3,2,1,0:T(8,128)} fusion(bf16[4,64,8,64]{1,3,2,0:T(8,128)(2,1)S(1)} %copy-done.7, bf16[4,8,64,576]{3,2,1,0:T(8,128)(2,1)S(1)} %multiply_convert_fusion), kind=kOutput, calls=%fused_computation.136 | convolution fusion | flops 150994944 | bytes 7340032 | tf_op jit(solution)/shard_map/whqk,wqhd->wkhd/dot_general | solution.py:147
  83.1 5.7 %copy.98 = f32[4,576,512]{2,1,0:T(8,128)} copy(f32[4,576,512]{1,2,0:T(8,128)} %bitcast.245) | data formatting | bytes 9437184 | tf_op jit(solution)/shard_map/reshape | solution.py:149
  88.8 5.7 %copy.99 = f32[4,576,512]{2,1,0:T(8,128)} copy(f32[4,576,512]{1,2,0:T(8,128)} %bitcast.244) | data formatting | bytes 9437184 | tf_op jit(solution)/shard_map/reshape | solution.py:155
  94.6 4.1 %pad_maximum_fusion.1 = (f32[4,64,1024]{2,1,0:T(8,128)S(1)}, f32[4,64,1024]{2,1,0:T(8,128)S(1)}, f32[4,64,1024]{2,1,0:T(8,128)S(1)}, f32[4,64,1024]{2,1,0:T(8,12...) fusion(f32[4,576,512]{2,1,0:T(8,128)} %copy.99, ...), kind=kLoop, calls=%fused_computation.53 | loop fusion | flops 2359296 | bytes 18874368 | tf_op jit(solution)/shard_map/concatenate | solution.py:156
  106.4 2.5 scatter-add.44
  108.9 3.2 %add_select_fusion.1 = f32[16,16,1024]{2,1,0:T(8,128)} fusion(f32[16,16,1024]{2,1,0:T(8,128)S(1)} %bitcast.273, s32[]{:T(128)} %bitcast.70, s32[]{:T(128)} %bitcast.71, f32[16,16,1024]{2,1,0:T(8,128)S(1)} %bitcast.253, pred[]{:T(512)} %get-tuple-element.164), kind=kLoop, calls=%fused_computation.30 | loop fusion | flops 524288 | bytes 3145737 | tf_op jit(solution)/shard_map/select.14
  112.1 7.3 %scatter-add.45 = f32[32,32,1024]{2,1,0:T(8,128)} dynamic-update-slice(f32[32,32,1024]{2,1,0:T(8,128)} %scatter-add.44, f32[16,16,1024]{2,1,0:T(8,128)} %add_select_fusion.1, s32[]{:T(128)} %bitcast.70, s32[]{:T(128)} %bitcast.71, s32[]{:T(128)} %constant.392.clone.1) | dynamic-update-slice | bytes 2097156 | tf_op jit(solution)/shard_map/scatter-add | solution.py:81
  119.4 4.7 %add_select_fusion = f32[16,16,1024]{2,1,0:T(8,128)} fusion(f32[16,16,1024]{2,1,0:T(8,128)} %bitcast.272, f32[32,32,1024]{2,1,0:T(8,128)} %scatter-add.45, s32[]{:T(128)} %bitcast.75, s32[]{:T(128)} %bitcast.76, pred[]{:T(512)} %get-tuple-element.163), kind=kLoop, calls=%fused_computation.29 | loop fusion | flops 524288 | bytes 3145737 | tf_op jit(solution)/shard_map/select.15
  124.1 6.7 %scatter-add.46 = f32[32,32,1024]{2,1,0:T(8,128)} dynamic-update-slice(f32[32,32,1024]{2,1,0:T(8,128)} %scatter-add.45, f32[16,16,1024]{2,1,0:T(8,128)} %add_select_fusion, s32[]{:T(128)} %bitcast.75, s32[]{:T(128)} %bitcast.76, s32[]{:T(128)} %constant.392.clone.1) | dynamic-update-slice | bytes 2097156 | tf_op jit(solution)/shard_map/scatter-add | solution.py:81
  130.8 2.8 %fusion.23 = f32[32,32,1024]{2,1,0:T(8,128)} fusion(f32[32,32,1024]{2,1,0:T(8,128)} %scatter-add.46, f32[16,16,1024]{2,1,0:T(8,128)} %bitcast.262), kind=kLoop, calls=%fused_computation.65 | loop fusion | flops 262144 | bytes 3145728 | tf_op jit(solution)/shard_map/scatter-add | solution.py:81
  133.6 2.8 %fusion.22 = f32[32,32,1024]{2,1,0:T(8,128)} fusion(f32[32,32,1024]{2,1,0:T(8,128)} %fusion.23, f32[16,16,1024]{2,1,0:T(8,128)} %bitcast.261), kind=kLoop, calls=%fused_computation.63 | loop fusion | flops 262144 | bytes 3145728 | tf_op jit(solution)/shard_map/scatter-add | solution.py:81
  136.4 2.4 fusion.21
  138.9 2.4 fusion.20
  143.6 2.4 fusion.18
  145.9 3.2 %fusion.38 = (f32[8,32,1024]{2,1,0:T(8,128)}, f32[8,32,1024]{2,1,0:T(8,128)}) fusion(f32[32,32,1024]{2,1,0:T(8,128)} %fusion.18), kind=kLoop, calls=%fused_computation.125 | loop fusion | bytes 4194304 | tf_op jit(solution)/shard_map/slice | solution.py:163
  149.1 3.3 %collective-permute-start.8 = (f32[8,32,1024]{2,1,0:T(8,128)}, f32[8,32,1024]{2,1,0:T(8,128)}, u32[]{:S(2)}, u32[]{:S(2)}) collective-permute-start(f32[8,32,1024]{2,1,0:T(8,128)} %get-tuple-element.179), channel_id=1, source_target_pairs={{0,4},{4,8},{8,12},{12,16},{16,20},{20,24},{24,28},{1,5},{5,9},{9,... | collective-permute-start | bytes 3145736 | tf_op jit(solution)/shard_map/ppermute | solution.py:20
  156.5 3.2 %slice.633 = f32[16,32,1024]{2,1,0:T(8,128)} slice(f32[32,32,1024]{2,1,0:T(8,128)} %fusion.18), slice={[8:24], [0:32], [0:1024]} | slice | bytes 4194304 | tf_op jit(solution)/shard_map/slice | solution.py:166
  159.7 2.5 copy.90
  164.5 3.7 %fusion.5 = bf16[4,64,8,64]{1,3,2,0:T(8,128)(2,1)} fusion(bf16[4,576,8,64]{1,3,2,0:T(8,128)(2,1)S(1)} %bitcast.247, bf16[4,8,64,576]{3,2,1,0:T(8,128)(2,1)} %copy-done.1), kind=kOutput, calls=%fused_computation.35 | convolution fusion | flops 151126016 | bytes 4980736 | tf_op jit(solution)/shard_map/whqk,wkhd->wqhd/dot_general | solution.py:140
  168.2 4.2 %collective-permute-done.8 = f32[8,32,1024]{2,1,0:T(8,128)} collective-permute-done((f32[8,32,1024]{2,1,0:T(8,128)}, f32[8,32,1024]{2,1,0:T(8,128)}, u32[]{:S(2)}, u32[]{:S(2)}) %collective-permute-start.8) | collective-permute-done | bytes 1048608 | tf_op jit(solution)/shard_map/ppermute | solution.py:20
  174.0 3.5 %collective-permute-done.9 = f32[8,32,1024]{2,1,0:T(8,128)} collective-permute-done((f32[8,32,1024]{2,1,0:T(8,128)}, f32[8,32,1024]{2,1,0:T(8,128)}, u32[]{:S(2)}, u32[]{:S(2)}) %collective-permute-start.9) | collective-permute-done | bytes 1048608 | tf_op jit(solution)/shard_map/ppermute | solution.py:23
  181.4 3.9 %collective-permute-start.10 = (f32[16,8,1024]{2,1,0:T(8,128)}, f32[16,8,1024]{2,1,0:T(8,128)}, u32[]{:S(2)}, u32[]{:S(2)}) collective-permute-start(f32[16,8,1024]{2,1,0:T(8,128)} %get-tuple-element.181), channel_id=1, source_target_pairs={{0,32},{32,64},{64,96},{96,128},{128,160},{160,192},{192,224},{224... | collective-permute-start | bytes 1572872 | tf_op jit(solution)/shard_map/ppermute | solution.py:20
  194.6 9.1 %collective-permute-done.10 = f32[16,8,1024]{2,1,0:T(8,128)} collective-permute-done((f32[16,8,1024]{2,1,0:T(8,128)}, f32[16,8,1024]{2,1,0:T(8,128)}, u32[]{:S(2)}, u32[]{:S(2)}) %collective-permute-start.10) | collective-permute-done | bytes 524320 | tf_op jit(solution)/shard_map/ppermute | solution.py:20
  209.0 46.4 %shard_map.101 = f32[128,2048]{1,0:T(8,128)S(1)} custom-call(bf16[4,128,2048]{2,1,0:T(8,128)(2,1)S(1)} %pad_maximum_fusion.wg_ref), custom_call_target="tpu_custom_call" | custom-call | tf_op jit(solution)/shard_map/pallas_call | solution.py:333
  (193 shorter events, 72.9 us)
Async XLA Ops:
  0.6 15.5 %copy-start = (bf16[512,512]{1,0:T(8,128)(2,1)S(1)}, bf16[512,512]{1,0:T(8,128)(2,1)}, u32[]{:S(2)}) copy-start(bf16[512,512]{1,0:T(8,128)(2,1)} %param.35) | copy-start | bytes 1572868
  0.6 15.3 %copy-start.15 = (bf16[1,16,16,512]{3,2,1,0:T(8,128)(2,1)S(1)}, bf16[1,16,16,512]{3,2,1,0:T(8,128)(2,1)}, u32[]{:S(2)}) copy-start(bf16[1,16,16,512]{3,2,1,0:T(8,128)(2,1)} %param.33) | copy-start | bytes 786436
  1.4 21.6 %collective-permute-start.4 = (bf16[8,16]{1,0:T(8,128)(2,1)S(1)}, bf16[8,16]{1,0:T(8,128)(2,1)S(1)}, u32[]{:S(2)}, u32[]{:S(2)}) collective-permute-start(bf16[8,16]{1,0:T(8,128)(2,1)S(1)} %get-tuple-element.210), channel_id=1, source_target_pairs={{0,4},{4,8},{8,12},{12,16},{16,20},{20,24},{24,28},{28,0},{1,5},{5... | collective-permute-start | bytes 776 | tf_op jit(solution)/shard_map/ppermute | solution.py:20
  3.4 19.7 %collective-permute-start.5 = (bf16[8,16]{1,0:T(8,128)(2,1)S(1)}, bf16[8,16]{1,0:T(8,128)(2,1)S(1)}, u32[]{:S(2)}, u32[]{:S(2)}) collective-permute-start(bf16[8,16]{1,0:T(8,128)(2,1)S(1)} %get-tuple-element.211), channel_id=1, source_target_pairs={{4,0},{8,4},{12,8},{16,12},{20,16},{24,20},{28,24},{0,28},{5,1},{9... | collective-permute-start | bytes 776 | tf_op jit(solution)/shard_map/ppermute | solution.py:23
  10.8 5.7 %copy-start.16 = (bf16[256,512]{1,0:T(8,128)(2,1)}, bf16[256,512]{1,0:T(8,128)(2,1)S(1)}, u32[]{:S(2)}) copy-start(bf16[256,512]{1,0:T(8,128)(2,1)S(1)} %multiply_convert_fusion.3) | copy-start | bytes 786436
  13.8 11.4 %collective-permute-start.1 = (bf16[8,16,1024]{2,1,0:T(8,128)(2,1)}, bf16[8,16,1024]{2,1,0:T(8,128)(2,1)}, u32[]{:S(2)}, u32[]{:S(2)}) collective-permute-start(bf16[8,16,1024]{2,1,0:T(8,128)(2,1)} %bitcast.5), channel_id=1, source_target_pairs={{4,0},{8,4},{12,8},{16,12},{20,16},{24,20},{28,24},{0,28},{5,1},{9... | collective-permute-start | bytes 786440 | tf_op jit(solution)/shard_map/ppermute | solution.py:23
  15.8 9.4 %collective-permute-start = (bf16[8,16,1024]{2,1,0:T(8,128)(2,1)}, bf16[8,16,1024]{2,1,0:T(8,128)(2,1)}, u32[]{:S(2)}, u32[]{:S(2)}) collective-permute-start(bf16[8,16,1024]{2,1,0:T(8,128)(2,1)} %bitcast.3), channel_id=1, source_target_pairs={{0,4},{4,8},{8,12},{12,16},{16,20},{20,24},{24,28},{28,0},{1,5},{5... | collective-permute-start | bytes 786440 | tf_op jit(solution)/shard_map/ppermute | solution.py:20
  16.1 4.7 %copy-start.21 = (s32[3]{0:T(128)S(1)}, s32[3]{0:T(128)}, u32[]{:S(2)}) copy-start(s32[3]{0:T(128)} %constant.401.clone.1) | copy-start | bytes 40
  23.1 6.6 %collective-permute-start.6 = (bf16[32,8]{1,0:T(8,128)(2,1)S(1)}, bf16[32,8]{1,0:T(8,128)(2,1)S(1)}, u32[]{:S(2)}, u32[]{:S(2)}) collective-permute-start(bf16[32,8]{1,0:T(8,128)(2,1)S(1)} %get-tuple-element.206), channel_id=1, source_target_pairs={{0,32},{32,64},{64,96},{96,128},{128,160},{160,192},{192,224},{224... | collective-permute-start | bytes 1544 | tf_op jit(solution)/shard_map/ppermute | solution.py:20
  24.5 5.3 %collective-permute-start.7 = (bf16[32,8]{1,0:T(8,128)(2,1)S(1)}, bf16[32,8]{1,0:T(8,128)(2,1)S(1)}, u32[]{:S(2)}, u32[]{:S(2)}) collective-permute-start(bf16[32,8]{1,0:T(8,128)(2,1)S(1)} %get-tuple-element.207), channel_id=1, source_target_pairs={{32,0},{64,32},{96,64},{128,96},{160,128},{192,160},{224,192},{0,2... | collective-permute-start | bytes 1544 | tf_op jit(solution)/shard_map/ppermute | solution.py:23
  27.2 24.5 %collective-permute-start.2 = (bf16[32,8,1024]{2,1,0:T(8,128)(2,1)}, bf16[32,8,1024]{2,1,0:T(8,128)(2,1)S(1)}, u32[]{:S(2)}, u32[]{:S(2)}) collective-permute-start(bf16[32,8,1024]{2,1,0:T(8,128)(2,1)} %get-tuple-element.191), channel_id=1, source_target_pairs={{0,32},{32,64},{64,96},{96,128},{128,160},{160,192},{192,224},{224... | collective-permute-start | bytes 1572872 | tf_op jit(solution)/shard_map/ppermute | solution.py:20
  29.5 22.3 %collective-permute-start.3 = (bf16[32,8,1024]{2,1,0:T(8,128)(2,1)S(1)}, bf16[32,8,1024]{2,1,0:T(8,128)(2,1)S(1)}, u32[]{:S(2)}, u32[]{:S(2)}) collective-permute-start(bf16[32,8,1024]{2,1,0:T(8,128)(2,1)S(1)} %get-tuple-element.192), channel_id=1, source_target_pairs={{32,0},{64,32},{96,64},{128,96},{160,128},{192,160},{224,192},{0,2... | collective-permute-start | bytes 1572872 | tf_op jit(solution)/shard_map/ppermute | solution.py:23
  70.1 8.3 %slice-start = ((s8[5242880]{0:T(1024)(128)(4,1)}), s8[4194304]{0:T(1024)(128)(4,1)S(1)}, s32[]{:S(2)}) async-start(s8[5242880]{0:T(1024)(128)(4,1)} %bitcast.248), calls=%async_computation | async-start | bytes 8388608
  73.2 3.3 %copy-start.5 = (bf16[4,576,512]{1,2,0:T(8,128)(2,1)S(1)}, bf16[4,576,512]{1,2,0:T(8,128)(2,1)}, u32[]{:S(2)}) copy-start(bf16[4,576,512]{1,2,0:T(8,128)(2,1)} %copy.77) | copy-start | bytes 7077892
  73.2 3.3 %copy-start.12 = (f32[4,8,64,64]{2,3,1,0:T(8,128)S(1)}, f32[4,8,64,64]{2,3,1,0:T(8,128)}, u32[]{:S(2)}) copy-start(f32[4,8,64,64]{2,3,1,0:T(8,128)} %copy.116) | copy-start | bytes 1572868
  73.2 5.2 %slice-start.1 = ((s8[5242880]{0:T(1024)(128)(4,1)}), s8[1048576]{0:T(1024)(128)(4,1)S(1)}, s32[]{:S(2)}) async-start(s8[5242880]{0:T(1024)(128)(4,1)} %bitcast.248), calls=%async_computation.1 | async-start | bytes 2097152
  79.9 3.2 %copy-start.1 = (bf16[4,8,64,576]{3,2,1,0:T(8,128)(2,1)}, bf16[4,8,64,576]{3,2,1,0:T(8,128)(2,1)S(1)}, u32[]{:S(2)}) copy-start(bf16[4,8,64,576]{3,2,1,0:T(8,128)(2,1)S(1)} %multiply_convert_fusion) | copy-start | bytes 7077892
  130.8 5.7 %copy-start.11 = (f32[2,8,2,8,1024]{4,3,2,1,0:T(8,128)S(1)}, f32[2,8,2,8,1024]{4,3,2,1,0:T(8,128)}, u32[]{:S(2)}) copy-start(f32[2,8,2,8,1024]{4,3,2,1,0:T(8,128)} %copy.105) | copy-start | bytes 3145732
  130.8 8.1 %copy-start.9 = (f32[2,8,2,8,1024]{4,3,2,1,0:T(8,128)S(1)}, f32[2,8,2,8,1024]{4,3,2,1,0:T(8,128)}, u32[]{:S(2)}) copy-start(f32[2,8,2,8,1024]{4,3,2,1,0:T(8,128)} %copy.106) | copy-start | bytes 3145732
  133.6 7.6 %copy-start.10 = (f32[2,8,2,8,1024]{4,3,2,1,0:T(8,128)S(1)}, f32[2,8,2,8,1024]{4,3,2,1,0:T(8,128)}, u32[]{:S(2)}) copy-start(f32[2,8,2,8,1024]{4,3,2,1,0:T(8,128)} %copy.107) | copy-start | bytes 3145732
  136.4 7.1 %copy-start.8 = (f32[2,8,2,8,1024]{4,3,2,1,0:T(8,128)S(1)}, f32[2,8,2,8,1024]{4,3,2,1,0:T(8,128)}, u32[]{:S(2)}) copy-start(f32[2,8,2,8,1024]{4,3,2,1,0:T(8,128)} %copy.108) | copy-start | bytes 3145732
  149.1 23.2 %collective-permute-start.8 = (f32[8,32,1024]{2,1,0:T(8,128)}, f32[8,32,1024]{2,1,0:T(8,128)}, u32[]{:S(2)}, u32[]{:S(2)}) collective-permute-start(f32[8,32,1024]{2,1,0:T(8,128)} %get-tuple-element.179), channel_id=1, source_target_pairs={{0,4},{4,8},{8,12},{12,16},{16,20},{20,24},{24,28},{1,5},{5,9},{9,... | collective-permute-start | bytes 3145736 | tf_op jit(solution)/shard_map/ppermute | solution.py:20
  152.4 25.1 %collective-permute-start.9 = (f32[8,32,1024]{2,1,0:T(8,128)}, f32[8,32,1024]{2,1,0:T(8,128)}, u32[]{:S(2)}, u32[]{:S(2)}) collective-permute-start(f32[8,32,1024]{2,1,0:T(8,128)} %get-tuple-element.178), channel_id=1, source_target_pairs={{4,0},{8,4},{12,8},{16,12},{20,16},{24,20},{28,24},{5,1},{9,5},{13... | collective-permute-start | bytes 3145736 | tf_op jit(solution)/shard_map/ppermute | solution.py:23
  164.5 7.8 %copy-start.2 = (f32[16,32,1024]{2,1,0:T(8,128)S(1)}, f32[16,32,1024]{2,1,0:T(8,128)}, u32[]{:S(2)}) copy-start(f32[16,32,1024]{2,1,0:T(8,128)} %slice.633) | copy-start | bytes 6291460
  168.2 17.1 %copy-start.17 = (f32[2,2,8,8,512]{4,3,2,1,0:T(8,128)S(1)}, f32[2,2,8,8,512]{4,3,2,1,0:T(8,128)}, u32[]{:S(2)}) copy-start(f32[2,2,8,8,512]{4,3,2,1,0:T(8,128)} %reshape.878) | copy-start | bytes 1572868
  180.3 13.2 %copy-start.6 = (bf16[1,16,16,512]{3,2,1,0:T(8,128)(2,1)S(1)}, bf16[1,16,16,512]{3,2,1,0:T(8,128)(2,1)}, u32[]{:S(2)}) copy-start(bf16[1,16,16,512]{3,2,1,0:T(8,128)(2,1)} %param.32) | copy-start | bytes 786436
  181.4 13.2 %copy-start.4 = (f32[16,32,1024]{2,1,0:T(8,128)S(1)}, f32[16,32,1024]{2,1,0:T(8,128)}, u32[]{:S(2)}) copy-start(f32[16,32,1024]{2,1,0:T(8,128)} %copy-done.3) | copy-start | bytes 6291460
  181.4 22.4 %collective-permute-start.10 = (f32[16,8,1024]{2,1,0:T(8,128)}, f32[16,8,1024]{2,1,0:T(8,128)}, u32[]{:S(2)}, u32[]{:S(2)}) collective-permute-start(f32[16,8,1024]{2,1,0:T(8,128)} %get-tuple-element.181), channel_id=1, source_target_pairs={{0,32},{32,64},{64,96},{96,128},{128,160},{160,192},{192,224},{224... | collective-permute-start | bytes 1572872 | tf_op jit(solution)/shard_map/ppermute | solution.py:20
  186.2 19.9 %collective-permute-start.11 = (f32[16,8,1024]{2,1,0:T(8,128)}, f32[16,8,1024]{2,1,0:T(8,128)}, u32[]{:S(2)}, u32[]{:S(2)}) collective-permute-start(f32[16,8,1024]{2,1,0:T(8,128)} %get-tuple-element.180), channel_id=1, source_target_pairs={{32,0},{64,32},{96,64},{128,96},{160,128},{192,160},{224,192},{0,2... | collective-permute-start | bytes 1572872 | tf_op jit(solution)/shard_map/ppermute | solution.py:23
  193.5 13.9 %copy-start.14 = (bf16[512,1536]{1,0:T(8,128)(2,1)S(1)}, bf16[512,1536]{1,0:T(8,128)(2,1)}, u32[]{:S(2)}) copy-start(bf16[512,1536]{1,0:T(8,128)(2,1)} %param.34) | copy-start | bytes 4718596
  193.5 13.9 %copy-start.20 = (f32[512]{0:T(512)S(1)}, f32[512]{0:T(512)}, u32[]{:S(2)}) copy-start(f32[512]{0:T(512)} %param.36) | copy-start | bytes 6148
  194.6 13.5 %copy-start.19 = (bf16[512,256]{1,0:T(8,128)(2,1)S(1)}, bf16[512,256]{1,0:T(8,128)(2,1)}, u32[]{:S(2)}) copy-start(bf16[512,256]{1,0:T(8,128)(2,1)} %copy.117) | copy-start | bytes 786436
  (4 other events, 7.3 us)

commit v2 on v1

v2 whole, which is shorter than its diff:
```python
import jax
import jax.numpy as jnp
from jax import lax
from jax.experimental import pallas as pl
from jax.experimental.pallas import tpu as pltpu
from jax.sharding import PartitionSpec as P

MESH = pl.DeviceIdType.MESH


def halo_kernel(tokens_ref, mask_ref, ext_ref, near_ref, own_sem, s_lon, v_lon, s_lat, v_lat, s_rel, v_rel, s_m, v_m):
    lon = lax.axis_index("lon")
    lat = lax.axis_index("lat")
    lev = lax.axis_index("lev")
    west = ((lon + 7) % 8, lat, lev)
    east = ((lon + 1) % 8, lat, lev)
    north = (lon, (lat + 7) % 8, lev)
    south = (lon, (lat + 1) % 8, lev)
    barrier = pltpu.get_barrier_semaphore()
    for peer in (west, east, north, south):
        pl.semaphore_signal(barrier, inc=1, device_id=peer, device_id_type=MESH)

    def window(row, col):
        return tokens_ref.at[0, row * 8 : row * 8 + 8, col * 8 : col * 8 + 8, :]

    own = []
    for row in range(2):
        for col in range(2):
            own.append(
                pltpu.make_async_copy(
                    window(row, col), ext_ref.at[1 + row, 1 + col], own_sem.at[row * 2 + col]
                )
            )
            own[-1].start()
    mask_copy = pltpu.make_async_copy(mask_ref, near_ref.at[1, 1], own_sem.at[4])
    mask_copy.start()
    pl.semaphore_wait(barrier, 4)

    def remote(src, dst, send, recv, peer):
        copy = pltpu.make_async_remote_copy(
            src_ref=src, dst_ref=dst, send_sem=send, recv_sem=recv, device_id=peer,
            device_id_type=MESH,
        )
        copy.start()
        return copy

    mask_lon = [
        remote(mask_ref, near_ref.at[1, 2], s_m.at[0], v_m.at[0], west),
        remote(mask_ref, near_ref.at[1, 0], s_m.at[1], v_m.at[1], east),
    ]
    to_lon = []
    for row in range(2):
        to_lon.append(
            remote(window(row, 0), ext_ref.at[1 + row, 3], s_lon.at[row, 0], v_lon.at[row, 0], west)
        )
        to_lon.append(
            remote(window(row, 1), ext_ref.at[1 + row, 0], s_lon.at[row, 1], v_lon.at[row, 1], east)
        )
    to_lat = []
    for col in range(2):
        to_lat.append(
            remote(window(0, col), ext_ref.at[3, 1 + col], s_lat.at[0, col], v_lat.at[0, col], north)
        )
        to_lat.append(
            remote(window(1, col), ext_ref.at[0, 1 + col], s_lat.at[1, col], v_lat.at[1, col], south)
        )
    mask_copy.wait()
    for copy in mask_lon:
        copy.wait()
    mask_lat = [
        remote(near_ref.at[1], near_ref.at[2], s_m.at[2], v_m.at[2], north),
        remote(near_ref.at[1], near_ref.at[0], s_m.at[3], v_m.at[3], south),
    ]
    relayed = []
    for row, line, peer in ((0, 3, north), (1, 0, south)):
        for side, col in ((0, 3), (1, 0)):
            to_lon[row * 2 + side].wait()
            relayed.append(
                remote(
                    ext_ref.at[1 + row, col], ext_ref.at[line, col],
                    s_rel.at[row, side], v_rel.at[row, side], peer,
                )
            )
    for copy in own + to_lat + mask_lat + relayed:
        copy.wait()


def halo(tokens_in, mask_rows):
    dma = pltpu.SemaphoreType.DMA
    return pl.pallas_call(
        halo_kernel,
        out_shape=(
            jax.ShapeDtypeStruct((4, 4, 8, 8, 512), jnp.bfloat16),
            jax.ShapeDtypeStruct((3, 3, 8, 128), jnp.float32),
        ),
        in_specs=[pl.BlockSpec(memory_space=pl.ANY), pl.BlockSpec(memory_space=pltpu.VMEM)],
        out_specs=(
            pl.BlockSpec(memory_space=pltpu.VMEM),
            pl.BlockSpec(memory_space=pltpu.VMEM),
        ),
        scratch_shapes=[
            dma((5,)), dma((2, 2)), dma((2, 2)), dma((2, 2)), dma((2, 2)),
            dma((2, 2)), dma((2, 2)), dma((4,)), dma((4,)),
        ],
        compiler_params=pltpu.CompilerParams(
            collective_id=0, has_side_effects=True, vmem_limit_bytes=16 << 20
        ),
    )(tokens_in, mask_rows)


def dot_nn(left, right):
    return lax.dot_general(
        left, right, (((1,), (0,)), ((), ())), preferred_element_type=jnp.float32
    )


def dot_nt(left, right):
    return lax.dot_general(
        left, right, (((1,), (1,)), ((), ())), preferred_element_type=jnp.float32
    )


def dot_tn(left, right):
    return lax.dot_general(
        left, right, (((0,), (0,)), ((), ())), preferred_element_type=jnp.float32
    )


def norm_rows(values_in):
    center = values_in - jnp.mean(values_in, axis=-1, keepdims=True)
    spread = jnp.mean(center * center, axis=-1, keepdims=True)
    scaling = lax.rsqrt(spread + 1e-05)
    return (center * scaling, scaling)


def attend_kernel(
    ext_ref, near_ref, cot_ref, wqkv_ref, wout_ref, gain_ref,
    layer_ref, back_ref, own_ref, gq_ref, wg_ref,
    hid, kv, gkv, qs, gb, dout, mixed, pscr, dscr, rows_scr, bias,
):
    low = jnp.bfloat16
    full = jnp.float32
    lat = lax.axis_index("lat")
    has_north = jnp.where(lat > 0, 1.0, 0.0).astype(full)
    has_south = jnp.where(lat < 7, 1.0, 0.0).astype(full)
    gain = gain_ref[...]
    place = ((0, 1), (1, 0), (1, 1), (2, 0))
    for row in range(4):
        tile_row, in_row = place[row]
        for col in range(4):
            tile_col, in_col = place[col]
            line = near_ref[tile_row, tile_col, in_row * 2 + in_col : in_row * 2 + in_col + 1, :]
            if row == 0:
                line = line * has_north
            if row == 3:
                line = line * has_south
            rows_scr[row * 4 + col : row * 4 + col + 1, :] = line
    columns = jnp.transpose(jnp.concatenate([rows_scr[...]] * 8, axis=0))
    oceans = []
    for index in range(16):
        column = columns[:64, index : index + 1]
        wide = jnp.broadcast_to(column, (64, 128))
        bias[index * 64 : index * 64 + 64, :] = (wide - 1.0) * 1000000000.0
        if index in (5, 6, 9, 10):
            oceans.append(wide)
    for row in range(4):
        span = slice(row * 256, row * 256 + 256)
        normed, _ = norm_rows(ext_ref[row].astype(full).reshape(256, 512))
        hid[span, :] = (normed * gain).astype(low)
        kv[span, :] = dot_nn(hid[span, :], wqkv_ref[:, 512:]).astype(low)
        gkv[span, :] = jnp.zeros((256, 1024), full)
    for row in range(2):
        own_rows = slice(row * 256 + 320, row * 256 + 448)
        qs[row * 128 : row * 128 + 128, :] = (
            dot_nn(hid[own_rows, :], wqkv_ref[:, :512]) * 0.125
        ).astype(low)
        band = cot_ref[0, row * 8 : row * 8 + 8].astype(full)
        for col in range(2):
            at = (row * 2 + col) * 64
            piece = band[:, col * 8 : col * 8 + 8, :].reshape(64, 512)
            flags = jnp.concatenate([oceans[row * 2 + col]] * 4, axis=1)
            gb[at : at + 64, :] = (piece * flags).astype(low)
    dout[...] = dot_nt(gb[...], wout_ref[...]).astype(low)
    block_row = lax.broadcasted_iota(jnp.int32, (256, 256), 0) // 64
    block_col = lax.broadcasted_iota(jnp.int32, (256, 256), 1) // 64
    diag = jnp.where(block_row == block_col, 1.0, 0.0).astype(full)
    diag_low = diag.astype(low)

    def fold(square):
        kept = square * diag
        return (kept[:64] + kept[64:128]) + (kept[128:192] + kept[192:])

    for index in range(4):
        row, col = index // 2, index % 2
        at = slice(index * 64, index * 64 + 64)
        alive = jnp.max(oceans[index])
        spare = 192 if col == 0 else 0
        for part in range(3):
            pscr[part * 256 + spare : part * 256 + spare + 64, :] = jnp.zeros((64, 256), low)
            dscr[part * 256 + spare : part * 256 + spare + 64, :] = jnp.zeros((64, 256), low)
        spans = [
            slice((row + part) * 256 + col * 64, (row + part) * 256 + col * 64 + 192)
            for part in range(3)
        ]
        kept_spans = [
            slice(part * 256 + col * 64, part * 256 + col * 64 + 192) for part in range(3)
        ]
        slab = slice(row * 256, row * 256 + 768)
        for group in range(2):
            lanes = slice(group * 256, group * 256 + 256)
            value_lanes = slice(512 + group * 256, 512 + group * 256 + 256)
            qbd = jnp.concatenate([qs[at, lanes]] * 4, axis=0) * diag_low
            dbd = jnp.concatenate([dout[at, lanes]] * 4, axis=0) * diag_low
            scores = [
                dot_nt(kv[span, lanes], qbd) + jnp.concatenate([bias[span, :]] * 2, axis=1)
                for span in spans
            ]
            top = jnp.maximum(
                jnp.maximum(
                    jnp.max(scores[0], axis=0, keepdims=True),
                    jnp.max(scores[1], axis=0, keepdims=True),
                ),
                jnp.max(scores[2], axis=0, keepdims=True),
            )
            weights = [jnp.exp(part - top) for part in scores]
            total = (
                jnp.sum(weights[0], axis=0, keepdims=True)
                + jnp.sum(weights[1], axis=0, keepdims=True)
                + jnp.sum(weights[2], axis=0, keepdims=True)
            )
            inverse = 1.0 / total
            probs = [part * inverse for part in weights]
            for part in range(3):
                pscr[kept_spans[part], :] = probs[part].astype(low)
            out = fold(dot_tn(pscr[...], kv[slab, value_lanes]))
            mixed[at, lanes] = (out * alive).astype(low)
            gprobs = [dot_nt(kv[span, value_lanes], dbd) for span in spans]
            delta = (
                jnp.sum(probs[0] * gprobs[0], axis=0, keepdims=True)
                + jnp.sum(probs[1] * gprobs[1], axis=0, keepdims=True)
                + jnp.sum(probs[2] * gprobs[2], axis=0, keepdims=True)
            )
            for part in range(3):
                dscr[kept_spans[part], :] = (probs[part] * (gprobs[part] - delta)).astype(low)
            gq_ref[at, lanes] = (fold(dot_tn(dscr[...], kv[slab, lanes])) * 0.125).astype(low)
            for part in range(3):
                gkv[spans[part], lanes] += dot_nn(dscr[kept_spans[part], :], qbd)
                gkv[spans[part], value_lanes] += dot_nn(pscr[kept_spans[part], :], dbd)
    branch = dot_nn(mixed[...], wout_ref[...])
    for row in range(2):
        pieces = []
        for col in range(2):
            index = row * 2 + col
            flags = jnp.concatenate([oceans[index]] * 4, axis=1)
            here = ext_ref[1 + row, 1 + col].astype(full).reshape(64, 512)
            result = here + flags * branch[index * 64 : index * 64 + 64]
            pieces.append(result.reshape(8, 8, 512))
        layer_ref[0, row * 8 : row * 8 + 8] = jnp.concatenate(pieces, axis=1).astype(low)
    for row in range(4):
        for col in range(4):
            base = (row * 4 + col) * 64
            block = gkv[base : base + 64, :]
            back_ref[row, col] = block.astype(low)
            if row in (1, 2) and col in (1, 2):
                own_ref[(row - 1) * 2 + col - 1] = block
    wg_ref[:, :512] = (
        dot_tn(hid[320:448, :], gq_ref[:128, :]) + dot_tn(hid[576:704, :], gq_ref[128:, :])
    ).astype(low)
    wg_ref[:, 512:1536] = dot_tn(hid[...], back_ref[...].reshape(1024, 1024)).astype(low)
    wg_ref[:, 1536:] = dot_tn(mixed[...], gb[...]).astype(low)


def attend(ext, near, cotangent, qkv_weight, out_weight, gain):
    low, full = jnp.bfloat16, jnp.float32
    vmem = pl.BlockSpec(memory_space=pltpu.VMEM)
    return pl.pallas_call(
        attend_kernel,
        out_shape=(
            jax.ShapeDtypeStruct((1, 16, 16, 512), low),
            jax.ShapeDtypeStruct((4, 4, 64, 1024), low),
            jax.ShapeDtypeStruct((4, 64, 1024), full),
            jax.ShapeDtypeStruct((256, 512), low),
            jax.ShapeDtypeStruct((512, 2048), low),
        ),
        in_specs=[vmem] * 6,
        out_specs=(vmem,) * 5,
        scratch_shapes=[
            pltpu.VMEM((1024, 512), low),
            pltpu.VMEM((1024, 1024), low),
            pltpu.VMEM((1024, 1024), full),
            pltpu.VMEM((256, 512), low),
            pltpu.VMEM((256, 512), low),
            pltpu.VMEM((256, 512), low),
            pltpu.VMEM((256, 512), low),
            pltpu.VMEM((768, 256), low),
            pltpu.VMEM((768, 256), low),
            pltpu.VMEM((16, 128), full),
            pltpu.VMEM((1024, 128), full),
        ],
        compiler_params=pltpu.CompilerParams(vmem_limit_bytes=48 << 20),
    )(ext, near, cotangent, qkv_weight, out_weight, gain)


def input_kernel(tokens_ref, cot_ref, gq_ref, gkv_ref, wqkv_ref, gain_ref, out_ref):
    full = jnp.float32
    gain = gain_ref[...]
    grad_hidden = dot_nt(gq_ref[...], wqkv_ref[:, :512]) + dot_nt(
        gkv_ref[...].reshape(256, 1024), wqkv_ref[:, 512:]
    )
    for row in range(2):
        tokens = tokens_ref[0, row * 8 : row * 8 + 8].astype(full)
        cot = cot_ref[0, row * 8 : row * 8 + 8].astype(full)
        pieces = []
        for col in range(2):
            cols = slice(col * 8, col * 8 + 8)
            at = (row * 2 + col) * 64
            normed, scaling = norm_rows(tokens[:, cols, :].reshape(64, 512))
            scaled = grad_hidden[at : at + 64] * gain
            correction = (
                scaled
                - jnp.mean(scaled, axis=-1, keepdims=True)
                - normed * jnp.mean(scaled * normed, axis=-1, keepdims=True)
            )
            result = cot[:, cols, :].reshape(64, 512) + scaling * correction
            pieces.append(result.reshape(8, 8, 512))
        out_ref[0, row * 8 : row * 8 + 8] = jnp.concatenate(pieces, axis=1).astype(jnp.bfloat16)


def input_gradient(tokens_in, cotangent, gq, gkv, qkv_weight, gain):
    vmem = pl.BlockSpec(memory_space=pltpu.VMEM)
    return pl.pallas_call(
        input_kernel,
        out_shape=jax.ShapeDtypeStruct((1, 16, 16, 512), jnp.bfloat16),
        in_specs=[vmem] * 6,
        out_specs=vmem,
        compiler_params=pltpu.CompilerParams(vmem_limit_bytes=24 << 20),
    )(tokens_in, cotangent, gq, gkv, qkv_weight, gain)


def share_kernel(
    wg_ref, back_ref, own_ref, sum_ref, gkv_ref,
    r1, a1, r2, a2, r3, a3, g4, g5, from_north, from_south, from_west, from_east,
    to_west, to_east,
    s1, v1, s2, v2, s3, v3, s4, v4, s5, v5, s_lat, v_lat, s_lon, v_lon,
):
    low = jnp.bfloat16
    full = jnp.float32
    lon = lax.axis_index("lon")
    lat = lax.axis_index("lat")
    lev = lax.axis_index("lev")
    hi = lev // 2
    core = lev % 2
    here = hi * 8 + lon
    barrier = pltpu.get_barrier_semaphore()

    def plane_peer(step):
        there = (here + step) % 16
        return there // 8, there % 8

    def greet_plane(step, carry):
        peer_hi, peer_lon = plane_peer(step)
        pl.semaphore_signal(
            barrier, inc=1, device_id=(peer_lon, lat, peer_hi * 2 + core), device_id_type=MESH
        )
        return carry

    def greet_lat(step, carry):
        pl.semaphore_signal(
            barrier, inc=1, device_id=(lon, (lat + step) % 8, lev), device_id_type=MESH
        )
        return carry

    pl.semaphore_signal(
        barrier, inc=1, device_id=(lon, lat, hi * 2 + 1 - core), device_id_type=MESH
    )
    lax.fori_loop(1, 16, greet_plane, 0)
    lax.fori_loop(1, 8, greet_lat, 0)
    pl.semaphore_wait(barrier, 23)

    def remote(src, dst, send, recv, peer):
        return pltpu.make_async_remote_copy(
            src_ref=src, dst_ref=dst, send_sem=send, recv_sem=recv, device_id=peer,
            device_id_type=MESH,
        )

    def begin(copy):
        def one(step, carry):
            copy(step).start()
            return carry

        return one

    def finish(copy):
        def one(step, carry):
            copy(step).wait()
            return carry

        return one

    def pair_copy(part):
        return remote(
            wg_ref.at[part * 2 + 1 - core], r1.at[part], s1.at[part], v1.at[part],
            (lon, lat, hi * 2 + 1 - core),
        )

    def plane_copy(step):
        peer_hi, peer_lon = plane_peer(step)
        return remote(
            a1.at[peer_hi * 8 + peer_lon], r2.at[step - 1], s2.at[step - 1], v2.at[step - 1],
            (peer_lon, lat, peer_hi * 2 + core),
        )

    def lat_copy(step):
        peer = (lat + step) % 8
        return remote(
            a2.at[peer], r3.at[step - 1], s3.at[step - 1], v3.at[step - 1], (lon, peer, lev)
        )

    def lat_gather(step):
        return remote(
            a3, g4.at[lat], s4.at[step - 1], v4.at[step - 1], (lon, (lat + step) % 8, lev)
        )

    def lon_gather(step):
        return remote(
            g4, g5.at[lon], s5.at[step - 1], v5.at[step - 1], ((lon + step) % 8, lat, lev)
        )

    north = (lon, (lat + 7) % 8, lev)
    south = (lon, (lat + 1) % 8, lev)
    west = ((lon + 7) % 8, lat, lev)
    east = ((lon + 1) % 8, lat, lev)
    corners = []
    edges = []
    for line, target, peer, side in ((0, from_south, north, 0), (3, from_north, south, 1)):
        for col in (0, 3):
            corners.append(
                remote(
                    back_ref.at[line, col], target.at[col],
                    s_lat.at[side, col], v_lat.at[side, col], peer,
                )
            )
        edges.append(
            remote(
                back_ref.at[line, pl.ds(1, 2)], target.at[pl.ds(1, 2)],
                s_lat.at[side, 1], v_lat.at[side, 1], peer,
            )
        )
    pairs = [pair_copy(part) for part in range(2)]
    for copy in pairs:
        copy.start()
    for copy in corners:
        copy.start()
    for part in range(2):
        pairs[part].wait()

        def add_pair(piece, carry):
            rows = pl.ds(pl.multiple_of(piece * 16, 16), 16)
            total = wg_ref[part * 2 + core, rows, :].astype(full) + r1[part, rows, :].astype(full)
            a1[part * 8 + piece] = total.astype(low)
            return carry

        lax.fori_loop(0, 8, add_pair, 0)
    lax.fori_loop(1, 16, begin(plane_copy), 0)
    for copy in edges:
        copy.start()
    for copy in corners:
        copy.wait()
    sources = (from_north, from_south)

    def add_corner(piece, carry):
        rows = pl.ds(pl.multiple_of(piece * 16, 16), 16)
        for row in range(2):
            to_west[row, rows, :] = (
                back_ref[1 + row, 0, rows, :].astype(full)
                + sources[row][0, rows, :].astype(full)
            ).astype(low)
            to_east[row, rows, :] = (
                back_ref[1 + row, 3, rows, :].astype(full)
                + sources[row][3, rows, :].astype(full)
            ).astype(low)
        return carry

    lax.fori_loop(0, 4, add_corner, 0)
    sides = [
        remote(to_west, from_east, s_lon.at[0], v_lon.at[0], west),
        remote(to_east, from_west, s_lon.at[1], v_lon.at[1], east),
    ]
    for copy in sides:
        copy.start()
    lax.fori_loop(1, 16, finish(plane_copy), 0)
    for part in range(8):
        cols = slice(part * 256, (part + 1) * 256)
        total = a1[here, :, cols].astype(full)
        for step in range(15):
            total = total + r2[step, :, cols].astype(full)
        a2[part] = total
    lax.fori_loop(1, 8, begin(lat_copy), 0)
    lax.fori_loop(1, 8, finish(lat_copy), 0)
    total = a2[lat]
    for step in range(7):
        total = total + r3[step]
    a3[...] = total.astype(low)
    g4[lat] = a3[...]
    lax.fori_loop(1, 8, begin(lat_gather), 0)
    lax.fori_loop(1, 8, finish(lat_gather), 0)
    g5[lon] = g4[...]
    lax.fori_loop(1, 8, begin(lon_gather), 0)
    for copy in edges + sides:
        copy.wait()

    def add_own(piece, carry):
        rows = pl.ds(pl.multiple_of(piece * 16, 16), 16)
        for row in range(2):
            for col in range(2):
                index = row * 2 + col
                side = (from_west, from_east)[col]
                gkv_ref[index, rows, :] = (
                    own_ref[index, rows, :]
                    + sources[row][1 + col, rows, :].astype(full)
                    + side[row, rows, :].astype(full)
                ).astype(low)
        return carry

    lax.fori_loop(0, 4, add_own, 0)
    lax.fori_loop(1, 8, finish(lon_gather), 0)
    for row in range(8):
        for col in range(8):
            sum_ref[row * 16 : (row + 1) * 16, col * 256 : (col + 1) * 256] = g5[row, col].astype(
                full
            )


def share(wg, back, own):
    dma = pltpu.SemaphoreType.DMA
    low, full = jnp.bfloat16, jnp.float32
    vmem = pl.BlockSpec(memory_space=pltpu.VMEM)
    return pl.pallas_call(
        share_kernel,
        out_shape=(
            jax.ShapeDtypeStruct((128, 2048), full),
            jax.ShapeDtypeStruct((4, 64, 1024), low),
        ),
        in_specs=[vmem] * 3,
        out_specs=(vmem, vmem),
        scratch_shapes=[
            pltpu.VMEM((2, 128, 2048), low),
            pltpu.VMEM((16, 16, 2048), low),
            pltpu.VMEM((15, 16, 2048), low),
            pltpu.VMEM((8, 16, 256), full),
            pltpu.VMEM((7, 16, 256), full),
            pltpu.VMEM((16, 256), low),
            pltpu.VMEM((8, 16, 256), low),
            pltpu.VMEM((8, 8, 16, 256), low),
            pltpu.VMEM((4, 64, 1024), low),
            pltpu.VMEM((4, 64, 1024), low),
            pltpu.VMEM((2, 64, 1024), low),
            pltpu.VMEM((2, 64, 1024), low),
            pltpu.VMEM((2, 64, 1024), low),
            pltpu.VMEM((2, 64, 1024), low),
            dma((2,)), dma((2,)), dma((15,)), dma((15,)), dma((7,)), dma((7,)),
            dma((7,)), dma((7,)), dma((7,)), dma((7,)),
            dma((2, 4)), dma((2, 4)), dma((2,)), dma((2,)),
        ],
        compiler_params=pltpu.CompilerParams(
            collective_id=1, has_side_effects=True, vmem_limit_bytes=40 << 20
        ),
    )(wg, back, own)


def on_device(tokens_in, cotangent, qkv_weight, out_weight, norm_gain, ocean_mask):
    features = tokens_in.shape[3]
    ocean = ocean_mask[0].astype(jnp.float32).reshape(2, 8, 2, 8)
    mask_rows = jnp.pad(jnp.transpose(ocean, (0, 2, 1, 3)).reshape(4, 64), ((0, 4), (0, 64)))
    ext, near = halo(tokens_in, mask_rows)
    gain = norm_gain.reshape(1, features)
    layer_out, back, own, gq, wg = attend(ext, near, cotangent, qkv_weight, out_weight, gain)
    shared, gkv = share(wg.reshape(4, features // 4, 4 * features), back, own)
    input_grad = input_gradient(tokens_in, cotangent, gq, gkv, qkv_weight, gain)
    qkv_grad = shared[:, : 3 * features]
    out_grad = shared[:, 3 * features :]
    first = lax.axis_index("lev") * (features // 4)
    weight_rows = lax.dynamic_slice_in_dim(qkv_weight, first, features // 4, 0)
    gain_rows = lax.dynamic_slice_in_dim(norm_gain, first, features // 4, 0)
    gain_grad = jnp.sum(weight_rows.astype(jnp.float32) * qkv_grad, axis=1) / gain_rows
    return (layer_out, input_grad, qkv_grad, out_grad, gain_grad)


def solution(mesh):
    placed = (
        P("lev", "lat", "lon", None),
        P("lev", "lat", "lon", None),
        P(),
        P(),
        P(),
        P("lev", "lat", "lon"),
    )
    return jax.shard_map(
        on_device,
        mesh=mesh,
        in_specs=placed,
        out_specs=(
            P("lev", "lat", "lon", None),
            P("lev", "lat", "lon", None),
            P("lev", None),
            P("lev", None),
            P("lev"),
        ),
        check_vma=False,
    )
```

time: 260 us -> 93.8 us (0.36)
  local copies, waits for them, and re-layouts: 78.8 us -> 9.11 us
  other arithmetic: 47.3 us -> 3.91 us
  waiting for transfers between devices: 38.1 us -> 0 us
  Pallas kernels: 46.4 us -> 79.6 us
  matrix products: 25.6 us -> 0 us
  starting transfers between devices: 21.1 us -> 0 us
    ppermute x12 -> x0, waiting for transfers between devices: 38.1 us -> none  [the longest x6 33.4 us: with_halo(): lax.ppermute(lax.slice_in_dim(block, block.shape[dim] - width, None, axis...]
    pallas_call x1 -> x4, Pallas kernels: 46.4 us -> 79.6 us  [the longest x1 48.2 us: share(): pl.pallas_call(share_kernel, out_shape=(jax.ShapeDtypeStruct((128, 2048),...]
    ppermute x12 -> x0, starting transfers between devices: 21.1 us -> none  [the longest x6 12.7 us: with_halo(): lax.ppermute(lax.slice_in_dim(block, block.shape[dim] - width, None, axis...]
    scatter-add x10 -> x0, other arithmetic: 20.6 us -> none  [the longest x6 15.1 us: spread_back(): totals = totals.at[lat_step * window_side:(lat_step + lat_windows) * wind...]
    dot_general x11 -> x0, matrix products: 20.4 us -> none  [the longest x1 3.66 us: attend_backward(): jnp.einsum('whqk,wkhd->wqhd', grad_scores, split_heads(key_rows, head_cou...]
    slice x15 -> x0, local copies, waits for them, and re-layouts: 20.2 us -> none  [the longest x2 5.69 us: on_device(): key_rows = near[..., :features]]
    scatter-add x3 -> x0, local copies, waits for them, and re-layouts: 16.4 us -> none  [spread_back(): totals = totals.at[lat_step * window_side:(lat_step + lat_windows) * wind...]
    reshape x21 -> x1, local copies, waits for them, and re-layouts: 15.3 us -> 0.08 us  [on_device(): jnp.transpose(ocean, (0, 2, 1, 3)).reshape(4, 64)]
  transfers between devices with their start and end apart: 12 -> 0, of which waited for: 5 -> 0; matrix products, arithmetic and copies ran while one was open for 17% -> 0% of each run, Pallas kernels for 0% -> 0%
where the time goes in v2:
time: 93.8 us; the launch traced here: 93.3 us
  Pallas kernels  79.6 us (85%)
  local copies, waits for them, and re-layouts  9.11 us (10%)
  other arithmetic  3.91 us (4%)
    pallas_call x1, Pallas kernels, share(): pl.pallas_call(share_kernel, out_shape=(jax.ShapeDtypeStruct((128, 2048),...  48.2 us
    pallas_call x1, Pallas kernels, halo(): pl.pallas_call(halo_kernel, out_shape=(jax.ShapeDtypeStruct((4, 4, 8, 8,...  17.7 us
    pallas_call x1, Pallas kernels, attend(): pl.pallas_call(attend_kernel, out_shape=(jax.ShapeDtypeStruct((1, 16, 16,...  12.3 us
    unnamed x16, local copies, waits for them, and re-layouts  8.21 us
    reduce_sum x1, other arithmetic, on_device(): jnp.sum(weight_rows.astype(jnp.float32) * qkv_grad, axis=1) / gain_rows  1.94 us

profile of v2, /device:TPU:8, one launch (start us, length us, event | category | flops | bytes accessed | tf_op | source)
XLA Modules:
  0.0 93.3 jit_solution(13920837723769045261)
XLA Ops:
  0.6 0.7 convert_element_type.12
  1.3 0.1 convert_element_type.13
  1.4 0.1 reshape.22
  1.5 0.0 copy-start.4
  1.5 0.9 %copy-done.4 = bf16[1,16,16,512]{3,2,1,0:T(8,128)(2,1)S(1)} copy-done((bf16[1,16,16,512]{3,2,1,0:T(8,128)(2,1)S(1)}, bf16[1,16,16,512]{3,2,1,0:T(8,128)(2,1)}, u32[]{:S(2)}) %copy-start.4) | copy-done | bytes 262168
  2.5 17.7 %shard_map.101 = (bf16[4,4,8,8,512]{4,3,2,1,0:T(8,128)(2,1)S(1)}, f32[3,3,8,128]{3,2,1,0:T(8,128)S(1)}) custom-call(bf16[1,16,16,512]{3,2,1,0:T(8,128)(2,1)S(1)} %copy-done.4, f32[8,128]{1,0:T(8,128)S(1)} %pad.4.mask_ref), custom_call_target="tpu_custom_call" | custom-call | tf_op jit(solution)/shard_map/pallas_call | solution.py:90
  20.1 0.0 copy-start
  20.2 1.4 %copy-done = bf16[512,1536]{1,0:T(8,128)(2,1)S(1)} copy-done((bf16[512,1536]{1,0:T(8,128)(2,1)S(1)}, bf16[512,1536]{1,0:T(8,128)(2,1)}, u32[]{:S(2)}) %copy-start) | copy-done | bytes 1572888
  21.6 0.0 copy-start.3
  21.6 0.9 %copy-done.3 = bf16[1,16,16,512]{3,2,1,0:T(8,128)(2,1)S(1)} copy-done((bf16[1,16,16,512]{3,2,1,0:T(8,128)(2,1)S(1)}, bf16[1,16,16,512]{3,2,1,0:T(8,128)(2,1)}, u32[]{:S(2)}) %copy-start.3) | copy-done | bytes 262168
  22.5 0.0 copy-start.6
  22.5 1.0 %copy-done.6 = bf16[512,512]{1,0:T(8,128)(2,1)S(1)} copy-done((bf16[512,512]{1,0:T(8,128)(2,1)S(1)}, bf16[512,512]{1,0:T(8,128)(2,1)}, u32[]{:S(2)}) %copy-start.6) | copy-done | bytes 524312
  23.5 0.0 copy-start.7
  23.5 0.7 copy-done.7
  24.2 12.3 %shard_map.102 = (bf16[1,16,16,512]{3,2,1,0:T(8,128)(2,1)}, bf16[4,4,64,1024]{3,2,1,0:T(8,128)(2,1)}, f32[4,64,1024]{2,1,0:T(8,128)S(1)}, bf16[256,512]{1,0:T(8,128)(2,1)S(1)}, bf16[512,2048]{1,0:T(8,128)(2,1)}) custom-call(bf16[4,4,8,8,512]{4,3,2,1,0:T(8,128)(2,1)S(1)} %get-tuple-element.14.ext_ref, f32[3,3,8,128]{3,2,1,0:T(8,128)S(1)} %get-tuple-element.15.near_ref, ...), custom_call_target="tpu_custom_call" | custom-call | tf_op jit(solution)/shard_map/pallas_call | solution.py:276
  36.5 0.0 copy-start.1
  36.5 1.6 %copy-done.1 = bf16[4,4,64,1024]{3,2,1,0:T(8,128)(2,1)S(1)} copy-done((bf16[4,4,64,1024]{3,2,1,0:T(8,128)(2,1)S(1)}, bf16[4,4,64,1024]{3,2,1,0:T(8,128)(2,1)}, u32[]{:S(2)}) %copy-start.1) | copy-done | bytes 2097176
  38.1 0.0 copy-start.2
  38.1 1.6 %copy-done.2 = bf16[512,2048]{1,0:T(8,128)(2,1)S(1)} copy-done((bf16[512,2048]{1,0:T(8,128)(2,1)S(1)}, bf16[512,2048]{1,0:T(8,128)(2,1)}, u32[]{:S(2)}) %copy-start.2) | copy-done | bytes 2097176
  39.7 0.0 copy-start.5
  39.7 48.2 %shard_map.103 = (f32[128,2048]{1,0:T(8,128)S(1)}, bf16[4,64,1024]{2,1,0:T(8,128)(2,1)S(1)}) custom-call(bf16[4,128,2048]{2,1,0:T(8,128)(2,1)S(1)} %bitcast.7, bf16[4,4,64,1024]{3,2,1,0:T(8,128)(2,1)S(1)} %copy-done.1, f32[4,64,1024]{2,1,0:T(8,128)S(1)} %get-tuple-element.20.own_ref), custom_call_target="tpu_custom_call" | custom-call | tf_op jit(solution)/shard_map/pallas_call | solution.py:538
  87.9 0.0 copy-done.5
  87.9 1.5 %shard_map.104 = bf16[1,16,16,512]{3,2,1,0:T(8,128)(2,1)} custom-call(bf16[1,16,16,512]{3,2,1,0:T(8,128)(2,1)S(1)} %copy-done.5, bf16[1,16,16,512]{3,2,1,0:T(8,128)(2,1)S(1)} %copy-done.3, bf16[256,512]{1,0:T(8,128)(2,1)S(1)} %get-tuple-element.17.gq_ref, bf16[4,64,1024]{2,1,0:T(8,128)(2,1)S(1)} %get-tuple-element.21.gkv_ref, bf16[512,1536]{1,0:T(8,128)(2,1)S(1)} %copy-done, ...), custom_call_target="tpu_custom_call" | custom-call | tf_op jit(solution)/shard_map/pallas_call | solution.py:331
  89.4 1.9 %multiply_reduce_fusion = (f32[128]{0:T(128)S(1)}, f32[128,1536]{1,0:T(8,128)}) fusion(bf16[512,1536]{1,0:T(8,128)(2,1)} %wqkv_ref.3, s32[]{:T(128)S(6)} %select_n.4, f32[128,2048]{1,0:T(8,128)S(1)} %get-tuple-element.22), kind=kLoop, calls=%fused_computation | loop fusion | flops 589696 | bytes 1966596 | tf_op jit(solution)/shard_map/reduce_sum | solution.py:585
  91.3 0.7 slice.7
  92.1 1.3 %dynamic-slice_divide_fusion = f32[128]{0:T(128)} fusion(f32[128]{0:T(128)S(1)} %get-tuple-element.23, f32[512]{0:T(512)} %param.10, s32[]{:T(128)S(6)} %select_n.4), kind=kLoop, calls=%fused_computation.2 | loop fusion | flops 128 | bytes 1540 | tf_op jit(solution)/shard_map/div | solution.py:585
  (2 shorter events, 0.0 us)
Async XLA Ops:
  1.5 1.0 %copy-start.4 = (bf16[1,16,16,512]{3,2,1,0:T(8,128)(2,1)S(1)}, bf16[1,16,16,512]{3,2,1,0:T(8,128)(2,1)}, u32[]{:S(2)}) copy-start(bf16[1,16,16,512]{3,2,1,0:T(8,128)(2,1)} %tokens_ref.3) | copy-start | bytes 786436
  20.1 1.4 %copy-start = (bf16[512,1536]{1,0:T(8,128)(2,1)S(1)}, bf16[512,1536]{1,0:T(8,128)(2,1)}, u32[]{:S(2)}) copy-start(bf16[512,1536]{1,0:T(8,128)(2,1)} %wqkv_ref.3) | copy-start | bytes 4718596
  21.6 0.9 %copy-start.3 = (bf16[1,16,16,512]{3,2,1,0:T(8,128)(2,1)S(1)}, bf16[1,16,16,512]{3,2,1,0:T(8,128)(2,1)}, u32[]{:S(2)}) copy-start(bf16[1,16,16,512]{3,2,1,0:T(8,128)(2,1)} %cot_ref.3) | copy-start | bytes 786436
  22.5 1.0 %copy-start.6 = (bf16[512,512]{1,0:T(8,128)(2,1)S(1)}, bf16[512,512]{1,0:T(8,128)(2,1)}, u32[]{:S(2)}) copy-start(bf16[512,512]{1,0:T(8,128)(2,1)} %wout_ref.1) | copy-start | bytes 1572868
  23.5 0.7 copy-start.7
  36.5 1.6 %copy-start.1 = (bf16[4,4,64,1024]{3,2,1,0:T(8,128)(2,1)S(1)}, bf16[4,4,64,1024]{3,2,1,0:T(8,128)(2,1)}, u32[]{:S(2)}) copy-start(bf16[4,4,64,1024]{3,2,1,0:T(8,128)(2,1)} %get-tuple-element.19.back_ref) | copy-start | bytes 6291460
  38.1 1.6 %copy-start.2 = (bf16[512,2048]{1,0:T(8,128)(2,1)S(1)}, bf16[512,2048]{1,0:T(8,128)(2,1)}, u32[]{:S(2)}) copy-start(bf16[512,2048]{1,0:T(8,128)(2,1)} %get-tuple-element.18) | copy-start | bytes 6291460
  39.7 48.2 %copy-start.5 = (bf16[1,16,16,512]{3,2,1,0:T(8,128)(2,1)S(1)}, bf16[1,16,16,512]{3,2,1,0:T(8,128)(2,1)}, u32[]{:S(2)}) copy-start(bf16[1,16,16,512]{3,2,1,0:T(8,128)(2,1)} %tokens_ref.3) | copy-start | bytes 786436

commit v3 on v0

v3 whole, which is shorter than its diff:
```python
import jax
import jax.numpy as jnp
from jax import lax
from jax.experimental import pallas as pl
from jax.experimental.pallas import tpu as pltpu
from jax.sharding import PartitionSpec as P

MESH = pl.DeviceIdType.MESH
LOW = jnp.bfloat16
FULL = jnp.float32
WIDTHS = (768, 512, 768)


def dot_nn(left, right):
    return lax.dot_general(
        left, right, (((1,), (0,)), ((), ())), preferred_element_type=jnp.float32
    )


def dot_nt(left, right):
    return lax.dot_general(
        left, right, (((1,), (1,)), ((), ())), preferred_element_type=jnp.float32
    )


def dot_tn(left, right):
    return lax.dot_general(
        left, right, (((0,), (0,)), ((), ())), preferred_element_type=jnp.float32
    )


def norm_rows(values_in):
    center = values_in - jnp.mean(values_in, axis=-1, keepdims=True)
    spread = jnp.mean(center * center, axis=-1, keepdims=True)
    scaling = lax.rsqrt(spread + 1e-05)
    return (center * scaling, scaling)


def layer_kernel(
    tokens_ref, cot_ref, wqkv_ref, wout_ref, gain_ref, mask_ref,
    layer_ref, grad_ref, sum_a, sum_c, sum_b,
    ext, near, cots, wq, wo, hid, kv, gkv, back, qs, gb, dout, mixed, gq, pscr, dscr, bias,
    wg_a, wg_c, wg_b, r1_a, r1_c, r1_b, a1_a, a1_c, a1_b, r2_a, r2_c, r2_b,
    a2_a, a2_c, a2_b, r3_a, r3_c, r3_b,
    from_north, from_south, from_west, from_east, to_west, to_east,
    local_sem, s_lon, v_lon, s_lat, v_lat, s_rel, v_rel, s_m, v_m,
    s_pair, v_pair, s_plane, v_plane, s_z, v_z, s_all, v_all, s_gz, v_gz, s_gx, v_gx,
):
    lon = lax.axis_index("lon")
    lat = lax.axis_index("lat")
    lev = lax.axis_index("lev")
    hi = lev // 2
    core = lev % 2
    here = hi * 8 + lon
    west = ((lon + 7) % 8, lat, lev)
    east = ((lon + 1) % 8, lat, lev)
    north = (lon, (lat + 7) % 8, lev)
    south = (lon, (lat + 1) % 8, lev)
    partner = (lon, lat, hi * 2 + 1 - core)

    def plane_peer(step):
        there = (here + step) % 16
        return there // 8, there % 8

    def window(row, col):
        return tokens_ref.at[0, row * 8 : row * 8 + 8, col * 8 : col * 8 + 8, :]

    def local(src, dst, slot):
        copy = pltpu.make_async_copy(src, dst, local_sem.at[slot])
        copy.start()
        return copy

    def remote(src, dst, send, recv, peer):
        return pltpu.make_async_remote_copy(
            src_ref=src, dst_ref=dst, send_sem=send, recv_sem=recv, device_id=peer,
            device_id_type=MESH,
        )

    def begin(copy):
        def one(step, carry):
            copy(step).start()
            return carry

        return one

    def finish(copy):
        def one(step, carry):
            copy(step).wait()
            return carry

        return one

    mask_copy = local(mask_ref.at[0], near.at[1, 1], 0)
    own = [
        local(window(row, col), ext.at[1 + row, 1 + col], 1 + row * 2 + col)
        for row in range(2)
        for col in range(2)
    ]
    wq_copy = local(wqkv_ref, wq, 5)
    cot_copy = local(cot_ref.at[0], cots, 6)
    wo_copy = local(wout_ref, wo, 7)

    barrier = pltpu.get_barrier_semaphore()

    def greet(peer):
        pl.semaphore_signal(barrier, inc=1, device_id=peer, device_id_type=MESH)

    def greet_plane(step, carry):
        peer_hi, peer_lon = plane_peer(step)
        greet((peer_lon, lat, peer_hi * 2 + core))
        return carry

    def greet_lat(step, carry):
        greet((lon, (lat + step) % 8, lev))
        return carry

    greet(partner)
    lax.fori_loop(1, 16, greet_plane, 0)
    lax.fori_loop(1, 8, greet_lat, 0)
    mask_copy.wait()
    pl.semaphore_wait(barrier, 23)

    mask_lon = [
        remote(near.at[1, 1], near.at[1, 2], s_m.at[0], v_m.at[0], west),
        remote(near.at[1, 1], near.at[1, 0], s_m.at[1], v_m.at[1], east),
    ]
    to_lon = []
    to_lat = []
    for row in range(2):
        to_lon.append(
            remote(window(row, 0), ext.at[1 + row, 3], s_lon.at[row, 0], v_lon.at[row, 0], west)
        )
        to_lon.append(
            remote(window(row, 1), ext.at[1 + row, 0], s_lon.at[row, 1], v_lon.at[row, 1], east)
        )
    for col in range(2):
        to_lat.append(
            remote(window(0, col), ext.at[3, 1 + col], s_lat.at[0, col], v_lat.at[0, col], north)
        )
        to_lat.append(
            remote(window(1, col), ext.at[0, 1 + col], s_lat.at[1, col], v_lat.at[1, col], south)
        )
    for copy in mask_lon + to_lon + to_lat:
        copy.start()

    gain = gain_ref[...]

    def normalise(row, col):
        normed, _ = norm_rows(ext[row, col].astype(FULL).reshape(64, 512))
        at = (row * 4 + col) * 64
        hid[at : at + 64, :] = (normed * gain).astype(LOW)

    def project(spots):
        for row, col in spots:
            normalise(row, col)
        rows = jnp.concatenate(
            [hid[(row * 4 + col) * 64 : (row * 4 + col) * 64 + 64, :] for row, col in spots], axis=0
        )
        for group in range(2):
            for part in range(2):
                first = 512 + part * 512 + group * 256
                result = dot_nn(rows, wq[:, first : first + 256]).astype(LOW)
                for index, (row, col) in enumerate(spots):
                    at = (row * 4 + col) * 64
                    kv[group, at : at + 64, part * 256 : part * 256 + 256] = result[
                        index * 64 : index * 64 + 64
                    ]
        return rows

    token_of = lax.broadcasted_iota(jnp.int32, (128, 16), 0)
    lane_of = lax.broadcasted_iota(jnp.int32, (128, 16), 1)
    repeat_rows = jnp.where(token_of // 8 == lane_of, 1.0, 0.0).astype(LOW)
    picks = [jnp.where(lane_of == token_of % 8 + 8 * side, 1.0, 0.0) for side in range(2)]
    has_north = jnp.where(lat > 0, 1.0, 0.0).astype(FULL)
    has_south = jnp.where(lat < 7, 1.0, 0.0).astype(FULL)

    def mask_columns(tile_row, tile_col):
        tall = dot_nn(repeat_rows, near[tile_row, tile_col].astype(FULL).astype(LOW))
        return [
            jnp.broadcast_to(jnp.sum(tall * pick, axis=1, keepdims=True), (128, 128))
            for pick in picks
        ]

    for copy in own:
        copy.wait()
    oceans = [None] * 4
    centre = mask_columns(1, 1)
    for row in range(2):
        for col in range(2):
            oceans[row * 2 + col] = centre[col][row * 64 : row * 64 + 64]
    wq_copy.wait()
    rows = project(((1, 1), (1, 2), (2, 1), (2, 2)))
    qs[...] = (dot_nn(rows, wq[:, :512]) * 0.125).astype(LOW)
    for copy in mask_lon:
        copy.wait()
    mask_lat = [
        remote(near.at[1], near.at[2], s_m.at[2], v_m.at[2], north),
        remote(near.at[1], near.at[0], s_m.at[3], v_m.at[3], south),
    ]
    for copy in mask_lat:
        copy.start()
    cot_copy.wait()
    for row in range(2):
        band = cots[row * 8 : row * 8 + 8].astype(FULL)
        for col in range(2):
            at = (row * 2 + col) * 64
            piece = band[:, col * 8 : col * 8 + 8, :].reshape(64, 512)
            flags = jnp.concatenate([oceans[row * 2 + col]] * 4, axis=1)
            gb[at : at + 64, :] = (piece * flags).astype(LOW)
    wo_copy.wait()
    dout[...] = dot_nt(gb[...], wo[...]).astype(LOW)
    for group in range(2):
        for row in range(4):
            gkv[group, row * 256 : row * 256 + 256, :] = jnp.zeros((256, 512), FULL)
    relayed = []
    for row, line, peer in ((0, 3, north), (1, 0, south)):
        for side, col in ((0, 3), (1, 0)):
            to_lon[row * 2 + side].wait()
            relayed.append(
                remote(
                    ext.at[1 + row, col], ext.at[line, col],
                    s_rel.at[row, side], v_rel.at[row, side], peer,
                )
            )
            relayed[-1].start()
    project(((1, 0), (2, 0), (1, 3), (2, 3)))
    for copy in mask_lat:
        copy.wait()
    place = ((0, 1), (1, 0), (1, 1), (2, 0))
    for tile_row in range(3):
        for tile_col in range(3):
            sides = centre if (tile_row, tile_col) == (1, 1) else mask_columns(tile_row, tile_col)
            for row in range(4):
                for col in range(4):
                    if place[row][0] != tile_row or place[col][0] != tile_col:
                        continue
                    at = (row * 4 + col) * 64
                    flags = sides[place[col][1]][place[row][1] * 64 : place[row][1] * 64 + 64]
                    if row == 0:
                        flags = flags * has_north
                    if row == 3:
                        flags = flags * has_south
                    bias[at : at + 64, :] = (flags - 1.0) * 1000000000.0
    for copy in to_lat:
        copy.wait()
    project(((0, 1), (0, 2), (3, 1), (3, 2)))
    for copy in relayed:
        copy.wait()
    project(((0, 0), (0, 3), (3, 0), (3, 3)))

    block_row = lax.broadcasted_iota(jnp.int32, (256, 256), 0) // 64
    block_col = lax.broadcasted_iota(jnp.int32, (256, 256), 1) // 64
    diag = jnp.where(block_row == block_col, 1.0, 0.0).astype(FULL)
    diag_low = diag.astype(LOW)

    def fold(square):
        kept = square * diag
        return (kept[:64] + kept[64:128]) + (kept[128:192] + kept[192:])

    def attend(index, group):
        row, col = index // 2, index % 2
        at = slice(index * 64, index * 64 + 64)
        lanes = slice(group * 256, group * 256 + 256)
        alive = jnp.max(oceans[index], axis=(0, 1), keepdims=True)
        slot = index % 2
        spare = 192 if col == 0 else 0
        for part in range(3):
            pscr[slot, part * 256 + spare : part * 256 + spare + 64, :] = jnp.zeros((64, 256), LOW)
            dscr[slot, part * 256 + spare : part * 256 + spare + 64, :] = jnp.zeros((64, 256), LOW)
        starts = [(row + part) * 256 + col * 64 for part in range(3)]
        spans = [slice(start, start + 192) for start in starts]
        inner = [slice(part * 256 + col * 64, part * 256 + col * 64 + 192) for part in range(3)]
        slab = slice(row * 256, row * 256 + 768)
        qbd = jnp.concatenate([qs[at, lanes]] * 4, axis=0) * diag_low
        dbd = jnp.concatenate([dout[at, lanes]] * 4, axis=0) * diag_low
        scores = [
            dot_nt(kv[group, span, :256], qbd) + jnp.concatenate([bias[span, :]] * 2, axis=1)
            for span in spans
        ]
        tops = [jnp.max(part, axis=0, keepdims=True) for part in scores]
        top = jnp.maximum(jnp.maximum(tops[0], tops[1]), tops[2])
        weights = [jnp.exp(part - top) for part in scores]
        sums = [jnp.sum(part, axis=0, keepdims=True) for part in weights]
        inverse = 1.0 / (sums[0] + sums[1] + sums[2])
        probs = [part * inverse for part in weights]
        for part in range(3):
            pscr[slot, inner[part], :] = probs[part].astype(LOW)
        out = fold(dot_tn(pscr[slot], kv[group, slab, 256:]))
        mixed[at, lanes] = (out * alive).astype(LOW)
        gprobs = [dot_nt(kv[group, span, 256:], dbd) for span in spans]
        deltas = [
            jnp.sum(probs[part] * gprobs[part], axis=0, keepdims=True) for part in range(3)
        ]
        delta = deltas[0] + deltas[1] + deltas[2]
        for part in range(3):
            dscr[slot, inner[part], :] = (probs[part] * (gprobs[part] - delta)).astype(LOW)
        gq[at, lanes] = (fold(dot_tn(dscr[slot], kv[group, slab, :256])) * 0.125).astype(LOW)
        for part in range(3):
            gkv[group, spans[part], :256] += dot_nn(dscr[slot, inner[part], :], qbd)
            gkv[group, spans[part], 256:] += dot_nn(pscr[slot, inner[part], :], dbd)

    wgs = (wg_a, wg_c, wg_b)
    r1s = (r1_a, r1_c, r1_b)
    a1s = (a1_a, a1_c, a1_b)
    r2s = (r2_a, r2_c, r2_b)
    a2s = (a2_a, a2_c, a2_b)
    r3s = (r3_a, r3_c, r3_b)
    totals = (sum_a, sum_c, sum_b)

    def pair_copies(chunk):
        return [
            remote(
                wgs[chunk].at[part * 2 + 1 - core], r1s[chunk].at[part],
                s_pair.at[chunk, part], v_pair.at[chunk, part], partner,
            )
            for part in range(2)
        ]

    def plane_copy(chunk):
        def one(step):
            peer_hi, peer_lon = plane_peer(step)
            return remote(
                a1s[chunk].at[peer_hi * 8 + peer_lon], r2s[chunk].at[step - 1],
                s_plane.at[chunk, step - 1], v_plane.at[chunk, step - 1],
                (peer_lon, lat, peer_hi * 2 + core),
            )

        return one

    def z_copy(chunk):
        def one(step):
            return remote(
                a2s[chunk], r3s[chunk].at[step - 1],
                s_z.at[chunk, step - 1], v_z.at[chunk, step - 1], (lon, (lat + step) % 8, lev),
            )

        return one

    def all_copy(chunk):
        def one(step):
            return remote(
                totals[chunk].at[lon], totals[chunk].at[lon],
                s_all.at[chunk, step - 1], v_all.at[chunk, step - 1],
                ((lon + step) % 8, lat, lev),
            )

        return one

    def start_pair(chunk):
        for copy in pair_copies(chunk):
            copy.start()

    def pair_to_plane(chunk):
        for part, copy in enumerate(pair_copies(chunk)):
            copy.wait()

            def add(piece, carry):
                span = pl.ds(pl.multiple_of(piece * 16, 16), 16)
                total = wgs[chunk][part * 2 + core, span, :].astype(FULL) + r1s[chunk][
                    part, span, :
                ].astype(FULL)
                a1s[chunk][part * 8 + piece] = total.astype(LOW)
                return carry

            lax.fori_loop(0, 8, add, 0)
        lax.fori_loop(1, 16, begin(plane_copy(chunk)), 0)

    def plane_to_z(chunk):
        lax.fori_loop(1, 16, finish(plane_copy(chunk)), 0)
        for first in range(0, WIDTHS[chunk], 256):
            cols = slice(first, first + 256)
            total = a1s[chunk][here, :, cols].astype(FULL)
            for step in range(15):
                total = total + r2s[chunk][step, :, cols].astype(FULL)
            a2s[chunk][:, cols] = total.astype(LOW)
        lax.fori_loop(1, 8, begin(z_copy(chunk)), 0)

    def z_to_all(chunk):
        lax.fori_loop(1, 8, finish(z_copy(chunk)), 0)
        for first in range(0, WIDTHS[chunk], 256):
            cols = slice(first, first + 256)
            total = a2s[chunk][:, cols].astype(FULL)
            for step in range(7):
                total = total + r3s[chunk][step, :, cols].astype(FULL)
            totals[chunk][lon, :, cols] = total.astype(LOW)
        lax.fori_loop(1, 8, begin(all_copy(chunk)), 0)

    def return_lat(group):
        corners = []
        edges = []
        for line, target, peer, side in ((0, from_south, north, 0), (3, from_north, south, 1)):
            for col in (0, 3):
                corners.append(
                    remote(
                        back.at[group, line, col], target.at[group, col],
                        s_gz.at[group, side, col], v_gz.at[group, side, col], peer,
                    )
                )
            edges.append(
                remote(
                    back.at[group, line, pl.ds(1, 2)], target.at[group, pl.ds(1, 2)],
                    s_gz.at[group, side, 1], v_gz.at[group, side, 1], peer,
                )
            )
        return corners, edges

    def return_lon(group):
        return [
            remote(
                to_west.at[group], from_east.at[group], s_gx.at[group, 0], v_gx.at[group, 0], west
            ),
            remote(
                to_east.at[group], from_west.at[group], s_gx.at[group, 1], v_gx.at[group, 1], east
            ),
        ]

    sources = (from_north, from_south)

    def start_return(group):
        corners, edges = return_lat(group)
        for copy in corners + edges:
            copy.start()

    def corner_to_lon(group):
        for copy in return_lat(group)[0]:
            copy.wait()
        for row in range(2):
            to_west[group, row] = (
                back[group, 1 + row, 0].astype(FULL) + sources[row][group, 0].astype(FULL)
            ).astype(LOW)
            to_east[group, row] = (
                back[group, 1 + row, 3].astype(FULL) + sources[row][group, 3].astype(FULL)
            ).astype(LOW)
        for copy in return_lon(group):
            copy.start()

    def finish_return(group):
        for copy in return_lat(group)[1] + return_lon(group):
            copy.wait()
        pieces = []
        for row in range(2):
            for col in range(2):
                at = ((1 + row) * 4 + 1 + col) * 64
                side = (from_west, from_east)[col]
                pieces.append(
                    (
                        gkv[group, at : at + 64, :]
                        + sources[row][group, 1 + col].astype(FULL)
                        + side[group, row].astype(FULL)
                    ).astype(LOW)
                )
        return jnp.concatenate(pieces, axis=0)

    def settle(group):
        for row in range(4):
            for col in range(4):
                at = (row * 4 + col) * 64
                back[group, row, col] = gkv[group, at : at + 64, :].astype(LOW)

    def own_rows(row):
        return slice(row * 256 + 320, row * 256 + 448)

    def weight_chunk(group, chunk):
        lanes = slice(group * 256, group * 256 + 256)
        query = dot_tn(hid[own_rows(0), :], gq[:128, lanes]) + dot_tn(
            hid[own_rows(1), :], gq[128:, lanes]
        )
        wgs[chunk][:, :, :256] = query.astype(LOW).reshape(4, 128, 256)
        both = dot_tn(hid[...], back[group].reshape(1024, 512))
        wgs[chunk][:, :, 256:] = both.astype(LOW).reshape(4, 128, 512)

    for index in range(4):
        attend(index, 0)
    settle(0)
    weight_chunk(0, 0)
    start_pair(0)
    start_return(0)
    attend(0, 1)
    pair_to_plane(0)
    attend(1, 1)
    attend(2, 1)
    corner_to_lon(0)
    attend(3, 1)
    wg_c[...] = dot_tn(mixed[...], gb[...]).astype(LOW).reshape(4, 128, 512)
    start_pair(1)
    settle(1)
    weight_chunk(1, 2)
    start_pair(2)
    pair_to_plane(1)
    pair_to_plane(2)
    start_return(1)
    plane_to_z(0)
    branch = dot_nn(mixed[...], wo[...])
    for row in range(2):
        pieces = []
        for col in range(2):
            index = row * 2 + col
            flags = jnp.concatenate([oceans[index]] * 4, axis=1)
            tokens = ext[1 + row, 1 + col].astype(FULL).reshape(64, 512)
            result = tokens + flags * branch[index * 64 : index * 64 + 64]
            pieces.append(result.reshape(8, 8, 512))
        layer_ref[0, row * 8 : row * 8 + 8] = jnp.concatenate(pieces, axis=1).astype(LOW)
    z_to_all(0)
    plane_to_z(1)
    corner_to_lon(1)
    plane_to_z(2)
    z_to_all(1)
    grad_hidden = dot_nt(gq[...], wq[:, :512])
    for group in range(2):
        both = finish_return(group)
        for part in range(2):
            first = 512 + part * 512 + group * 256
            grad_hidden = grad_hidden + dot_nt(
                both[:, part * 256 : part * 256 + 256], wq[:, first : first + 256]
            )
    for row in range(2):
        pieces = []
        cot = cots[row * 8 : row * 8 + 8].astype(FULL)
        for col in range(2):
            at = (row * 2 + col) * 64
            normed, scaling = norm_rows(ext[1 + row, 1 + col].astype(FULL).reshape(64, 512))
            scaled = grad_hidden[at : at + 64] * gain
            correction = (
                scaled
                - jnp.mean(scaled, axis=-1, keepdims=True)
                - normed * jnp.mean(scaled * normed, axis=-1, keepdims=True)
            )
            result = cot[:, col * 8 : col * 8 + 8, :].reshape(64, 512) + scaling * correction
            pieces.append(result.reshape(8, 8, 512))
        grad_ref[0, row * 8 : row * 8 + 8] = jnp.concatenate(pieces, axis=1).astype(LOW)
    z_to_all(2)
    for chunk in range(3):
        lax.fori_loop(1, 8, finish(all_copy(chunk)), 0)


def layer(tokens_in, cotangent, qkv_weight, out_weight, gain, ocean_mask):
    dma = pltpu.SemaphoreType.DMA
    vmem = pl.BlockSpec(memory_space=pltpu.VMEM)
    hbm = pl.BlockSpec(memory_space=pltpu.HBM)
    scratch = [
        pltpu.VMEM((4, 4, 8, 8, 512), LOW),
        pltpu.VMEM((3, 3, 16, 16), jnp.int32),
        pltpu.VMEM((16, 16, 512), LOW),
        pltpu.VMEM((512, 1536), LOW),
        pltpu.VMEM((512, 512), LOW),
        pltpu.VMEM((1024, 512), LOW),
        pltpu.VMEM((2, 1024, 512), LOW),
        pltpu.VMEM((2, 1024, 512), FULL),
        pltpu.VMEM((2, 4, 4, 64, 512), LOW),
    ]
    scratch += [pltpu.VMEM((256, 512), LOW)] * 5
    scratch += [pltpu.VMEM((2, 768, 256), LOW)] * 2
    scratch += [pltpu.VMEM((1024, 128), FULL)]
    scratch += [pltpu.VMEM((4, 128, width), LOW) for width in WIDTHS]
    scratch += [pltpu.VMEM((2, 128, width), LOW) for width in WIDTHS]
    scratch += [pltpu.VMEM((16, 16, width), LOW) for width in WIDTHS]
    scratch += [pltpu.VMEM((15, 16, width), LOW) for width in WIDTHS]
    scratch += [pltpu.VMEM((16, width), LOW) for width in WIDTHS]
    scratch += [pltpu.VMEM((7, 16, width), LOW) for width in WIDTHS]
    scratch += [pltpu.VMEM((2, 4, 64, 512), LOW)] * 2
    scratch += [pltpu.VMEM((2, 2, 64, 512), LOW)] * 4
    scratch += [dma((8,))] + [dma((2, 2))] * 6 + [dma((4,))] * 2
    scratch += [dma((3, 2))] * 2 + [dma((3, 15))] * 2 + [dma((3, 7))] * 4
    scratch += [dma((2, 2, 4))] * 2 + [dma((2, 2))] * 2
    return pl.pallas_call(
        layer_kernel,
        out_shape=(
            jax.ShapeDtypeStruct((1, 16, 16, 512), LOW),
            jax.ShapeDtypeStruct((1, 16, 16, 512), LOW),
        )
        + tuple(jax.ShapeDtypeStruct((8, 16, width), LOW) for width in WIDTHS),
        in_specs=[hbm, hbm, hbm, hbm, vmem, hbm],
        out_specs=(vmem,) * 5,
        scratch_shapes=scratch,
        compiler_params=pltpu.CompilerParams(
            collective_id=0, has_side_effects=True, vmem_limit_bytes=44 << 20
        ),
    )(tokens_in, cotangent, qkv_weight, out_weight, gain, ocean_mask)


def finish_kernel(
    layer_ref, grad_ref, sum_a, sum_c, sum_b, wqkv_ref, gain_ref,
    layer_out, grad_out, qkv_out, out_out, gain_out, rows, sem,
):
    lev = lax.axis_index("lev")
    first = pl.multiple_of(lev * 128, 128)
    fetch = pltpu.make_async_copy(wqkv_ref.at[pl.ds(first, 128)], rows, sem)
    fetch.start()
    layer_out[...] = layer_ref[...]
    grad_out[...] = grad_ref[...]
    out_out[...] = sum_c[...].reshape(128, 512).astype(FULL)
    for part in range(3):
        for group, source in enumerate((sum_a, sum_b)):
            at = part * 512 + group * 256
            qkv_out[:, at : at + 256] = (
                source[:, :, part * 256 : part * 256 + 256].reshape(128, 256).astype(FULL)
            )
    fetch.wait()
    total = jnp.sum(rows[...].astype(FULL) * qkv_out[...], axis=1, keepdims=True)
    line = jnp.transpose(jnp.broadcast_to(total, (128, 128)))[:1]
    gain_out[...] = line / gain_ref[:, pl.ds(first, 128)]


def finish_outputs(parts, qkv_weight, gain):
    vmem = pl.BlockSpec(memory_space=pltpu.VMEM)
    return pl.pallas_call(
        finish_kernel,
        out_shape=(
            jax.ShapeDtypeStruct((1, 16, 16, 512), LOW),
            jax.ShapeDtypeStruct((1, 16, 16, 512), LOW),
            jax.ShapeDtypeStruct((128, 1536), FULL),
            jax.ShapeDtypeStruct((128, 512), FULL),
            jax.ShapeDtypeStruct((1, 128), FULL),
        ),
        in_specs=[vmem] * 5 + [pl.BlockSpec(memory_space=pltpu.HBM), vmem],
        out_specs=(vmem,) * 5,
        scratch_shapes=[pltpu.VMEM((128, 1536), LOW), pltpu.SemaphoreType.DMA],
        compiler_params=pltpu.CompilerParams(vmem_limit_bytes=16 << 20),
    )(*parts, qkv_weight, gain)


def on_device(tokens_in, cotangent, qkv_weight, out_weight, norm_gain, ocean_mask):
    gain = norm_gain.reshape(1, 512)
    parts = layer(tokens_in, cotangent, qkv_weight, out_weight, gain, ocean_mask)
    layer_out, input_grad, qkv_grad, out_grad, gain_grad = finish_outputs(parts, qkv_weight, gain)
    return (layer_out, input_grad, qkv_grad, out_grad, gain_grad.reshape(128))


def solution(mesh):
    placed = (
        P("lev", "lat", "lon", None),
        P("lev", "lat", "lon", None),
        P(),
        P(),
        P(),
        P("lev", "lat", "lon"),
    )
    return jax.shard_map(
        on_device,
        mesh=mesh,
        in_specs=placed,
        out_specs=(
            P("lev", "lat", "lon", None),
            P("lev", "lat", "lon", None),
            P("lev", None),
            P("lev", None),
            P("lev"),
        ),
        check_vma=False,
    )
```

time: 907 us -> 76.3 us (0.08); the launches traced: 895 us -> 75.9 us
  waiting for transfers between devices: 556 us -> 0 us
  blocking collectives: 151 us -> 0 us
  local copies, waits for them, and re-layouts: 76.9 us -> 5.72 us
  Pallas kernels: 0 us -> 69.4 us
  other arithmetic: 49.1 us -> 0 us
  matrix products: 24.9 us -> 0 us
  starting transfers between devices: 21.5 us -> 0 us
  between operations: 15.1 us -> 0.82 us
    psum x1 -> x0, waiting for transfers between devices: 448 us -> none  [plane_sum(): return lax.psum((gradients[0], gradients[1], gradients[2]), ('lon', 'lat'))]
    psum x1 -> x0, blocking collectives: 144 us -> none  [plane_sum(): return lax.psum((gradients[0], gradients[1], gradients[2]), ('lon', 'lat'))]
    pallas_call x0 -> x2, Pallas kernels: none -> 69.4 us  [the longest x1 67.9 us: layer(): pl.pallas_call(layer_kernel, out_shape=(jax.ShapeDtypeStruct((1, 16, 16,...]
    ppermute x12 -> x0, waiting for transfers between devices: 56.3 us -> none  [the longest x6 52.8 us: with_halo(): lax.ppermute(lax.slice_in_dim(block, block.shape[dim] - width, None, axis...]
    reduce_scatter x2 -> x0, waiting for transfers between devices: 51.7 us -> none  [the longest x1 51.7 us: level_share(): lax.psum_scatter(gradients[0], 'lev', scatter_dimension=0, tiled=True)]
    slice x15 -> x0, local copies, waits for them, and re-layouts: 23.3 us -> none  [the longest x2 6.93 us: on_device(): key_rows = near[..., :features]]
    scatter-add x10 -> x0, other arithmetic: 23 us -> none  [the longest x6 15.1 us: spread_back(): totals = totals.at[lat_step * window_side:(lat_step + lat_windows) * wind...]
    ppermute x12 -> x0, starting transfers between devices: 21.3 us -> none  [the longest x6 12.9 us: with_halo(): lax.ppermute(lax.slice_in_dim(block, block.shape[dim] - width, None, axis...]
  transfers between devices with their start and end apart: 15 -> 0, of which waited for: 7 -> 0; matrix products, arithmetic and copies ran while one was open for 5% -> 0% of each run, Pallas kernels for 0% -> 0%
where the time goes in v3:
time: 76.3 us; the launch traced here: 75.9 us
  Pallas kernels  69.4 us (91%)
  local copies, waits for them, and re-layouts  5.72 us (7%)
  between operations  0.82 us (1%)
    pallas_call x1, Pallas kernels, layer(): pl.pallas_call(layer_kernel, out_shape=(jax.ShapeDtypeStruct((1, 16, 16,...  67.9 us
    unnamed x12, local copies, waits for them, and re-layouts  5.72 us

profile of v3, /device:TPU:8, one launch (start us, length us, event | category | flops | bytes accessed | tf_op | source)
XLA Modules:
  0.0 75.9 jit_solution(6050479228060088628)
XLA Ops:
  0.6 0.0 copy-start
  0.6 1.4 %copy-done = bf16[512,1536]{1,0:T(8,128)(2,1)S(1)} copy-done((bf16[512,1536]{1,0:T(8,128)(2,1)S(1)}, bf16[512,1536]{1,0:T(8,128)(2,1)}, u32[]{:S(2)}) %copy-start) | copy-done | bytes 1572888
  2.0 0.0 copy-start.1
  2.0 1.0 %copy-done.1 = bf16[512,512]{1,0:T(8,128)(2,1)S(1)} copy-done((bf16[512,512]{1,0:T(8,128)(2,1)S(1)}, bf16[512,512]{1,0:T(8,128)(2,1)}, u32[]{:S(2)}) %copy-start.1) | copy-done | bytes 524312
  3.1 0.0 copy-start.2
  3.1 0.9 %copy-done.2 = bf16[1,16,16,512]{3,2,1,0:T(8,128)(2,1)S(1)} copy-done((bf16[1,16,16,512]{3,2,1,0:T(8,128)(2,1)S(1)}, bf16[1,16,16,512]{3,2,1,0:T(8,128)(2,1)}, u32[]{:S(2)}) %copy-start.2) | copy-done | bytes 262168
  4.0 0.0 copy-start.3
  4.0 0.9 %copy-done.3 = bf16[1,16,16,512]{3,2,1,0:T(8,128)(2,1)S(1)} copy-done((bf16[1,16,16,512]{3,2,1,0:T(8,128)(2,1)S(1)}, bf16[1,16,16,512]{3,2,1,0:T(8,128)(2,1)}, u32[]{:S(2)}) %copy-start.3) | copy-done | bytes 262168
  5.0 0.0 copy-start.4
  5.0 0.7 copy-done.4
  5.7 0.0 copy-start.5
  5.7 0.7 copy-done.5
  6.4 67.9 %shard_map.101 = (bf16[1,16,16,512]{3,2,1,0:T(8,128)(2,1)S(1)}, bf16[1,16,16,512]{3,2,1,0:T(8,128)(2,1)S(1)}, bf16[8,16,768]{2,1,0:T(8,128)(2,1)S(1)}, bf16[8,16...) custom-call(bf16[1,16,16,512]{3,2,1,0:T(8,128)(2,1)S(1)} %copy-done.2, bf16[1,16,16,512]{3,2,1,0:T(8,128)(2,1)S(1)} %copy-done.3, ...), custom_call_target="tpu_custom_call" | custom-call | tf_op jit(solution)/shard_map/pallas_call | solution.py:565
  74.3 1.5 %shard_map.102 = (bf16[1,16,16,512]{3,2,1,0:T(8,128)(2,1)}, bf16[1,16,16,512]{3,2,1,0:T(8,128)(2,1)}, f32[128,1536]{1,0:T(8,128)}, f32[128,512]{1,0:T(8,128)}, f32[1,128]{1,0:T(1,128)}) custom-call(bf16[1,16,16,512]{3,2,1,0:T(8,128)(2,1)S(1)} %get-tuple-element.15.layer_ref, bf16[1,16,16,512]{3,2,1,0:T(8,128)(2,1)S(1)} %get-tuple-element.16.grad_ref, ...), custom_call_target="tpu_custom_call" | custom-call | tf_op jit(solution)/shard_map/pallas_call | solution.py:606
Async XLA Ops:
  0.6 1.4 %copy-start = (bf16[512,1536]{1,0:T(8,128)(2,1)S(1)}, bf16[512,1536]{1,0:T(8,128)(2,1)}, u32[]{:S(2)}) copy-start(bf16[512,1536]{1,0:T(8,128)(2,1)} %wqkv_ref.3) | copy-start | bytes 4718596
  2.0 1.0 %copy-start.1 = (bf16[512,512]{1,0:T(8,128)(2,1)S(1)}, bf16[512,512]{1,0:T(8,128)(2,1)}, u32[]{:S(2)}) copy-start(bf16[512,512]{1,0:T(8,128)(2,1)} %wout_ref.1) | copy-start | bytes 1572868
  3.1 0.9 %copy-start.2 = (bf16[1,16,16,512]{3,2,1,0:T(8,128)(2,1)S(1)}, bf16[1,16,16,512]{3,2,1,0:T(8,128)(2,1)}, u32[]{:S(2)}) copy-start(bf16[1,16,16,512]{3,2,1,0:T(8,128)(2,1)} %tokens_ref.1) | copy-start | bytes 786436
  4.0 0.9 %copy-start.3 = (bf16[1,16,16,512]{3,2,1,0:T(8,128)(2,1)S(1)}, bf16[1,16,16,512]{3,2,1,0:T(8,128)(2,1)}, u32[]{:S(2)}) copy-start(bf16[1,16,16,512]{3,2,1,0:T(8,128)(2,1)} %cot_ref.1) | copy-start | bytes 786436
  5.0 0.7 copy-start.4
  5.7 0.7 copy-start.5

commit v4 on v3

--- a/solution.py
+++ b/solution.py
@@ -8,7 +8,8 @@
 MESH = pl.DeviceIdType.MESH
 LOW = jnp.bfloat16
 FULL = jnp.float32
-WIDTHS = (768, 512, 768)
+WIDTHS = (1024, 512, 512)
+WHOLE_VMEM = 67043328
 
 
 def dot_nn(left, right):
@@ -38,12 +39,14 @@
 
 def layer_kernel(
     tokens_ref, cot_ref, wqkv_ref, wout_ref, gain_ref, mask_ref,
-    layer_ref, grad_ref, sum_a, sum_c, sum_b,
-    ext, near, cots, wq, wo, hid, kv, gkv, back, qs, gb, dout, mixed, gq, pscr, dscr, bias,
-    wg_a, wg_c, wg_b, r1_a, r1_c, r1_b, a1_a, a1_c, a1_b, r2_a, r2_c, r2_b,
-    a2_a, a2_c, a2_b, r3_a, r3_c, r3_b,
+    layer_ref, grad_ref, sum_0, sum_1, sum_2,
+    ext, near, cots, wq, wo, gains, layer_buf, grad_buf,
+    hid, keys, values, gkeys, gvalues, low_keys, low_values, ghidden, ghalo,
+    qs, gb, dout, mixed, gq, probs_all, pscr, dscr, bias,
+    wg_0, wg_1, wg_2, r1_0, r1_1, r1_2, a1_0, a1_1, a1_2, r2_0, r2_1, r2_2,
+    a2_0, a2_1, a2_2, r3_0, r3_1, r3_2, g5_0, g5_1, g5_2,
     from_north, from_south, from_west, from_east, to_west, to_east,
-    local_sem, s_lon, v_lon, s_lat, v_lat, s_rel, v_rel, s_m, v_m,
+    local_sem, out_sem, s_lon, v_lon, s_lat, v_lat, s_rel, v_rel, s_m, v_m,
     s_pair, v_pair, s_plane, v_plane, s_z, v_z, s_all, v_all, s_gz, v_gz, s_gx, v_gx,
 ):
     lon = lax.axis_index("lon")
@@ -99,6 +102,7 @@
     wq_copy = local(wqkv_ref, wq, 5)
     cot_copy = local(cot_ref.at[0], cots, 6)
     wo_copy = local(wout_ref, wo, 7)
+    gain_copy = local(gain_ref, gains, 8)
 
     barrier = pltpu.get_barrier_semaphore()
 
@@ -143,7 +147,8 @@
     for copy in mask_lon + to_lon + to_lat:
         copy.start()
 
-    gain = gain_ref[...]
+    gain_copy.wait()
+    gain = gains[...]
 
     def normalise(row, col):
         normed, _ = norm_rows(ext[row, col].astype(FULL).reshape(64, 512))
@@ -156,15 +161,12 @@
         rows = jnp.concatenate(
             [hid[(row * 4 + col) * 64 : (row * 4 + col) * 64 + 64, :] for row, col in spots], axis=0
         )
-        for group in range(2):
-            for part in range(2):
-                first = 512 + part * 512 + group * 256
-                result = dot_nn(rows, wq[:, first : first + 256]).astype(LOW)
-                for index, (row, col) in enumerate(spots):
-                    at = (row * 4 + col) * 64
-                    kv[group, at : at + 64, part * 256 : part * 256 + 256] = result[
-                        index * 64 : index * 64 + 64
-                    ]
+        for part, target in enumerate((keys, values)):
+            first = 512 + part * 512
+            result = dot_nn(rows, wq[:, first : first + 512]).astype(LOW)
+            for index, (row, col) in enumerate(spots):
+                at = (row * 4 + col) * 64
+                target[at : at + 64, :] = result[index * 64 : index * 64 + 64]
         return rows
 
     token_of = lax.broadcasted_iota(jnp.int32, (128, 16), 0)
@@ -209,9 +211,9 @@
             gb[at : at + 64, :] = (piece * flags).astype(LOW)
     wo_copy.wait()
     dout[...] = dot_nt(gb[...], wo[...]).astype(LOW)
-    for group in range(2):
-        for row in range(4):
-            gkv[group, row * 256 : row * 256 + 256, :] = jnp.zeros((256, 512), FULL)
+    for row in range(4):
+        gkeys[row * 256 : row * 256 + 256, :] = jnp.zeros((256, 512), FULL)
+        gvalues[row * 256 : row * 256 + 256, :] = jnp.zeros((256, 512), FULL)
     relayed = []
     for row, line, peer in ((0, 3, north), (1, 0, south)):
         for side, col in ((0, 3), (1, 0)):
@@ -257,24 +259,30 @@
         kept = square * diag
         return (kept[:64] + kept[64:128]) + (kept[128:192] + kept[192:])
 
-    def attend(index, group):
+    def shape_of(index, group):
         row, col = index // 2, index % 2
         at = slice(index * 64, index * 64 + 64)
         lanes = slice(group * 256, group * 256 + 256)
-        alive = jnp.max(oceans[index], axis=(0, 1), keepdims=True)
-        slot = index % 2
-        spare = 192 if col == 0 else 0
-        for part in range(3):
-            pscr[slot, part * 256 + spare : part * 256 + spare + 64, :] = jnp.zeros((64, 256), LOW)
-            dscr[slot, part * 256 + spare : part * 256 + spare + 64, :] = jnp.zeros((64, 256), LOW)
         starts = [(row + part) * 256 + col * 64 for part in range(3)]
         spans = [slice(start, start + 192) for start in starts]
         inner = [slice(part * 256 + col * 64, part * 256 + col * 64 + 192) for part in range(3)]
         slab = slice(row * 256, row * 256 + 768)
-        qbd = jnp.concatenate([qs[at, lanes]] * 4, axis=0) * diag_low
-        dbd = jnp.concatenate([dout[at, lanes]] * 4, axis=0) * diag_low
+        spare = 192 if col == 0 else 0
+        return at, lanes, spans, inner, slab, spare
+
+    def spread_heads(rows):
+        return jnp.concatenate([rows] * 4, axis=0) * diag_low
+
+    def attend(index, group):
+        at, lanes, spans, inner, slab, spare = shape_of(index, group)
+        slot = index * 2 + group
+        alive = jnp.max(oceans[index], axis=(0, 1), keepdims=True)
+        for part in range(3):
+            pscr[slot, part * 256 + spare : part * 256 + spare + 64, :] = jnp.zeros((64, 256), LOW)
+        qbd = spread_heads(qs[at, lanes])
+        dbd = spread_heads(dout[at, lanes])
         scores = [
-            dot_nt(kv[group, span, :256], qbd) + jnp.concatenate([bias[span, :]] * 2, axis=1)
+            dot_nt(keys[span, lanes], qbd) + jnp.concatenate([bias[span, :]] * 2, axis=1)
             for span in spans
         ]
         tops = [jnp.max(part, axis=0, keepdims=True) for part in scores]
@@ -282,30 +290,45 @@
         weights = [jnp.exp(part - top) for part in scores]
         sums = [jnp.sum(part, axis=0, keepdims=True) for part in weights]
         inverse = 1.0 / (sums[0] + sums[1] + sums[2])
-        probs = [part * inverse for part in weights]
         for part in range(3):
-            pscr[slot, inner[part], :] = probs[part].astype(LOW)
-        out = fold(dot_tn(pscr[slot], kv[group, slab, 256:]))
+            probs = weights[part] * inverse
+            probs_all[slot, part] = probs
+            pscr[slot, inner[part], :] = probs.astype(LOW)
+        out = fold(dot_tn(pscr[slot], values[slab, lanes]))
         mixed[at, lanes] = (out * alive).astype(LOW)
-        gprobs = [dot_nt(kv[group, span, 256:], dbd) for span in spans]
+        for part in range(3):
+            gvalues[spans[part], lanes] += dot_nn(pscr[slot, inner[part], :], dbd)
+
+    def retreat(index, group):
+        at, lanes, spans, inner, slab, spare = shape_of(index, group)
+        slot = index * 2 + group
+        side = index % 2
+        for part in range(3):
+            dscr[side, part * 256 + spare : part * 256 + spare + 64, :] = jnp.zeros((64, 256), LOW)
+        qbd = spread_heads(qs[at, lanes])
+        dbd = spread_heads(dout[at, lanes])
+        gprobs = [dot_nt(values[span, lanes], dbd) for span in spans]
         deltas = [
-            jnp.sum(probs[part] * gprobs[part], axis=0, keepdims=True) for part in range(3)
+            jnp.sum(probs_all[slot, part] * gprobs[part], axis=0, keepdims=True)
+            for part in range(3)
         ]
         delta = deltas[0] + deltas[1] + deltas[2]
         for part in range(3):
-            dscr[slot, inner[part], :] = (probs[part] * (gprobs[part] - delta)).astype(LOW)
-        gq[at, lanes] = (fold(dot_tn(dscr[slot], kv[group, slab, :256])) * 0.125).astype(LOW)
+            dscr[side, inner[part], :] = (
+                probs_all[slot, part] * (gprobs[part] - delta)
+            ).astype(LOW)
+        gq[at, lanes] = (fold(dot_tn(dscr[side], keys[slab, lanes])) * 0.125).astype(LOW)
         for part in range(3):
-            gkv[group, spans[part], :256] += dot_nn(dscr[slot, inner[part], :], qbd)
-            gkv[group, spans[part], 256:] += dot_nn(pscr[slot, inner[part], :], dbd)
-
-    wgs = (wg_a, wg_c, wg_b)
-    r1s = (r1_a, r1_c, r1_b)
-    a1s = (a1_a, a1_c, a1_b)
-    r2s = (r2_a, r2_c, r2_b)
-    a2s = (a2_a, a2_c, a2_b)
-    r3s = (r3_a, r3_c, r3_b)
-    totals = (sum_a, sum_c, sum_b)
+            gkeys[spans[part], lanes] += dot_nn(dscr[side, inner[part], :], qbd)
+
+    wgs = (wg_0, wg_1, wg_2)
+    r1s = (r1_0, r1_1, r1_2)
+    a1s = (a1_0, a1_1, a1_2)
+    r2s = (r2_0, r2_1, r2_2)
+    a2s = (a2_0, a2_1, a2_2)
+    r3s = (r3_0, r3_1, r3_2)
+    totals = (g5_0, g5_1, g5_2)
+    outputs = (sum_0, sum_1, sum_2)
 
     def pair_copies(chunk):
         return [
@@ -356,9 +379,7 @@
 
             def add(piece, carry):
                 span = pl.ds(pl.multiple_of(piece * 16, 16), 16)
-                total = wgs[chunk][part * 2 + core, span, :].astype(FULL) + r1s[chunk][
-                    part, span, :
-                ].astype(FULL)
+                total = wgs[chunk][part * 2 + core, span, :] + r1s[chunk][part, span, :]
                 a1s[chunk][part * 8 + piece] = total.astype(LOW)
                 return carry
 
@@ -385,110 +406,77 @@
             totals[chunk][lon, :, cols] = total.astype(LOW)
         lax.fori_loop(1, 8, begin(all_copy(chunk)), 0)
 
-    def return_lat(group):
-        corners = []
-        edges = []
-        for line, target, peer, side in ((0, from_south, north, 0), (3, from_north, south, 1)):
-            for col in (0, 3):
-                corners.append(
-                    remote(
-                        back.at[group, line, col], target.at[group, col],
-                        s_gz.at[group, side, col], v_gz.at[group, side, col], peer,
-                    )
+    corners = []
+    edges = []
+    for line, target, peer, side in ((0, from_south, north, 0), (3, from_north, south, 1)):
+        for col in (0, 3):
+            corners.append(
+                remote(
+                    ghalo.at[line, col], target.at[col],
+                    s_gz.at[side, col], v_gz.at[side, col], peer,
                 )
-            edges.append(
-                remote(
-                    back.at[group, line, pl.ds(1, 2)], target.at[group, pl.ds(1, 2)],
-                    s_gz.at[group, side, 1], v_gz.at[group, side, 1], peer,
-                )
-            )
-        return corners, edges
-
-    def return_lon(group):
-        return [
+            )
+        edges.append(
             remote(
-                to_west.at[group], from_east.at[group], s_gx.at[group, 0], v_gx.at[group, 0], west
-            ),
-            remote(
-                to_east.at[group], from_west.at[group], s_gx.at[group, 1], v_gx.at[group, 1], east
-            ),
-        ]
-
+                ghalo.at[line, pl.ds(1, 2)], target.at[pl.ds(1, 2)],
+                s_gz.at[side, 1], v_gz.at[side, 1], peer,
+            )
+        )
+    sideways = [
+        remote(to_west, from_east, s_gx.at[0], v_gx.at[0], west),
+        remote(to_east, from_west, s_gx.at[1], v_gx.at[1], east),
+    ]
     sources = (from_north, from_south)
-
-    def start_return(group):
-        corners, edges = return_lat(group)
-        for copy in corners + edges:
-            copy.start()
-
-    def corner_to_lon(group):
-        for copy in return_lat(group)[0]:
-            copy.wait()
-        for row in range(2):
-            to_west[group, row] = (
-                back[group, 1 + row, 0].astype(FULL) + sources[row][group, 0].astype(FULL)
-            ).astype(LOW)
-            to_east[group, row] = (
-                back[group, 1 + row, 3].astype(FULL) + sources[row][group, 3].astype(FULL)
-            ).astype(LOW)
-        for copy in return_lon(group):
-            copy.start()
-
-    def finish_return(group):
-        for copy in return_lat(group)[1] + return_lon(group):
-            copy.wait()
-        pieces = []
-        for row in range(2):
-            for col in range(2):
-                at = ((1 + row) * 4 + 1 + col) * 64
-                side = (from_west, from_east)[col]
-                pieces.append(
-                    (
-                        gkv[group, at : at + 64, :]
-                        + sources[row][group, 1 + col].astype(FULL)
-                        + side[group, row].astype(FULL)
-                    ).astype(LOW)
-                )
-        return jnp.concatenate(pieces, axis=0)
-
-    def settle(group):
-        for row in range(4):
-            for col in range(4):
-                at = (row * 4 + col) * 64
-                back[group, row, col] = gkv[group, at : at + 64, :].astype(LOW)
 
     def own_rows(row):
         return slice(row * 256 + 320, row * 256 + 448)
 
-    def weight_chunk(group, chunk):
+    def query_key_chunk(group):
         lanes = slice(group * 256, group * 256 + 256)
+        for row in range(4):
+            span = slice(row * 256, row * 256 + 256)
+            low_keys[span, lanes] = gkeys[span, lanes].astype(LOW)
         query = dot_tn(hid[own_rows(0), :], gq[:128, lanes]) + dot_tn(
             hid[own_rows(1), :], gq[128:, lanes]
         )
-        wgs[chunk][:, :, :256] = query.astype(LOW).reshape(4, 128, 256)
-        both = dot_tn(hid[...], back[group].reshape(1024, 512))
-        wgs[chunk][:, :, 256:] = both.astype(LOW).reshape(4, 128, 512)
-
-    for index in range(4):
-        attend(index, 0)
-    settle(0)
-    weight_chunk(0, 0)
+        wgs[1 + group][:, :, :256] = query.reshape(4, 128, 256)
+        wgs[1 + group][:, :, 256:] = dot_tn(hid[...], low_keys[:, lanes]).reshape(4, 128, 256)
+        start_pair(1 + group)
+
+    for group in range(2):
+        for index in range(4):
+            attend(index, group)
+    wg_0[:, :, :512] = dot_tn(mixed[...], gb[...]).reshape(4, 128, 512)
+    for row in range(4):
+        span = slice(row * 256, row * 256 + 256)
+        low_values[span, :] = gvalues[span, :].astype(LOW)
+    wg_0[:, :, 512:] = dot_tn(hid[...], low_values[...]).reshape(4, 128, 512)
     start_pair(0)
-    start_return(0)
-    attend(0, 1)
+    retreat(0, 0)
     pair_to_plane(0)
-    attend(1, 1)
-    attend(2, 1)
-    corner_to_lon(0)
-    attend(3, 1)
-    wg_c[...] = dot_tn(mixed[...], gb[...]).astype(LOW).reshape(4, 128, 512)
-    start_pair(1)
-    settle(1)
-    weight_chunk(1, 2)
-    start_pair(2)
+    for index in range(1, 4):
+        retreat(index, 0)
+    query_key_chunk(0)
+    for row in range(4):
+        span = slice(row * 256, row * 256 + 256)
+        ghidden[span, :] = dot_nt(low_values[span, :], wq[:, 1024:])
+    retreat(0, 1)
     pair_to_plane(1)
+    for index in range(1, 4):
+        retreat(index, 1)
+    query_key_chunk(1)
+    for row in (0, 3, 1, 2):
+        span = slice(row * 256, row * 256 + 256)
+        total = ghidden[span, :] + dot_nt(low_keys[span, :], wq[:, 512:1024])
+        if row in (1, 2):
+            ghidden[span, :] = total
+        for col in range(4):
+            if row in (0, 3) or col in (0, 3):
+                ghalo[row, col] = total[col * 64 : col * 64 + 64].astype(LOW)
+        if row == 3:
+            for copy in corners + edges:
+                copy.start()
     pair_to_plane(2)
-    start_return(1)
     plane_to_z(0)
     branch = dot_nn(mixed[...], wo[...])
     for row in range(2):
@@ -499,27 +487,42 @@
             tokens = ext[1 + row, 1 + col].astype(FULL).reshape(64, 512)
             result = tokens + flags * branch[index * 64 : index * 64 + 64]
             pieces.append(result.reshape(8, 8, 512))
-        layer_ref[0, row * 8 : row * 8 + 8] = jnp.concatenate(pieces, axis=1).astype(LOW)
+        layer_buf[0, row * 8 : row * 8 + 8] = jnp.concatenate(pieces, axis=1).astype(LOW)
+    layer_copy = pltpu.make_async_copy(layer_buf, layer_ref, out_sem.at[0])
+    layer_copy.start()
+    grad_query = dot_nt(gq[...], wq[:, :512])
+    for copy in corners:
+        copy.wait()
+    for row in range(2):
+        to_west[row] = (
+            ghalo[1 + row, 0].astype(FULL) + sources[row][0].astype(FULL)
+        ).astype(LOW)
+        to_east[row] = (
+            ghalo[1 + row, 3].astype(FULL) + sources[row][3].astype(FULL)
+        ).astype(LOW)
+    for copy in sideways:
+        copy.start()
+    plane_to_z(1)
     z_to_all(0)
-    plane_to_z(1)
-    corner_to_lon(1)
     plane_to_z(2)
     z_to_all(1)
-    grad_hidden = dot_nt(gq[...], wq[:, :512])
-    for group in range(2):
-        both = finish_return(group)
-        for part in range(2):
-            first = 512 + part * 512 + group * 256
-            grad_hidden = grad_hidden + dot_nt(
-                both[:, part * 256 : part * 256 + 256], wq[:, first : first + 256]
-            )
+    for copy in edges + sideways:
+        copy.wait()
     for row in range(2):
         pieces = []
         cot = cots[row * 8 : row * 8 + 8].astype(FULL)
         for col in range(2):
-            at = (row * 2 + col) * 64
+            index = row * 2 + col
+            at = ((1 + row) * 4 + 1 + col) * 64
+            side = (from_west, from_east)[col]
+            grad_hidden = (
+                grad_query[index * 64 : index * 64 + 64]
+                + ghidden[at : at + 64, :]
+                + sources[row][1 + col].astype(FULL)
+                + side[row].astype(FULL)
+            )
             normed, scaling = norm_rows(ext[1 + row, 1 + col].astype(FULL).reshape(64, 512))
-            scaled = grad_hidden[at : at + 64] * gain
+            scaled = grad_hidden * gain
             correction = (
                 scaled
                 - jnp.mean(scaled, axis=-1, keepdims=True)
@@ -527,15 +530,23 @@
             )
             result = cot[:, col * 8 : col * 8 + 8, :].reshape(64, 512) + scaling * correction
             pieces.append(result.reshape(8, 8, 512))
-        grad_ref[0, row * 8 : row * 8 + 8] = jnp.concatenate(pieces, axis=1).astype(LOW)
+        grad_buf[0, row * 8 : row * 8 + 8] = jnp.concatenate(pieces, axis=1).astype(LOW)
+    grad_copy = pltpu.make_async_copy(grad_buf, grad_ref, out_sem.at[1])
+    grad_copy.start()
     z_to_all(2)
+    sum_copies = [
+        pltpu.make_async_copy(totals[chunk], outputs[chunk], out_sem.at[2 + chunk])
+        for chunk in range(3)
+    ]
     for chunk in range(3):
         lax.fori_loop(1, 8, finish(all_copy(chunk)), 0)
+        sum_copies[chunk].start()
+    for copy in [layer_copy, grad_copy] + sum_copies:
+        copy.wait()
 
 
 def layer(tokens_in, cotangent, qkv_weight, out_weight, gain, ocean_mask):
     dma = pltpu.SemaphoreType.DMA
-    vmem = pl.BlockSpec(memory_space=pltpu.VMEM)
     hbm = pl.BlockSpec(memory_space=pltpu.HBM)
     scratch = [
         pltpu.VMEM((4, 4, 8, 8, 512), LOW),
@@ -543,25 +554,30 @@
         pltpu.VMEM((16, 16, 512), LOW),
         pltpu.VMEM((512, 1536), LOW),
         pltpu.VMEM((512, 512), LOW),
-        pltpu.VMEM((1024, 512), LOW),
-        pltpu.VMEM((2, 1024, 512), LOW),
-        pltpu.VMEM((2, 1024, 512), FULL),
-        pltpu.VMEM((2, 4, 4, 64, 512), LOW),
+        pltpu.VMEM((1, 512), FULL),
+        pltpu.VMEM((1, 16, 16, 512), LOW),
+        pltpu.VMEM((1, 16, 16, 512), LOW),
     ]
+    scratch += [pltpu.VMEM((1024, 512), LOW)] * 3
+    scratch += [pltpu.VMEM((1024, 512), FULL)] * 2
+    scratch += [pltpu.VMEM((1024, 512), LOW)] * 2
+    scratch += [pltpu.VMEM((1024, 512), FULL), pltpu.VMEM((4, 4, 64, 512), LOW)]
     scratch += [pltpu.VMEM((256, 512), LOW)] * 5
-    scratch += [pltpu.VMEM((2, 768, 256), LOW)] * 2
+    scratch += [pltpu.VMEM((8, 3, 192, 256), FULL)]
+    scratch += [pltpu.VMEM((8, 768, 256), LOW), pltpu.VMEM((2, 768, 256), LOW)]
     scratch += [pltpu.VMEM((1024, 128), FULL)]
-    scratch += [pltpu.VMEM((4, 128, width), LOW) for width in WIDTHS]
-    scratch += [pltpu.VMEM((2, 128, width), LOW) for width in WIDTHS]
+    scratch += [pltpu.VMEM((4, 128, width), FULL) for width in WIDTHS]
+    scratch += [pltpu.VMEM((2, 128, width), FULL) for width in WIDTHS]
     scratch += [pltpu.VMEM((16, 16, width), LOW) for width in WIDTHS]
     scratch += [pltpu.VMEM((15, 16, width), LOW) for width in WIDTHS]
     scratch += [pltpu.VMEM((16, width), LOW) for width in WIDTHS]
     scratch += [pltpu.VMEM((7, 16, width), LOW) for width in WIDTHS]
-    scratch += [pltpu.VMEM((2, 4, 64, 512), LOW)] * 2
-    scratch += [pltpu.VMEM((2, 2, 64, 512), LOW)] * 4
-    scratch += [dma((8,))] + [dma((2, 2))] * 6 + [dma((4,))] * 2
+    scratch += [pltpu.VMEM((8, 16, width), LOW) for width in WIDTHS]
+    scratch += [pltpu.VMEM((4, 64, 512), LOW)] * 2
+    scratch += [pltpu.VMEM((2, 64, 512), LOW)] * 4
+    scratch += [dma((9,)), dma((5,))] + [dma((2, 2))] * 6 + [dma((4,))] * 2
     scratch += [dma((3, 2))] * 2 + [dma((3, 15))] * 2 + [dma((3, 7))] * 4
-    scratch += [dma((2, 2, 4))] * 2 + [dma((2, 2))] * 2
+    scratch += [dma((2, 4))] * 2 + [dma((2,))] * 2
     return pl.pallas_call(
         layer_kernel,
         out_shape=(
@@ -569,40 +585,69 @@
             jax.ShapeDtypeStruct((1, 16, 16, 512), LOW),
         )
         + tuple(jax.ShapeDtypeStruct((8, 16, width), LOW) for width in WIDTHS),
-        in_specs=[hbm, hbm, hbm, hbm, vmem, hbm],
-        out_specs=(vmem,) * 5,
+        in_specs=[hbm] * 6,
+        out_specs=(hbm,) * 5,
         scratch_shapes=scratch,
         compiler_params=pltpu.CompilerParams(
-            collective_id=0, has_side_effects=True, vmem_limit_bytes=44 << 20
+            collective_id=0, has_side_effects=True, vmem_limit_bytes=WHOLE_VMEM
         ),
     )(tokens_in, cotangent, qkv_weight, out_weight, gain, ocean_mask)
 
 
 def finish_kernel(
-    layer_ref, grad_ref, sum_a, sum_c, sum_b, wqkv_ref, gain_ref,
-    layer_out, grad_out, qkv_out, out_out, gain_out, rows, sem,
+    layer_ref, grad_ref, sum_0, sum_1, sum_2, wqkv_ref, gain_ref,
+    layer_out, grad_out, qkv_out, out_out, gain_out,
+    layer_buf, grad_buf, buf_0, buf_1, buf_2, rows, gains, qkv, outs, line_buf, in_sem, out_sem,
 ):
     lev = lax.axis_index("lev")
     first = pl.multiple_of(lev * 128, 128)
-    fetch = pltpu.make_async_copy(wqkv_ref.at[pl.ds(first, 128)], rows, sem)
-    fetch.start()
-    layer_out[...] = layer_ref[...]
-    grad_out[...] = grad_ref[...]
-    out_out[...] = sum_c[...].reshape(128, 512).astype(FULL)
-    for part in range(3):
-        for group, source in enumerate((sum_a, sum_b)):
+    pairs = (
+        (sum_1, buf_1), (sum_2, buf_2), (sum_0, buf_0), (wqkv_ref.at[pl.ds(first, 128)], rows),
+        (gain_ref, gains), (layer_ref, layer_buf), (grad_ref, grad_buf),
+    )
+    fetches = [
+        pltpu.make_async_copy(src, dst, in_sem.at[slot]) for slot, (src, dst) in enumerate(pairs)
+    ]
+    for copy in fetches:
+        copy.start()
+    stores = [
+        pltpu.make_async_copy(src, dst, out_sem.at[slot])
+        for slot, (src, dst) in enumerate(
+            (
+                (qkv, qkv_out), (outs, out_out), (layer_buf, layer_out), (grad_buf, grad_out),
+                (line_buf, gain_out),
+            )
+        )
+    ]
+    for group, source in enumerate((buf_1, buf_2)):
+        fetches[group].wait()
+        for part in range(2):
             at = part * 512 + group * 256
-            qkv_out[:, at : at + 256] = (
+            qkv[:, at : at + 256] = (
                 source[:, :, part * 256 : part * 256 + 256].reshape(128, 256).astype(FULL)
             )
-    fetch.wait()
-    total = jnp.sum(rows[...].astype(FULL) * qkv_out[...], axis=1, keepdims=True)
+    fetches[2].wait()
+    qkv[:, 1024:] = buf_0[:, :, 512:].reshape(128, 512).astype(FULL)
+    stores[0].start()
+    outs[...] = buf_0[:, :, :512].reshape(128, 512).astype(FULL)
+    stores[1].start()
+    fetches[5].wait()
+    stores[2].start()
+    fetches[6].wait()
+    stores[3].start()
+    fetches[3].wait()
+    fetches[4].wait()
+    total = jnp.sum(rows[...].astype(FULL) * qkv[...], axis=1, keepdims=True)
     line = jnp.transpose(jnp.broadcast_to(total, (128, 128)))[:1]
-    gain_out[...] = line / gain_ref[:, pl.ds(first, 128)]
+    line_buf[...] = line / gains[:, pl.ds(first, 128)]
+    stores[4].start()
+    for copy in stores:
+        copy.wait()
 
 
 def finish_outputs(parts, qkv_weight, gain):
-    vmem = pl.BlockSpec(memory_space=pltpu.VMEM)
+    hbm = pl.BlockSpec(memory_space=pltpu.HBM)
+    dma = pltpu.SemaphoreType.DMA
     return pl.pallas_call(
         finish_kernel,
         out_shape=(
@@ -612,10 +657,16 @@
             jax.ShapeDtypeStruct((128, 512), FULL),
             jax.ShapeDtypeStruct((1, 128), FULL),
         ),
-        in_specs=[vmem] * 5 + [pl.BlockSpec(memory_space=pltpu.HBM), vmem],
-        out_specs=(vmem,) * 5,
-        scratch_shapes=[pltpu.VMEM((128, 1536), LOW), pltpu.SemaphoreType.DMA],
-        compiler_params=pltpu.CompilerParams(vmem_limit_bytes=16 << 20),
+        in_specs=[hbm] * 7,
+        out_specs=(hbm,) * 5,
+        scratch_shapes=[pltpu.VMEM((1, 16, 16, 512), LOW)] * 2
+        + [pltpu.VMEM((8, 16, width), LOW) for width in WIDTHS]
+        + [
+            pltpu.VMEM((128, 1536), LOW), pltpu.VMEM((1, 512), FULL),
+            pltpu.VMEM((128, 1536), FULL), pltpu.VMEM((128, 512), FULL),
+            pltpu.VMEM((1, 128), FULL), dma((7,)), dma((5,)),
+        ],
+        compiler_params=pltpu.CompilerParams(vmem_limit_bytes=WHOLE_VMEM),
     )(*parts, qkv_weight, gain)
 
 

time: 76.3 us -> 70.8 us (0.928)
  local copies, waits for them, and re-layouts: 5.72 us -> 0 us
    unnamed x12 -> x0, local copies, waits for them, and re-layouts: 5.72 us -> none
    pallas_call x1, Pallas kernels: 1.45 us -> 2.34 us  [finish_outputs(): pl.pallas_call(finish_kernel, out_shape=(jax.ShapeDtypeStruct((1, 16, 16,...]
    pallas_call x1, Pallas kernels: 67.9 us -> 67.1 us  [layer(): pl.pallas_call(layer_kernel, out_shape=(jax.ShapeDtypeStruct((1, 16, 16,...]
where the time goes in v4:
time: 70.8 us; the launch traced here: 70.2 us
  Pallas kernels  69.4 us (98%)
  between operations  0.8 us (1%)
    pallas_call x1, Pallas kernels, layer(): pl.pallas_call(layer_kernel, out_shape=(jax.ShapeDtypeStruct((1, 16, 16,...  67.1 us
    pallas_call x1, Pallas kernels, finish_outputs(): pl.pallas_call(finish_kernel, out_shape=(jax.ShapeDtypeStruct((1, 16, 16,...  2.34 us

profile of v4, /device:TPU:8, one launch (start us, length us, event | category | flops | bytes accessed | tf_op | source)
XLA Modules:
  0.0 70.2 jit_solution(12125720614724595440)
XLA Ops:
  0.6 67.1 %shard_map.101 = (bf16[1,16,16,512]{3,2,1,0:T(8,128)(2,1)}, bf16[1,16,16,512]{3,2,1,0:T(8,128)(2,1)}, bf16[8,16,1024]{2,1,0:T(8,128)(2,1)}, bf16[8,16,512]{2,1,0:T(8,128)(2,1)}, bf16[8,16,512]{2,1,0:T(8,128)(2,1)}) custom-call(bf16[1,16,16,512]{3,2,1,0:T(8,128)(2,1)} %tokens_ref.1, bf16[1,16,16,512]{3,2,1,0:T(8,128)(2,1)} %cot_ref.1, ...), custom_call_target="tpu_custom_call" | custom-call | tf_op jit(solution)/shard_map/pallas_call | solution.py:581
  67.7 2.3 %shard_map.102 = (bf16[1,16,16,512]{3,2,1,0:T(8,128)(2,1)}, bf16[1,16,16,512]{3,2,1,0:T(8,128)(2,1)}, f32[128,1536]{1,0:T(8,128)}, f32[128,512]{1,0:T(8,128)}, f32[1,128]{1,0:T(1,128)}) custom-call(bf16[1,16,16,512]{3,2,1,0:T(8,128)(2,1)} %get-tuple-element.15.layer_ref, bf16[1,16,16,512]{3,2,1,0:T(8,128)(2,1)} %get-tuple-element.16.grad_ref, ...), custom_call_target="tpu_custom_call" | custom-call | tf_op jit(solution)/shard_map/pallas_call | solution.py:651

commit v5 on v4

--- a/solution.py
+++ b/solution.py
@@ -8,7 +8,7 @@
 MESH = pl.DeviceIdType.MESH
 LOW = jnp.bfloat16
 FULL = jnp.float32
-WIDTHS = (1024, 512, 512)
+WIDTHS = (512, 512, 512, 512)
 WHOLE_VMEM = 67043328
 
 
@@ -39,12 +39,12 @@
 
 def layer_kernel(
     tokens_ref, cot_ref, wqkv_ref, wout_ref, gain_ref, mask_ref,
-    layer_ref, grad_ref, sum_0, sum_1, sum_2,
+    layer_ref, grad_ref, sum_0, sum_1, sum_2, sum_3,
     ext, near, cots, wq, wo, gains, layer_buf, grad_buf,
     hid, keys, values, gkeys, gvalues, low_keys, low_values, ghidden, ghalo,
     qs, gb, dout, mixed, gq, probs_all, pscr, dscr, bias,
-    wg_0, wg_1, wg_2, r1_0, r1_1, r1_2, a1_0, a1_1, a1_2, r2_0, r2_1, r2_2,
-    a2_0, a2_1, a2_2, r3_0, r3_1, r3_2, g5_0, g5_1, g5_2,
+    wg_0, wg_1, wg_2, wg_3, r1_0, r1_1, r1_2, r1_3, a1_0, a1_1, a1_2, a1_3, r2_0, r2_1, r2_2, r2_3,
+    a2_0, a2_1, a2_2, a2_3, r3_0, r3_1, r3_2, r3_3, g5_0, g5_1, g5_2, g5_3,
     from_north, from_south, from_west, from_east, to_west, to_east,
     local_sem, out_sem, s_lon, v_lon, s_lat, v_lat, s_rel, v_rel, s_m, v_m,
     s_pair, v_pair, s_plane, v_plane, s_z, v_z, s_all, v_all, s_gz, v_gz, s_gx, v_gx,
@@ -62,8 +62,8 @@
     partner = (lon, lat, hi * 2 + 1 - core)
 
     def plane_peer(step):
-        there = (here + step) % 16
-        return there // 8, there % 8
+        there = (here + step) & 15
+        return there >> 3, there & 7
 
     def window(row, col):
         return tokens_ref.at[0, row * 8 : row * 8 + 8, col * 8 : col * 8 + 8, :]
@@ -321,14 +321,14 @@
         for part in range(3):
             gkeys[spans[part], lanes] += dot_nn(dscr[side, inner[part], :], qbd)
 
-    wgs = (wg_0, wg_1, wg_2)
-    r1s = (r1_0, r1_1, r1_2)
-    a1s = (a1_0, a1_1, a1_2)
-    r2s = (r2_0, r2_1, r2_2)
-    a2s = (a2_0, a2_1, a2_2)
-    r3s = (r3_0, r3_1, r3_2)
-    totals = (g5_0, g5_1, g5_2)
-    outputs = (sum_0, sum_1, sum_2)
+    wgs = (wg_0, wg_1, wg_2, wg_3)
+    r1s = (r1_0, r1_1, r1_2, r1_3)
+    a1s = (a1_0, a1_1, a1_2, a1_3)
+    r2s = (r2_0, r2_1, r2_2, r2_3)
+    a2s = (a2_0, a2_1, a2_2, a2_3)
+    r3s = (r3_0, r3_1, r3_2, r3_3)
+    totals = (g5_0, g5_1, g5_2, g5_3)
+    outputs = (sum_0, sum_1, sum_2, sum_3)
 
     def pair_copies(chunk):
         return [
@@ -439,31 +439,36 @@
         query = dot_tn(hid[own_rows(0), :], gq[:128, lanes]) + dot_tn(
             hid[own_rows(1), :], gq[128:, lanes]
         )
-        wgs[1 + group][:, :, :256] = query.reshape(4, 128, 256)
-        wgs[1 + group][:, :, 256:] = dot_tn(hid[...], low_keys[:, lanes]).reshape(4, 128, 256)
-        start_pair(1 + group)
+        wgs[2 + group][:, :, :256] = query.reshape(4, 128, 256)
+        wgs[2 + group][:, :, 256:] = dot_tn(hid[...], low_keys[:, lanes]).reshape(4, 128, 256)
+        start_pair(2 + group)
 
     for group in range(2):
         for index in range(4):
             attend(index, group)
-    wg_0[:, :, :512] = dot_tn(mixed[...], gb[...]).reshape(4, 128, 512)
+    wg_0[...] = dot_tn(mixed[...], gb[...]).reshape(4, 128, 512)
+    start_pair(0)
     for row in range(4):
         span = slice(row * 256, row * 256 + 256)
         low_values[span, :] = gvalues[span, :].astype(LOW)
-    wg_0[:, :, 512:] = dot_tn(hid[...], low_values[...]).reshape(4, 128, 512)
-    start_pair(0)
+    wg_1[...] = dot_tn(hid[...], low_values[...]).reshape(4, 128, 512)
+    start_pair(1)
     retreat(0, 0)
+    retreat(1, 0)
     pair_to_plane(0)
-    for index in range(1, 4):
-        retreat(index, 0)
+    retreat(2, 0)
+    pair_to_plane(1)
+    retreat(3, 0)
     query_key_chunk(0)
     for row in range(4):
         span = slice(row * 256, row * 256 + 256)
         ghidden[span, :] = dot_nt(low_values[span, :], wq[:, 1024:])
     retreat(0, 1)
-    pair_to_plane(1)
-    for index in range(1, 4):
-        retreat(index, 1)
+    retreat(1, 1)
+    pair_to_plane(2)
+    retreat(2, 1)
+    plane_to_z(0)
+    retreat(3, 1)
     query_key_chunk(1)
     for row in (0, 3, 1, 2):
         span = slice(row * 256, row * 256 + 256)
@@ -476,8 +481,8 @@
         if row == 3:
             for copy in corners + edges:
                 copy.start()
-    pair_to_plane(2)
-    plane_to_z(0)
+    pair_to_plane(3)
+    plane_to_z(1)
     branch = dot_nn(mixed[...], wo[...])
     for row in range(2):
         pieces = []
@@ -491,6 +496,7 @@
     layer_copy = pltpu.make_async_copy(layer_buf, layer_ref, out_sem.at[0])
     layer_copy.start()
     grad_query = dot_nt(gq[...], wq[:, :512])
+    z_to_all(0)
     for copy in corners:
         copy.wait()
     for row in range(2):
@@ -502,10 +508,10 @@
         ).astype(LOW)
     for copy in sideways:
         copy.start()
-    plane_to_z(1)
-    z_to_all(0)
     plane_to_z(2)
     z_to_all(1)
+    plane_to_z(3)
+    z_to_all(2)
     for copy in edges + sideways:
         copy.wait()
     for row in range(2):
@@ -533,12 +539,12 @@
         grad_buf[0, row * 8 : row * 8 + 8] = jnp.concatenate(pieces, axis=1).astype(LOW)
     grad_copy = pltpu.make_async_copy(grad_buf, grad_ref, out_sem.at[1])
     grad_copy.start()
-    z_to_all(2)
+    z_to_all(3)
     sum_copies = [
         pltpu.make_async_copy(totals[chunk], outputs[chunk], out_sem.at[2 + chunk])
-        for chunk in range(3)
+        for chunk in range(4)
     ]
-    for chunk in range(3):
+    for chunk in range(4):
         lax.fori_loop(1, 8, finish(all_copy(chunk)), 0)
         sum_copies[chunk].start()
     for copy in [layer_copy, grad_copy] + sum_copies:
@@ -575,8 +581,8 @@
     scratch += [pltpu.VMEM((8, 16, width), LOW) for width in WIDTHS]
     scratch += [pltpu.VMEM((4, 64, 512), LOW)] * 2
     scratch += [pltpu.VMEM((2, 64, 512), LOW)] * 4
-    scratch += [dma((9,)), dma((5,))] + [dma((2, 2))] * 6 + [dma((4,))] * 2
-    scratch += [dma((3, 2))] * 2 + [dma((3, 15))] * 2 + [dma((3, 7))] * 4
+    scratch += [dma((9,)), dma((6,))] + [dma((2, 2))] * 6 + [dma((4,))] * 2
+    scratch += [dma((4, 2))] * 2 + [dma((4, 15))] * 2 + [dma((4, 7))] * 4
     scratch += [dma((2, 4))] * 2 + [dma((2,))] * 2
     return pl.pallas_call(
         layer_kernel,
@@ -586,7 +592,7 @@
         )
         + tuple(jax.ShapeDtypeStruct((8, 16, width), LOW) for width in WIDTHS),
         in_specs=[hbm] * 6,
-        out_specs=(hbm,) * 5,
+        out_specs=(hbm,) * 6,
         scratch_shapes=scratch,
         compiler_params=pltpu.CompilerParams(
             collective_id=0, has_side_effects=True, vmem_limit_bytes=WHOLE_VMEM
@@ -595,14 +601,15 @@
 
 
 def finish_kernel(
-    layer_ref, grad_ref, sum_0, sum_1, sum_2, wqkv_ref, gain_ref,
+    layer_ref, grad_ref, sum_0, sum_1, sum_2, sum_3, wqkv_ref, gain_ref,
     layer_out, grad_out, qkv_out, out_out, gain_out,
-    layer_buf, grad_buf, buf_0, buf_1, buf_2, rows, gains, qkv, outs, line_buf, in_sem, out_sem,
+    layer_buf, grad_buf, buf_0, buf_1, buf_2, buf_3, rows, gains, qkv, outs, line_buf, in_sem,
+    out_sem,
 ):
     lev = lax.axis_index("lev")
     first = pl.multiple_of(lev * 128, 128)
     pairs = (
-        (sum_1, buf_1), (sum_2, buf_2), (sum_0, buf_0), (wqkv_ref.at[pl.ds(first, 128)], rows),
+        (sum_2, buf_2), (sum_3, buf_3), (sum_1, buf_1), (sum_0, buf_0), (wqkv_ref.at[pl.ds(first, 128)], rows),
         (gain_ref, gains), (layer_ref, layer_buf), (grad_ref, grad_buf),
     )
     fetches = [
@@ -619,7 +626,7 @@
             )
         )
     ]
-    for group, source in enumerate((buf_1, buf_2)):
+    for group, source in enumerate((buf_2, buf_3)):
         fetches[group].wait()
         for part in range(2):
             at = part * 512 + group * 256
@@ -627,16 +634,17 @@
                 source[:, :, part * 256 : part * 256 + 256].reshape(128, 256).astype(FULL)
             )
     fetches[2].wait()
-    qkv[:, 1024:] = buf_0[:, :, 512:].reshape(128, 512).astype(FULL)
+    qkv[:, 1024:] = buf_1[...].reshape(128, 512).astype(FULL)
     stores[0].start()
-    outs[...] = buf_0[:, :, :512].reshape(128, 512).astype(FULL)
+    fetches[3].wait()
+    outs[...] = buf_0[...].reshape(128, 512).astype(FULL)
     stores[1].start()
+    fetches[6].wait()
+    stores[2].start()
+    fetches[7].wait()
+    stores[3].start()
+    fetches[4].wait()
     fetches[5].wait()
-    stores[2].start()
-    fetches[6].wait()
-    stores[3].start()
-    fetches[3].wait()
-    fetches[4].wait()
     total = jnp.sum(rows[...].astype(FULL) * qkv[...], axis=1, keepdims=True)
     line = jnp.transpose(jnp.broadcast_to(total, (128, 128)))[:1]
     line_buf[...] = line / gains[:, pl.ds(first, 128)]
@@ -657,14 +665,14 @@
             jax.ShapeDtypeStruct((128, 512), FULL),
             jax.ShapeDtypeStruct((1, 128), FULL),
         ),
-        in_specs=[hbm] * 7,
+        in_specs=[hbm] * 8,
         out_specs=(hbm,) * 5,
         scratch_shapes=[pltpu.VMEM((1, 16, 16, 512), LOW)] * 2
         + [pltpu.VMEM((8, 16, width), LOW) for width in WIDTHS]
         + [
             pltpu.VMEM((128, 1536), LOW), pltpu.VMEM((1, 512), FULL),
             pltpu.VMEM((128, 1536), FULL), pltpu.VMEM((128, 512), FULL),
-            pltpu.VMEM((1, 128), FULL), dma((7,)), dma((5,)),
+            pltpu.VMEM((1, 128), FULL), dma((8,)), dma((5,)),
         ],
         compiler_params=pltpu.CompilerParams(vmem_limit_bytes=WHOLE_VMEM),
     )(*parts, qkv_weight, gain)

time: 70.8 us -> 69.2 us (0.977)
  Pallas kernels: 69.4 us -> 68.2 us
    pallas_call x1, Pallas kernels: 67.1 us -> 65.9 us  [layer(): pl.pallas_call(layer_kernel, out_shape=(jax.ShapeDtypeStruct((1, 16, 16,...]
where the time goes in v5:
time: 69.2 us; the launch traced here: 69 us
  Pallas kernels  68.2 us (99%)
  between operations  0.8 us (1%)
    pallas_call x1, Pallas kernels, layer(): pl.pallas_call(layer_kernel, out_shape=(jax.ShapeDtypeStruct((1, 16, 16,...  65.9 us
    pallas_call x1, Pallas kernels, finish_outputs(): pl.pallas_call(finish_kernel, out_shape=(jax.ShapeDtypeStruct((1, 16, 16,...  2.3 us

profile of v5, /device:TPU:8, one launch (start us, length us, event | category | flops | bytes accessed | tf_op | source)
XLA Modules:
  0.0 69.0 jit_solution(16594040596412270486)
XLA Ops:
  0.6 65.9 %shard_map.101 = (bf16[1,16,16,512]{3,2,1,0:T(8,128)(2,1)}, bf16[1,16,16,512]{3,2,1,0:T(8,128)(2,1)}, bf16[8,16,512]{2,1,0:T(8,128)(2,1)}, bf16[8,16,512]{2,1,0:...) custom-call(bf16[1,16,16,512]{3,2,1,0:T(8,128)(2,1)} %tokens_ref.1, ...), custom_call_target="tpu_custom_call" | custom-call | tf_op jit(solution)/shard_map/pallas_call | solution.py:587
  66.6 2.3 %shard_map.102 = (bf16[1,16,16,512]{3,2,1,0:T(8,128)(2,1)}, bf16[1,16,16,512]{3,2,1,0:T(8,128)(2,1)}, f32[128,1536]{1,0:T(8,128)}, f32[128,512]{1,0:T(8,128)}, f32[1,128]{1,0:T(1,128)}) custom-call(bf16[1,16,16,512]{3,2,1,0:T(8,128)(2,1)} %get-tuple-element.16.layer_ref, bf16[1,16,16,512]{3,2,1,0:T(8,128)(2,1)} %get-tuple-element.17.grad_ref, ...), custom_call_target="tpu_custom_call" | custom-call | tf_op jit(solution)/shard_map/pallas_call | solution.py:659

commit v6 on v5

--- a/solution.py
+++ b/solution.py
@@ -46,7 +46,7 @@
     wg_0, wg_1, wg_2, wg_3, r1_0, r1_1, r1_2, r1_3, a1_0, a1_1, a1_2, a1_3, r2_0, r2_1, r2_2, r2_3,
     a2_0, a2_1, a2_2, a2_3, r3_0, r3_1, r3_2, r3_3, g5_0, g5_1, g5_2, g5_3,
     from_north, from_south, from_west, from_east, to_west, to_east,
-    local_sem, out_sem, s_lon, v_lon, s_lat, v_lat, s_rel, v_rel, s_m, v_m,
+    ready, local_sem, out_sem, s_lon, v_lon, s_lat, v_lat, s_rel, v_rel, s_m, v_m,
     s_pair, v_pair, s_plane, v_plane, s_z, v_z, s_all, v_all, s_gz, v_gz, s_gx, v_gx,
 ):
     lon = lax.axis_index("lon")
@@ -109,20 +109,21 @@
     def greet(peer):
         pl.semaphore_signal(barrier, inc=1, device_id=peer, device_id_type=MESH)
 
-    def greet_plane(step, carry):
-        peer_hi, peer_lon = plane_peer(step)
-        greet((peer_lon, lat, peer_hi * 2 + core))
-        return carry
-
-    def greet_lat(step, carry):
-        greet((lon, (lat + step) % 8, lev))
-        return carry
-
-    greet(partner)
-    lax.fori_loop(1, 16, greet_plane, 0)
-    lax.fori_loop(1, 8, greet_lat, 0)
+    close = (west, east, north, south, partner, (lon, lat, (1 - hi) * 2 + core))
+    for peer in close:
+        greet(peer)
+
+    def spread_word(turn):
+        if turn:
+            pl.semaphore_wait(ready.at[turn - 1], 6)
+        if turn < 4:
+            for peer in close:
+                pl.semaphore_signal(
+                    ready.at[turn], inc=1, device_id=peer, device_id_type=MESH
+                )
+
     mask_copy.wait()
-    pl.semaphore_wait(barrier, 23)
+    pl.semaphore_wait(barrier, 6)
 
     mask_lon = [
         remote(near.at[1, 1], near.at[1, 2], s_m.at[0], v_m.at[0], west),
@@ -146,6 +147,7 @@
         )
     for copy in mask_lon + to_lon + to_lat:
         copy.start()
+    spread_word(0)
 
     gain_copy.wait()
     gain = gains[...]
@@ -193,6 +195,7 @@
     wq_copy.wait()
     rows = project(((1, 1), (1, 2), (2, 1), (2, 2)))
     qs[...] = (dot_nn(rows, wq[:, :512]) * 0.125).astype(LOW)
+    spread_word(1)
     for copy in mask_lon:
         copy.wait()
     mask_lat = [
@@ -214,6 +217,7 @@
     for row in range(4):
         gkeys[row * 256 : row * 256 + 256, :] = jnp.zeros((256, 512), FULL)
         gvalues[row * 256 : row * 256 + 256, :] = jnp.zeros((256, 512), FULL)
+    spread_word(2)
     relayed = []
     for row, line, peer in ((0, 3, north), (1, 0, south)):
         for side, col in ((0, 3), (1, 0)):
@@ -243,9 +247,11 @@
                     if row == 3:
                         flags = flags * has_south
                     bias[at : at + 64, :] = (flags - 1.0) * 1000000000.0
+    spread_word(3)
     for copy in to_lat:
         copy.wait()
     project(((0, 1), (0, 2), (3, 1), (3, 2)))
+    spread_word(4)
     for copy in relayed:
         copy.wait()
     project(((0, 0), (0, 3), (3, 0), (3, 3)))
@@ -465,11 +471,11 @@
         ghidden[span, :] = dot_nt(low_values[span, :], wq[:, 1024:])
     retreat(0, 1)
     retreat(1, 1)
+    retreat(2, 1)
     pair_to_plane(2)
-    retreat(2, 1)
-    plane_to_z(0)
     retreat(3, 1)
     query_key_chunk(1)
+    plane_to_z(0)
     for row in (0, 3, 1, 2):
         span = slice(row * 256, row * 256 + 256)
         total = ghidden[span, :] + dot_nt(low_keys[span, :], wq[:, 512:1024])
@@ -479,10 +485,26 @@
             if row in (0, 3) or col in (0, 3):
                 ghalo[row, col] = total[col * 64 : col * 64 + 64].astype(LOW)
         if row == 3:
-            for copy in corners + edges:
+            for copy in corners:
                 copy.start()
-    pair_to_plane(3)
-    plane_to_z(1)
+            pair_to_plane(3)
+            plane_to_z(1)
+    for copy in edges:
+        copy.start()
+    for copy in corners:
+        copy.wait()
+    for row in range(2):
+        to_west[row] = (
+            ghalo[1 + row, 0].astype(FULL) + sources[row][0].astype(FULL)
+        ).astype(LOW)
+        to_east[row] = (
+            ghalo[1 + row, 3].astype(FULL) + sources[row][3].astype(FULL)
+        ).astype(LOW)
+    for copy in sideways:
+        copy.start()
+    z_to_all(0)
+    plane_to_z(2)
+    z_to_all(1)
     branch = dot_nn(mixed[...], wo[...])
     for row in range(2):
         pieces = []
@@ -496,22 +518,9 @@
     layer_copy = pltpu.make_async_copy(layer_buf, layer_ref, out_sem.at[0])
     layer_copy.start()
     grad_query = dot_nt(gq[...], wq[:, :512])
-    z_to_all(0)
-    for copy in corners:
-        copy.wait()
-    for row in range(2):
-        to_west[row] = (
-            ghalo[1 + row, 0].astype(FULL) + sources[row][0].astype(FULL)
-        ).astype(LOW)
-        to_east[row] = (
-            ghalo[1 + row, 3].astype(FULL) + sources[row][3].astype(FULL)
-        ).astype(LOW)
-    for copy in sideways:
-        copy.start()
-    plane_to_z(2)
-    z_to_all(1)
     plane_to_z(3)
     z_to_all(2)
+    z_to_all(3)
     for copy in edges + sideways:
         copy.wait()
     for row in range(2):
@@ -539,7 +548,6 @@
         grad_buf[0, row * 8 : row * 8 + 8] = jnp.concatenate(pieces, axis=1).astype(LOW)
     grad_copy = pltpu.make_async_copy(grad_buf, grad_ref, out_sem.at[1])
     grad_copy.start()
-    z_to_all(3)
     sum_copies = [
         pltpu.make_async_copy(totals[chunk], outputs[chunk], out_sem.at[2 + chunk])
         for chunk in range(4)
@@ -581,6 +589,7 @@
     scratch += [pltpu.VMEM((8, 16, width), LOW) for width in WIDTHS]
     scratch += [pltpu.VMEM((4, 64, 512), LOW)] * 2
     scratch += [pltpu.VMEM((2, 64, 512), LOW)] * 4
+    scratch += [pltpu.SemaphoreType.REGULAR((4,))]
     scratch += [dma((9,)), dma((6,))] + [dma((2, 2))] * 6 + [dma((4,))] * 2
     scratch += [dma((4, 2))] * 2 + [dma((4, 15))] * 2 + [dma((4, 7))] * 4
     scratch += [dma((2, 4))] * 2 + [dma((2,))] * 2

time: 69.2 us -> 66.5 us (0.961)
  Pallas kernels: 68.2 us -> 65.4 us
    pallas_call x1, Pallas kernels: 65.9 us -> 63.1 us  [layer(): pl.pallas_call(layer_kernel, out_shape=(jax.ShapeDtypeStruct((1, 16, 16,...]
where the time goes in v6:
time: 66.5 us; the launch traced here: 66.2 us
  Pallas kernels  65.4 us (98%)
  between operations  0.8 us (1%)
    pallas_call x1, Pallas kernels, layer(): pl.pallas_call(layer_kernel, out_shape=(jax.ShapeDtypeStruct((1, 16, 16,...  63.1 us
    pallas_call x1, Pallas kernels, finish_outputs(): pl.pallas_call(finish_kernel, out_shape=(jax.ShapeDtypeStruct((1, 16, 16,...  2.3 us

profile of v6, /device:TPU:8, one launch (start us, length us, event | category | flops | bytes accessed | tf_op | source)
XLA Modules:
  0.0 66.2 jit_solution(17750345474007501027)
XLA Ops:
  0.6 63.1 %shard_map.101 = (bf16[1,16,16,512]{3,2,1,0:T(8,128)(2,1)}, bf16[1,16,16,512]{3,2,1,0:T(8,128)(2,1)}, bf16[8,16,512]{2,1,0:T(8,128)(2,1)}, bf16[8,16,512]{2,1,0:...) custom-call(bf16[1,16,16,512]{3,2,1,0:T(8,128)(2,1)} %tokens_ref.1, ...), custom_call_target="tpu_custom_call" | custom-call | tf_op jit(solution)/shard_map/pallas_call | solution.py:596
  63.8 2.3 %shard_map.102 = (bf16[1,16,16,512]{3,2,1,0:T(8,128)(2,1)}, bf16[1,16,16,512]{3,2,1,0:T(8,128)(2,1)}, f32[128,1536]{1,0:T(8,128)}, f32[128,512]{1,0:T(8,128)}, f32[1,128]{1,0:T(1,128)}) custom-call(bf16[1,16,16,512]{3,2,1,0:T(8,128)(2,1)} %get-tuple-element.16.layer_ref, bf16[1,16,16,512]{3,2,1,0:T(8,128)(2,1)} %get-tuple-element.17.grad_ref, ...), custom_call_target="tpu_custom_call" | custom-call | tf_op jit(solution)/shard_map/pallas_call | solution.py:668

commit v7 on v6

--- a/solution.py
+++ b/solution.py
@@ -41,7 +41,7 @@
     tokens_ref, cot_ref, wqkv_ref, wout_ref, gain_ref, mask_ref,
     layer_ref, grad_ref, sum_0, sum_1, sum_2, sum_3,
     ext, near, cots, wq, wo, gains, layer_buf, grad_buf,
-    hid, keys, values, gkeys, gvalues, low_keys, low_values, ghidden, ghalo,
+    stats, hid, keys, values, gkeys, gvalues, low_keys, low_values, ghidden, ghalo,
     qs, gb, dout, mixed, gq, probs_all, pscr, dscr, bias,
     wg_0, wg_1, wg_2, wg_3, r1_0, r1_1, r1_2, r1_3, a1_0, a1_1, a1_2, a1_3, r2_0, r2_1, r2_2, r2_3,
     a2_0, a2_1, a2_2, a2_3, r3_0, r3_1, r3_2, r3_3, g5_0, g5_1, g5_2, g5_3,
@@ -79,20 +79,6 @@
             device_id_type=MESH,
         )
 
-    def begin(copy):
-        def one(step, carry):
-            copy(step).start()
-            return carry
-
-        return one
-
-    def finish(copy):
-        def one(step, carry):
-            copy(step).wait()
-            return carry
-
-        return one
-
     mask_copy = local(mask_ref.at[0], near.at[1, 1], 0)
     own = [
         local(window(row, col), ext.at[1 + row, 1 + col], 1 + row * 2 + col)
@@ -170,6 +156,56 @@
                 at = (row * 4 + col) * 64
                 target[at : at + 64, :] = result[index * 64 : index * 64 + 64]
         return rows
+
+    block_row = lax.broadcasted_iota(jnp.int32, (256, 256), 0) // 64
+    block_col = lax.broadcasted_iota(jnp.int32, (256, 256), 1) // 64
+    diag = jnp.where(block_row == block_col, 1.0, 0.0).astype(FULL)
+    diag_low = diag.astype(LOW)
+
+    def fold(square):
+        kept = square * diag
+        return (kept[:64] + kept[64:128]) + (kept[128:192] + kept[192:])
+
+    def shape_of(index, group):
+        row, col = index // 2, index % 2
+        at = slice(index * 64, index * 64 + 64)
+        lanes = slice(group * 256, group * 256 + 256)
+        starts = [(row + part) * 256 + col * 64 for part in range(3)]
+        spans = [slice(start, start + 192) for start in starts]
+        inner = [slice(part * 256 + col * 64, part * 256 + col * 64 + 192) for part in range(3)]
+        slab = slice(row * 256, row * 256 + 768)
+        spare = 192 if col == 0 else 0
+        return at, lanes, spans, inner, slab, spare
+
+    def spread_heads(rows):
+        return jnp.concatenate([rows] * 4, axis=0) * diag_low
+
+    def middle_parts(index):
+        return (1, 2) if index < 2 else (0, 1)
+
+    def score(index, group, part, qbd):
+        at, lanes, spans, inner, slab, spare = shape_of(index, group)
+        span = spans[part]
+        return dot_nt(keys[span, lanes], qbd) + jnp.concatenate([bias[span, :]] * 2, axis=1)
+
+    def attend_early(index, group):
+        at, lanes, spans, inner, slab, spare = shape_of(index, group)
+        slot = index * 2 + group
+        qbd = spread_heads(qs[at, lanes])
+        first, second = middle_parts(index)
+        score_a = score(index, group, first, qbd)
+        score_b = score(index, group, second, qbd)
+        top = jnp.maximum(
+            jnp.max(score_a, axis=0, keepdims=True), jnp.max(score_b, axis=0, keepdims=True)
+        )
+        weights_a = jnp.exp(score_a - top)
+        weights_b = jnp.exp(score_b - top)
+        probs_all[slot, first] = weights_a
+        probs_all[slot, second] = weights_b
+        stats[slot, 0:1, :] = top
+        stats[slot, 1:2, :] = jnp.sum(weights_a, axis=0, keepdims=True) + jnp.sum(
+            weights_b, axis=0, keepdims=True
+        )
 
     token_of = lax.broadcasted_iota(jnp.int32, (128, 16), 0)
     lane_of = lax.broadcasted_iota(jnp.int32, (128, 16), 1)
@@ -230,23 +266,34 @@
             )
             relayed[-1].start()
     project(((1, 0), (2, 0), (1, 3), (2, 3)))
+    place = ((0, 1), (1, 0), (1, 1), (2, 0))
+
+    def write_bias(tile_rows):
+        for tile_row in tile_rows:
+            for tile_col in range(3):
+                if (tile_row, tile_col) == (1, 1):
+                    sides = centre
+                else:
+                    sides = mask_columns(tile_row, tile_col)
+                for row in range(4):
+                    for col in range(4):
+                        if place[row][0] != tile_row or place[col][0] != tile_col:
+                            continue
+                        at = (row * 4 + col) * 64
+                        flags = sides[place[col][1]][place[row][1] * 64 : place[row][1] * 64 + 64]
+                        if row == 0:
+                            flags = flags * has_north
+                        if row == 3:
+                            flags = flags * has_south
+                        bias[at : at + 64, :] = (flags - 1.0) * 1000000000.0
+
+    write_bias((1,))
+    for index in range(4):
+        for group in range(2):
+            attend_early(index, group)
     for copy in mask_lat:
         copy.wait()
-    place = ((0, 1), (1, 0), (1, 1), (2, 0))
-    for tile_row in range(3):
-        for tile_col in range(3):
-            sides = centre if (tile_row, tile_col) == (1, 1) else mask_columns(tile_row, tile_col)
-            for row in range(4):
-                for col in range(4):
-                    if place[row][0] != tile_row or place[col][0] != tile_col:
-                        continue
-                    at = (row * 4 + col) * 64
-                    flags = sides[place[col][1]][place[row][1] * 64 : place[row][1] * 64 + 64]
-                    if row == 0:
-                        flags = flags * has_north
-                    if row == 3:
-                        flags = flags * has_south
-                    bias[at : at + 64, :] = (flags - 1.0) * 1000000000.0
+    write_bias((0, 2))
     spread_word(3)
     for copy in to_lat:
         copy.wait()
@@ -255,29 +302,6 @@
     for copy in relayed:
         copy.wait()
     project(((0, 0), (0, 3), (3, 0), (3, 3)))
-
-    block_row = lax.broadcasted_iota(jnp.int32, (256, 256), 0) // 64
-    block_col = lax.broadcasted_iota(jnp.int32, (256, 256), 1) // 64
-    diag = jnp.where(block_row == block_col, 1.0, 0.0).astype(FULL)
-    diag_low = diag.astype(LOW)
-
-    def fold(square):
-        kept = square * diag
-        return (kept[:64] + kept[64:128]) + (kept[128:192] + kept[192:])
-
-    def shape_of(index, group):
-        row, col = index // 2, index % 2
-        at = slice(index * 64, index * 64 + 64)
-        lanes = slice(group * 256, group * 256 + 256)
-        starts = [(row + part) * 256 + col * 64 for part in range(3)]
-        spans = [slice(start, start + 192) for start in starts]
-        inner = [slice(part * 256 + col * 64, part * 256 + col * 64 + 192) for part in range(3)]
-        slab = slice(row * 256, row * 256 + 768)
-        spare = 192 if col == 0 else 0
-        return at, lanes, spans, inner, slab, spare
-
-    def spread_heads(rows):
-        return jnp.concatenate([rows] * 4, axis=0) * diag_low
 
     def attend(index, group):
         at, lanes, spans, inner, slab, spare = shape_of(index, group)
@@ -287,17 +311,20 @@
             pscr[slot, part * 256 + spare : part * 256 + spare + 64, :] = jnp.zeros((64, 256), LOW)
         qbd = spread_heads(qs[at, lanes])
         dbd = spread_heads(dout[at, lanes])
-        scores = [
-            dot_nt(keys[span, lanes], qbd) + jnp.concatenate([bias[span, :]] * 2, axis=1)
-            for span in spans
-        ]
-        tops = [jnp.max(part, axis=0, keepdims=True) for part in scores]
-        top = jnp.maximum(jnp.maximum(tops[0], tops[1]), tops[2])
-        weights = [jnp.exp(part - top) for part in scores]
-        sums = [jnp.sum(part, axis=0, keepdims=True) for part in weights]
-        inverse = 1.0 / (sums[0] + sums[1] + sums[2])
+        first, second = middle_parts(index)
+        last = 3 - first - second
+        scores = score(index, group, last, qbd)
+        early_top = stats[slot, 0:1, :]
+        top = jnp.maximum(jnp.max(scores, axis=0, keepdims=True), early_top)
+        weights = jnp.exp(scores - top)
+        shrink = jnp.exp(early_top - top)
+        total = jnp.sum(weights, axis=0, keepdims=True) + shrink * stats[slot, 1:2, :]
+        inverse = 1.0 / total
         for part in range(3):
-            probs = weights[part] * inverse
+            if part == last:
+                probs = weights * inverse
+            else:
+                probs = probs_all[slot, part] * (shrink * inverse)
             probs_all[slot, part] = probs
             pscr[slot, inner[part], :] = probs.astype(LOW)
         out = fold(dot_tn(pscr[slot], values[slab, lanes]))
@@ -390,27 +417,32 @@
                 return carry
 
             lax.fori_loop(0, 8, add, 0)
-        lax.fori_loop(1, 16, begin(plane_copy(chunk)), 0)
+        for step in range(1, 16):
+            plane_copy(chunk)(step).start()
 
     def plane_to_z(chunk):
-        lax.fori_loop(1, 16, finish(plane_copy(chunk)), 0)
+        for step in range(1, 16):
+            plane_copy(chunk)(step).wait()
         for first in range(0, WIDTHS[chunk], 256):
             cols = slice(first, first + 256)
             total = a1s[chunk][here, :, cols].astype(FULL)
             for step in range(15):
                 total = total + r2s[chunk][step, :, cols].astype(FULL)
             a2s[chunk][:, cols] = total.astype(LOW)
-        lax.fori_loop(1, 8, begin(z_copy(chunk)), 0)
+        for step in range(1, 8):
+            z_copy(chunk)(step).start()
 
     def z_to_all(chunk):
-        lax.fori_loop(1, 8, finish(z_copy(chunk)), 0)
+        for step in range(1, 8):
+            z_copy(chunk)(step).wait()
         for first in range(0, WIDTHS[chunk], 256):
             cols = slice(first, first + 256)
             total = a2s[chunk][:, cols].astype(FULL)
             for step in range(7):
                 total = total + r3s[chunk][step, :, cols].astype(FULL)
             totals[chunk][lon, :, cols] = total.astype(LOW)
-        lax.fori_loop(1, 8, begin(all_copy(chunk)), 0)
+        for step in range(1, 8):
+            all_copy(chunk)(step).start()
 
     corners = []
     edges = []
@@ -553,7 +585,8 @@
         for chunk in range(4)
     ]
     for chunk in range(4):
-        lax.fori_loop(1, 8, finish(all_copy(chunk)), 0)
+        for step in range(1, 8):
+            all_copy(chunk)(step).wait()
         sum_copies[chunk].start()
     for copy in [layer_copy, grad_copy] + sum_copies:
         copy.wait()
@@ -571,6 +604,7 @@
         pltpu.VMEM((1, 512), FULL),
         pltpu.VMEM((1, 16, 16, 512), LOW),
         pltpu.VMEM((1, 16, 16, 512), LOW),
+        pltpu.VMEM((8, 8, 256), FULL),
     ]
     scratch += [pltpu.VMEM((1024, 512), LOW)] * 3
     scratch += [pltpu.VMEM((1024, 512), FULL)] * 2

time: 66.5 us -> 65.2 us (0.980)
  Pallas kernels: 65.4 us -> 64.2 us
    pallas_call x1, Pallas kernels: 63.1 us -> 61.9 us  [layer(): pl.pallas_call(layer_kernel, out_shape=(jax.ShapeDtypeStruct((1, 16, 16,...]
where the time goes in v7:
time: 65.2 us; the launch traced here: 65 us
  Pallas kernels  64.2 us (98%)
  between operations  0.8 us (1%)
    pallas_call x1, Pallas kernels, layer(): pl.pallas_call(layer_kernel, out_shape=(jax.ShapeDtypeStruct((1, 16, 16,...  61.9 us
    pallas_call x1, Pallas kernels, finish_outputs(): pl.pallas_call(finish_kernel, out_shape=(jax.ShapeDtypeStruct((1, 16, 16,...  2.3 us

profile of v7, /device:TPU:8, one launch (start us, length us, event | category | flops | bytes accessed | tf_op | source)
XLA Modules:
  0.0 65.0 jit_solution(16649002561333307996)
XLA Ops:
  0.6 61.9 %shard_map.101 = (bf16[1,16,16,512]{3,2,1,0:T(8,128)(2,1)}, bf16[1,16,16,512]{3,2,1,0:T(8,128)(2,1)}, bf16[8,16,512]{2,1,0:T(8,128)(2,1)}, bf16[8,16,512]{2,1,0:...) custom-call(bf16[1,16,16,512]{3,2,1,0:T(8,128)(2,1)} %tokens_ref.1, ...), custom_call_target="tpu_custom_call" | custom-call | tf_op jit(solution)/shard_map/pallas_call | solution.py:630
  62.6 2.3 %shard_map.102 = (bf16[1,16,16,512]{3,2,1,0:T(8,128)(2,1)}, bf16[1,16,16,512]{3,2,1,0:T(8,128)(2,1)}, f32[128,1536]{1,0:T(8,128)}, f32[128,512]{1,0:T(8,128)}, f32[1,128]{1,0:T(1,128)}) custom-call(bf16[1,16,16,512]{3,2,1,0:T(8,128)(2,1)} %get-tuple-element.16.layer_ref, bf16[1,16,16,512]{3,2,1,0:T(8,128)(2,1)} %get-tuple-element.17.grad_ref, ...), custom_call_target="tpu_custom_call" | custom-call | tf_op jit(solution)/shard_map/pallas_call | solution.py:702

commit v8 on v7

--- a/solution.py
+++ b/solution.py
@@ -233,7 +233,7 @@
     qs[...] = (dot_nn(rows, wq[:, :512]) * 0.125).astype(LOW)
     spread_word(1)
     for copy in mask_lon:
-        copy.wait()
+        copy.wait_recv()
     mask_lat = [
         remote(near.at[1], near.at[2], s_m.at[2], v_m.at[2], north),
         remote(near.at[1], near.at[0], s_m.at[3], v_m.at[3], south),
@@ -257,7 +257,7 @@
     relayed = []
     for row, line, peer in ((0, 3, north), (1, 0, south)):
         for side, col in ((0, 3), (1, 0)):
-            to_lon[row * 2 + side].wait()
+            to_lon[row * 2 + side].wait_recv()
             relayed.append(
                 remote(
                     ext.at[1 + row, col], ext.at[line, col],
@@ -292,15 +292,15 @@
         for group in range(2):
             attend_early(index, group)
     for copy in mask_lat:
-        copy.wait()
+        copy.wait_recv()
     write_bias((0, 2))
     spread_word(3)
     for copy in to_lat:
-        copy.wait()
+        copy.wait_recv()
     project(((0, 1), (0, 2), (3, 1), (3, 2)))
     spread_word(4)
     for copy in relayed:
-        copy.wait()
+        copy.wait_recv()
     project(((0, 0), (0, 3), (3, 0), (3, 3)))
 
     def attend(index, group):
@@ -408,7 +408,7 @@
 
     def pair_to_plane(chunk):
         for part, copy in enumerate(pair_copies(chunk)):
-            copy.wait()
+            copy.wait_recv()
 
             def add(piece, carry):
                 span = pl.ds(pl.multiple_of(piece * 16, 16), 16)
@@ -422,7 +422,7 @@
 
     def plane_to_z(chunk):
         for step in range(1, 16):
-            plane_copy(chunk)(step).wait()
+            plane_copy(chunk)(step).wait_recv()
         for first in range(0, WIDTHS[chunk], 256):
             cols = slice(first, first + 256)
             total = a1s[chunk][here, :, cols].astype(FULL)
@@ -434,7 +434,7 @@
 
     def z_to_all(chunk):
         for step in range(1, 8):
-            z_copy(chunk)(step).wait()
+            z_copy(chunk)(step).wait_recv()
         for first in range(0, WIDTHS[chunk], 256):
             cols = slice(first, first + 256)
             total = a2s[chunk][:, cols].astype(FULL)
@@ -524,7 +524,7 @@
     for copy in edges:
         copy.start()
     for copy in corners:
-        copy.wait()
+        copy.wait_recv()
     for row in range(2):
         to_west[row] = (
             ghalo[1 + row, 0].astype(FULL) + sources[row][0].astype(FULL)
@@ -554,7 +554,7 @@
     z_to_all(2)
     z_to_all(3)
     for copy in edges + sideways:
-        copy.wait()
+        copy.wait_recv()
     for row in range(2):
         pieces = []
         cot = cots[row * 8 : row * 8 + 8].astype(FULL)
@@ -586,8 +586,16 @@
     ]
     for chunk in range(4):
         for step in range(1, 8):
-            all_copy(chunk)(step).wait()
+            all_copy(chunk)(step).wait_recv()
         sum_copies[chunk].start()
+    sent = mask_lon + to_lon + to_lat + mask_lat + relayed + corners + edges + sideways
+    for chunk in range(4):
+        sent += pair_copies(chunk)
+        sent += [plane_copy(chunk)(step) for step in range(1, 16)]
+        sent += [z_copy(chunk)(step) for step in range(1, 8)]
+        sent += [all_copy(chunk)(step) for step in range(1, 8)]
+    for copy in sent:
+        copy.wait_send()
     for copy in [layer_copy, grad_copy] + sum_copies:
         copy.wait()
 

time: 65.2 us -> 65.2 us (level)
  no operation moved by 1% of the time
where the time goes in v8:
time: 65.2 us; the launch traced here: 65.1 us
  Pallas kernels  64.3 us (99%)
  between operations  0.8 us (1%)
    pallas_call x1, Pallas kernels, layer(): pl.pallas_call(layer_kernel, out_shape=(jax.ShapeDtypeStruct((1, 16, 16,...  62 us
    pallas_call x1, Pallas kernels, finish_outputs(): pl.pallas_call(finish_kernel, out_shape=(jax.ShapeDtypeStruct((1, 16, 16,...  2.3 us

profile of v8, /device:TPU:8, one launch (start us, length us, event | category | flops | bytes accessed | tf_op | source)
XLA Modules:
  0.0 65.1 jit_solution(14907421448545051942)
XLA Ops:
  0.6 62.0 %shard_map.101 = (bf16[1,16,16,512]{3,2,1,0:T(8,128)(2,1)}, bf16[1,16,16,512]{3,2,1,0:T(8,128)(2,1)}, bf16[8,16,512]{2,1,0:T(8,128)(2,1)}, bf16[8,16,512]{2,1,0:...) custom-call(bf16[1,16,16,512]{3,2,1,0:T(8,128)(2,1)} %tokens_ref.1, ...), custom_call_target="tpu_custom_call" | custom-call | tf_op jit(solution)/shard_map/pallas_call | solution.py:638
  62.6 2.3 %shard_map.102 = (bf16[1,16,16,512]{3,2,1,0:T(8,128)(2,1)}, bf16[1,16,16,512]{3,2,1,0:T(8,128)(2,1)}, f32[128,1536]{1,0:T(8,128)}, f32[128,512]{1,0:T(8,128)}, f32[1,128]{1,0:T(1,128)}) custom-call(bf16[1,16,16,512]{3,2,1,0:T(8,128)(2,1)} %get-tuple-element.16.layer_ref, bf16[1,16,16,512]{3,2,1,0:T(8,128)(2,1)} %get-tuple-element.17.grad_ref, ...), custom_call_target="tpu_custom_call" | custom-call | tf_op jit(solution)/shard_map/pallas_call | solution.py:710
